TPU v7x, 32 devices: a whole 2x2x4 slice. The times are simulated.
32 devices in a mesh: inp: 16 (over z, x, core), chan: 2 (over y).
Axes of the slice: x: 2, y: 2, z: 4, core: 2. Of those that a mesh axis runs over, the one named last changes fastest.
Arguments:
- volt: bfloat16 [32, 1024, 2, 512], P('chan', 'inp'), may hold values from -16 to 16
- mask: int32 [1024], P('inp'), may hold values 0 or 1
- table: int32 [64], replicated, may hold values from 0 to 63, each once
Outputs:
- vis: bfloat16 [16, 2, 2, 4, 2, 128, 128], P('inp', None, 'chan')
- gains: float32 [2, 16, 1024], P('chan', 'inp')
Inputs may be any that keep to these rules, and one draw needn't show every extreme that they name: `table`: each tile number appears once.
All inputs are finite; a program needn't handle non-finite values. No bound on the sum of `mask` on one device may be relied on, other than what follows from the above.
Results may differ from a plain program's by a relative error of at most 0.001.
Values may be sent and summed in bfloat16 or wider, within the bound.
No kernel may reach another device: no remote copies, remote signals or barrier semaphores. Data moves between devices by JAX's collectives and lax.ppermute only.
A program may use at most 64 MiB of HBM per device.

v0:
```python
import math

import jax
import jax.numpy as jnp
from jax import lax
from jax.sharding import PartitionSpec as P

TB = 128
RANK = 4
ITERS = 8
KPO = 4


def gram_parts(v):
    flat = v.reshape(v.shape[0], -1)
    other = jnp.concatenate([v[:, 1, :], -v[:, 0, :]], axis=1)
    dims = (((1,), (1,)), ((), ()))
    real_part = lax.dot_general(flat, flat, dims, preferred_element_type=jnp.float32) / v.shape[2]
    imag_part = lax.dot_general(other, flat, dims, preferred_element_type=jnp.float32) / v.shape[2]
    return (real_part, imag_part)


def apply_gram(real_part, imag_part, q_real, q_imag):
    rank = q_real.shape[0]
    stacked = jnp.concatenate([q_real, q_imag], axis=0)
    first = jnp.einsum("kj,ij->ki", stacked, real_part, precision=lax.Precision.HIGHEST)
    second = jnp.einsum("kj,ij->ki", stacked, imag_part, precision=lax.Precision.HIGHEST)
    return (first[:rank] - second[rank:], first[rank:] + second[:rank])


def orthonormal(z_real, z_imag):
    outs_real = []
    outs_imag = []
    for k in range(z_real.shape[0]):
        w_real = z_real[k]
        w_imag = z_imag[k]
        for l in range(k):
            c_real = jnp.sum(outs_real[l] * z_real[k] + outs_imag[l] * z_imag[k])
            c_imag = jnp.sum(outs_real[l] * z_imag[k] - outs_imag[l] * z_real[k])
            w_real = w_real - (outs_real[l] * c_real - outs_imag[l] * c_imag)
            w_imag = w_imag - (outs_real[l] * c_imag + outs_imag[l] * c_real)
        scale = lax.rsqrt(jnp.sum(w_real * w_real + w_imag * w_imag) + 1e-06)
        outs_real.append(w_real * scale)
        outs_imag.append(w_imag * scale)
    return (jnp.stack(outs_real), jnp.stack(outs_imag))


def calibrate(real_part, imag_part, rank, steps):
    count = real_part.shape[0]
    places = jnp.arange(count, dtype=jnp.float32)
    orders = jnp.arange(rank, dtype=jnp.float32)
    angle = 2.0 * math.pi / count * orders[:, None] * places[None, :]
    q_real = jnp.cos(angle) / math.sqrt(count)
    q_imag = jnp.sin(angle) / math.sqrt(count)
    for step in range(steps):
        z_real, z_imag = apply_gram(real_part, imag_part, q_real, q_imag)
        q_real, q_imag = orthonormal(z_real, z_imag)
    z_real, z_imag = apply_gram(real_part, imag_part, q_real, q_imag)
    high = lax.Precision.HIGHEST
    h_real = jnp.einsum("kj,lj->kl", q_real, z_real, precision=high) + jnp.einsum(
        "kj,lj->kl", q_imag, z_imag, precision=high
    )
    h_imag = jnp.einsum("kj,lj->kl", q_real, z_imag, precision=high) - jnp.einsum(
        "kj,lj->kl", q_imag, z_real, precision=high
    )
    u_real = jnp.einsum("kl,ki->li", h_real, q_real, precision=high) - jnp.einsum(
        "kl,ki->li", h_imag, q_imag, precision=high
    )
    u_imag = jnp.einsum("kl,ki->li", h_imag, q_real, precision=high) + jnp.einsum(
        "kl,ki->li", h_real, q_imag, precision=high
    )
    diag_model = jnp.sum(u_real * q_real + u_imag * q_imag, axis=0)
    floor_value = 0.1 * jnp.mean(diag_model) + 1e-06
    return lax.rsqrt(jnp.maximum(diag_model, floor_value))


def tiles_of(gain_vec, real_part, imag_part, side):
    count = real_part.shape[0]
    outer = gain_vec[:, None] * gain_vec[None, :]
    tile_real = (outer * real_part).astype(jnp.bfloat16)
    tile_imag = (outer * imag_part).astype(jnp.bfloat16)
    blocks = count // side
    both = jnp.stack([tile_real, tile_imag], axis=0).reshape(2, blocks, side, blocks, side)
    return both.transpose(1, 3, 0, 2, 4).reshape(blocks * blocks, 2, side, side)


def body(volt, mask, table):
    masked = volt * mask.astype(jnp.bfloat16)[None, :, None, None]
    turned = lax.all_to_all(masked, "inp", split_axis=0, concat_axis=1, tiled=True)
    real_part, imag_part = gram_parts(turned[0])
    gain_vec = calibrate(real_part, imag_part, RANK, ITERS)
    tiles = tiles_of(gain_vec, real_part, imag_part, TB)
    owners = lax.axis_size("chan")
    slots = tiles.shape[0] // owners
    side = tiles.shape[2]
    outgoing = jnp.take(tiles, table, axis=0).reshape(1, 1, owners, slots, 2, side, side)
    arrived = lax.all_to_all(outgoing, "chan", split_axis=2, concat_axis=1, tiled=True)[
        :, :, :, :KPO
    ]
    return (arrived, gain_vec.reshape(1, 1, -1))


def solution(mesh):
    placed = (P("chan", "inp", None, None), P("inp"), P())
    return jax.shard_map(
        body,
        mesh=mesh,
        in_specs=placed,
        out_specs=(P("inp", None, "chan", None, None, None, None), P("chan", "inp", None)),
        check_vma=False,
    )
```

profile of v0, /device:TPU:10, one launch (start us, length us, event | category | flops | bytes accessed | tf_op | source)
XLA Modules:
  0.0 443.5 jit_solution(17917531039661410690)
XLA Ops:
  1.3 4.8 %broadcast_multiply_fusion = bf16[16,64,2,512]{3,2,1,0:T(2,128)(2,1)} fusion(bf16[16,64,2,512]{3,2,1,0:T(2,128)(2,1)} %param.3, bf16[64]{0:T(256)(128)(2,1)S(1)} %convert_element_type.9), kind=kLoop, calls=%fused_computation.21 | loop fusion | flops 1048576 | bytes 4194432 | tf_op jit(solution)/shard_map/mul | solution.py:88
  6.1 6.5 %all-to-all-start = ((bf16[16,64,2,512]{3,2,1,0:T(2,128)(2,1)}), bf16[16,64,2,512]{3,2,1,0:T(2,128)(2,1)S(1)}, u32[]{:S(2)}, u32[]{:S(2)}) async-start(bf16[16,64,2,512]{3,2,1,0:T(2,128)(2,1)} %broadcast_multiply_fusion), calls=%async_computation | async-start | bytes 4194304 | tf_op jit(solution)/shard_map/all_to_all | solution.py:89
  13.0 46.7 %all-to-all-done = bf16[16,64,2,512]{3,2,1,0:T(2,128)(2,1)S(1)} async-done(((bf16[16,64,2,512]{3,2,1,0:T(2,128)(2,1)}), bf16[16,64,2,512]{3,2,1,0:T(2,128)(2,1)S(1)}, u32[]{:S(2)}, u32[]{:S(2)}) %all-to-all-start) | async-done | bytes 2097184 | tf_op jit(solution)/shard_map/all_to_all | solution.py:89
  60.8 2.4 convolution_multiply_fusion.1
  63.2 2.4 convolution_multiply_fusion
  65.6 3.6 fusion.11
  69.2 3.6 fusion.12
  74.7 1.9 add_reduce_fusion.77
  77.8 3.0 add_reduce_fusion.74
  82.1 4.4 %add_reduce_fusion.70 = f32[]{:T(128)} fusion(f32[1024]{0:T(1024)S(1)} %bitcast.237, f32[1024]{0:T(1024)S(1)} %bitcast.145, f32[1024]{0:T(1024)S(1)} %bitcast.151, f32[1024]{0:T(1024)S(1)} %bitcast.239, f32[1024]{0:T(1024)S(1)} %get-tuple-element.234, f32[1024]{0:T(1024)S(1)} %get-tuple-element.233, f32[1024]{0:T(1024)S(1)} %get-tuple-element.237, ...), kind=kLoop, calls=%fused_computation.237 | loop fusion | flops 32767 | bytes 32804 | tf_op jit(solution)/shard_map/reduce_sum | solution.py:42
  87.2 7.5 %subtract_multiply_fusion.42 = (f32[1,1024]{1,0:T(1,128)S(1)}, f32[1,1024]{1,0:T(1,128)S(1)}, f32[1,1024]{1,0:T(1,128)S(1)}, f32[1,1024]{1,0:T(1,128)S(1)}, f32[1,1024]{1,0:T(1,128)S(1)}) fusion(f32[1,1024]{1,0:T(1,128)S(1)} %get-tuple-element.313, f32[1,1024]{1,0:T(1,128)S(1)} %get-tuple-element.326, f32[]{:T(128)S(6)} %rsqrt.120, f32[]{:T(128)} %get-tuple-element.144, ...), kind=kLoop, calls=%fused_computation.236 | loop fusion | flops 41984 | bytes 49212 | tf_op jit(solution)/shard_map/mul | solution.py:44
  94.8 3.8 subtract_multiply_fusion.43
  98.6 6.2 %fusion.37 = f32[8,1024]{1,0:T(8,128)S(1)} fusion(f32[8,1024]{1,0:T(8,128)S(1)} %concatenate.34, f32[1024,1024]{1,0:T(8,128)} %copy-done), kind=kOutput, calls=%fused_computation.305 | convolution fusion | flops 100663296 | bytes 4259840 | tf_op jit(solution)/shard_map/kj,ij->ki/dot_general | solution.py:26
  104.8 5.7 %fusion.38 = f32[8,1024]{1,0:T(8,128)S(1)} fusion(f32[8,1024]{1,0:T(8,128)S(1)} %concatenate.34, f32[1024,1024]{1,0:T(8,128)} %copy-done.1), kind=kOutput, calls=%fused_computation.306 | convolution fusion | flops 100663296 | bytes 4259840 | tf_op jit(solution)/shard_map/kj,ij->ki/dot_general | solution.py:27
  112.4 1.9 add_reduce_fusion.67
  115.5 3.0 add_reduce_fusion.64
  119.8 4.4 %add_reduce_fusion.60 = f32[]{:T(128)} fusion(f32[1024]{0:T(1024)S(1)} %bitcast.249, f32[1024]{0:T(1024)S(1)} %bitcast.169, f32[1024]{0:T(1024)S(1)} %bitcast.205, f32[1024]{0:T(1024)S(1)} %bitcast.263, f32[1024]{0:T(1024)S(1)} %get-tuple-element.223, f32[1024]{0:T(1024)S(1)} %get-tuple-element.222, f32[1024]{0:T(1024)S(1)} %get-tuple-element.226, ...), kind=kLoop, calls=%fused_computation.211 | loop fusion | flops 32767 | bytes 32804 | tf_op jit(solution)/shard_map/reduce_sum | solution.py:42
  124.9 7.5 %subtract_multiply_fusion.36 = (f32[1,1024]{1,0:T(1,128)S(1)}, f32[1,1024]{1,0:T(1,128)S(1)}, f32[1,1024]{1,0:T(1,128)S(1)}, f32[1,1024]{1,0:T(1,128)S(1)}, f32[1,1024]{1,0:T(1,128)S(1)}) fusion(f32[1,1024]{1,0:T(1,128)S(1)} %get-tuple-element.305, f32[1,1024]{1,0:T(1,128)S(1)} %get-tuple-element.309, f32[]{:T(128)S(6)} %rsqrt.124, f32[]{:T(128)} %get-tuple-element.138, ...), kind=kLoop, calls=%fused_computation.210 | loop fusion | flops 41984 | bytes 49212 | tf_op jit(solution)/shard_map/mul | solution.py:44
  132.5 3.8 subtract_multiply_fusion.37
  136.3 5.6 %fusion.39 = f32[8,1024]{1,0:T(8,128)S(1)} fusion(f32[8,1024]{1,0:T(8,128)S(1)} %concatenate.35, f32[1024,1024]{1,0:T(8,128)} %copy-done), kind=kOutput, calls=%fused_computation.307 | convolution fusion | flops 100663296 | bytes 4259840 | tf_op jit(solution)/shard_map/kj,ij->ki/dot_general | solution.py:26
  142.0 5.7 %fusion.40 = f32[8,1024]{1,0:T(8,128)S(1)} fusion(f32[8,1024]{1,0:T(8,128)S(1)} %concatenate.35, f32[1024,1024]{1,0:T(8,128)} %copy-done.1), kind=kOutput, calls=%fused_computation.308 | convolution fusion | flops 100663296 | bytes 4259840 | tf_op jit(solution)/shard_map/kj,ij->ki/dot_general | solution.py:27
  149.6 1.9 add_reduce_fusion.57
  152.7 3.0 add_reduce_fusion.54
  157.0 4.4 %add_reduce_fusion.50 = f32[]{:T(128)} fusion(f32[1024]{0:T(1024)S(1)} %bitcast.251, f32[1024]{0:T(1024)S(1)} %bitcast.175, f32[1024]{0:T(1024)S(1)} %bitcast.211, f32[1024]{0:T(1024)S(1)} %bitcast.265, f32[1024]{0:T(1024)S(1)} %get-tuple-element.212, f32[1024]{0:T(1024)S(1)} %get-tuple-element.211, f32[1024]{0:T(1024)S(1)} %get-tuple-element.215, ...), kind=kLoop, calls=%fused_computation.185 | loop fusion | flops 32767 | bytes 32804 | tf_op jit(solution)/shard_map/reduce_sum | solution.py:42
  162.1 7.5 %subtract_multiply_fusion.30 = (f32[1,1024]{1,0:T(1,128)S(1)}, f32[1,1024]{1,0:T(1,128)S(1)}, f32[1,1024]{1,0:T(1,128)S(1)}, f32[1,1024]{1,0:T(1,128)S(1)}, f32[1,1024]{1,0:T(1,128)S(1)}) fusion(f32[1,1024]{1,0:T(1,128)S(1)} %get-tuple-element.297, f32[1,1024]{1,0:T(1,128)S(1)} %get-tuple-element.301, f32[]{:T(128)S(6)} %rsqrt.128, f32[]{:T(128)} %get-tuple-element.132, ...), kind=kLoop, calls=%fused_computation.184 | loop fusion | flops 41984 | bytes 49212 | tf_op jit(solution)/shard_map/mul | solution.py:44
  169.7 3.8 subtract_multiply_fusion.31
  173.5 5.8 %fusion.41 = f32[8,1024]{1,0:T(8,128)S(1)} fusion(f32[8,1024]{1,0:T(8,128)S(1)} %concatenate.36, f32[1024,1024]{1,0:T(8,128)} %copy-done), kind=kOutput, calls=%fused_computation.309 | convolution fusion | flops 100663296 | bytes 4259840 | tf_op jit(solution)/shard_map/kj,ij->ki/dot_general | solution.py:26
  179.3 5.7 %fusion.42 = f32[8,1024]{1,0:T(8,128)S(1)} fusion(f32[8,1024]{1,0:T(8,128)S(1)} %concatenate.36, f32[1024,1024]{1,0:T(8,128)} %copy-done.1), kind=kOutput, calls=%fused_computation.310 | convolution fusion | flops 100663296 | bytes 4259840 | tf_op jit(solution)/shard_map/kj,ij->ki/dot_general | solution.py:27
  187.0 1.9 add_reduce_fusion.47
  190.1 3.0 add_reduce_fusion.44
  194.3 4.4 %add_reduce_fusion.40 = f32[]{:T(128)} fusion(f32[1024]{0:T(1024)S(1)} %bitcast.253, f32[1024]{0:T(1024)S(1)} %bitcast.181, f32[1024]{0:T(1024)S(1)} %bitcast.217, f32[1024]{0:T(1024)S(1)} %bitcast.267, f32[1024]{0:T(1024)S(1)} %get-tuple-element.201, f32[1024]{0:T(1024)S(1)} %get-tuple-element.200, f32[1024]{0:T(1024)S(1)} %get-tuple-element.204, ...), kind=kLoop, calls=%fused_computation.159 | loop fusion | flops 32767 | bytes 32804 | tf_op jit(solution)/shard_map/reduce_sum | solution.py:42
  199.5 7.5 %subtract_multiply_fusion.24 = (f32[1,1024]{1,0:T(1,128)S(1)}, f32[1,1024]{1,0:T(1,128)S(1)}, f32[1,1024]{1,0:T(1,128)S(1)}, f32[1,1024]{1,0:T(1,128)S(1)}, f32[1,1024]{1,0:T(1,128)S(1)}) fusion(f32[1,1024]{1,0:T(1,128)S(1)} %get-tuple-element.289, f32[1,1024]{1,0:T(1,128)S(1)} %get-tuple-element.293, f32[]{:T(128)S(6)} %rsqrt.132, f32[]{:T(128)} %get-tuple-element.126, ...), kind=kLoop, calls=%fused_computation.158 | loop fusion | flops 41984 | bytes 49212 | tf_op jit(solution)/shard_map/mul | solution.py:44
  207.0 3.8 subtract_multiply_fusion.25
  210.9 5.6 %fusion.43 = f32[8,1024]{1,0:T(8,128)S(1)} fusion(f32[8,1024]{1,0:T(8,128)S(1)} %concatenate.37, f32[1024,1024]{1,0:T(8,128)} %copy-done), kind=kOutput, calls=%fused_computation.311 | convolution fusion | flops 100663296 | bytes 4259840 | tf_op jit(solution)/shard_map/kj,ij->ki/dot_general | solution.py:26
  216.5 5.7 %fusion.44 = f32[8,1024]{1,0:T(8,128)S(1)} fusion(f32[8,1024]{1,0:T(8,128)S(1)} %concatenate.37, f32[1024,1024]{1,0:T(8,128)} %copy-done.1), kind=kOutput, calls=%fused_computation.312 | convolution fusion | flops 100663296 | bytes 4259840 | tf_op jit(solution)/shard_map/kj,ij->ki/dot_general | solution.py:27
  227.3 3.0 add_reduce_fusion.34
  231.5 4.4 %add_reduce_fusion.30 = f32[]{:T(128)} fusion(f32[1024]{0:T(1024)S(1)} %bitcast.255, f32[1024]{0:T(1024)S(1)} %bitcast.187, f32[1024]{0:T(1024)S(1)} %bitcast.223, f32[1024]{0:T(1024)S(1)} %bitcast.269, f32[1024]{0:T(1024)S(1)} %get-tuple-element.190, f32[1024]{0:T(1024)S(1)} %get-tuple-element.189, f32[1024]{0:T(1024)S(1)} %get-tuple-element.193, ...), kind=kLoop, calls=%fused_computation.133 | loop fusion | flops 32767 | bytes 32804 | tf_op jit(solution)/shard_map/reduce_sum | solution.py:42
  236.7 7.5 %subtract_multiply_fusion.18 = (f32[1,1024]{1,0:T(1,128)S(1)}, f32[1,1024]{1,0:T(1,128)S(1)}, f32[1,1024]{1,0:T(1,128)S(1)}, f32[1,1024]{1,0:T(1,128)S(1)}, f32[1,1024]{1,0:T(1,128)S(1)}) fusion(f32[1,1024]{1,0:T(1,128)S(1)} %get-tuple-element.281, f32[1,1024]{1,0:T(1,128)S(1)} %get-tuple-element.285, f32[]{:T(128)S(6)} %rsqrt.136, f32[]{:T(128)} %get-tuple-element.120, ...), kind=kLoop, calls=%fused_computation.132 | loop fusion | flops 41984 | bytes 49212 | tf_op jit(solution)/shard_map/mul | solution.py:44
  244.2 3.8 subtract_multiply_fusion.19
  248.1 5.9 %fusion.45 = f32[8,1024]{1,0:T(8,128)S(1)} fusion(f32[8,1024]{1,0:T(8,128)S(1)} %concatenate.38, f32[1024,1024]{1,0:T(8,128)} %copy-done), kind=kOutput, calls=%fused_computation.313 | convolution fusion | flops 100663296 | bytes 4259840 | tf_op jit(solution)/shard_map/kj,ij->ki/dot_general | solution.py:26
  253.9 5.7 %fusion.46 = f32[8,1024]{1,0:T(8,128)S(1)} fusion(f32[8,1024]{1,0:T(8,128)S(1)} %concatenate.38, f32[1024,1024]{1,0:T(8,128)} %copy-done.1), kind=kOutput, calls=%fused_computation.314 | convolution fusion | flops 100663296 | bytes 4259840 | tf_op jit(solution)/shard_map/kj,ij->ki/dot_general | solution.py:27
  264.7 3.0 add_reduce_fusion.24
  268.9 4.4 %add_reduce_fusion.20 = f32[]{:T(128)} fusion(f32[1024]{0:T(1024)S(1)} %bitcast.257, f32[1024]{0:T(1024)S(1)} %bitcast.193, f32[1024]{0:T(1024)S(1)} %bitcast.229, f32[1024]{0:T(1024)S(1)} %bitcast.271, f32[1024]{0:T(1024)S(1)} %get-tuple-element.179, f32[1024]{0:T(1024)S(1)} %get-tuple-element.178, f32[1024]{0:T(1024)S(1)} %get-tuple-element.182, ...), kind=kLoop, calls=%fused_computation.107 | loop fusion | flops 32767 | bytes 32804 | tf_op jit(solution)/shard_map/reduce_sum | solution.py:42
  274.1 7.5 %subtract_multiply_fusion.12 = (f32[1,1024]{1,0:T(1,128)S(1)}, f32[1,1024]{1,0:T(1,128)S(1)}, f32[1,1024]{1,0:T(1,128)S(1)}, f32[1,1024]{1,0:T(1,128)S(1)}, f32[1,1024]{1,0:T(1,128)S(1)}) fusion(f32[1,1024]{1,0:T(1,128)S(1)} %get-tuple-element.273, f32[1,1024]{1,0:T(1,128)S(1)} %get-tuple-element.277, f32[]{:T(128)S(6)} %rsqrt.140, f32[]{:T(128)} %get-tuple-element.114, ...), kind=kLoop, calls=%fused_computation.106 | loop fusion | flops 41984 | bytes 49212 | tf_op jit(solution)/shard_map/mul | solution.py:44
  281.6 3.8 subtract_multiply_fusion.13
  285.5 5.6 %fusion.47 = f32[8,1024]{1,0:T(8,128)S(1)} fusion(f32[8,1024]{1,0:T(8,128)S(1)} %concatenate.39, f32[1024,1024]{1,0:T(8,128)} %copy-done), kind=kOutput, calls=%fused_computation.315 | convolution fusion | flops 100663296 | bytes 4259840 | tf_op jit(solution)/shard_map/kj,ij->ki/dot_general | solution.py:26
  291.1 5.7 %fusion.48 = f32[8,1024]{1,0:T(8,128)S(1)} fusion(f32[8,1024]{1,0:T(8,128)S(1)} %concatenate.39, f32[1024,1024]{1,0:T(8,128)} %copy-done.1), kind=kOutput, calls=%fused_computation.316 | convolution fusion | flops 100663296 | bytes 4259840 | tf_op jit(solution)/shard_map/kj,ij->ki/dot_general | solution.py:27
  301.9 3.0 add_reduce_fusion.14
  306.1 4.4 %add_reduce_fusion.10 = f32[]{:T(128)} fusion(f32[1024]{0:T(1024)S(1)} %bitcast.259, f32[1024]{0:T(1024)S(1)} %bitcast.199, f32[1024]{0:T(1024)S(1)} %bitcast.235, f32[1024]{0:T(1024)S(1)} %bitcast.273, f32[1024]{0:T(1024)S(1)} %get-tuple-element.168, f32[1024]{0:T(1024)S(1)} %get-tuple-element.167, f32[1024]{0:T(1024)S(1)} %get-tuple-element.171, ...), kind=kLoop, calls=%fused_computation.81 | loop fusion | flops 32767 | bytes 32804 | tf_op jit(solution)/shard_map/reduce_sum | solution.py:42
  311.3 7.5 %subtract_multiply_fusion.6 = (f32[1,1024]{1,0:T(1,128)S(1)}, f32[1,1024]{1,0:T(1,128)S(1)}, f32[1,1024]{1,0:T(1,128)S(1)}, f32[1,1024]{1,0:T(1,128)S(1)}, f32[1,1024]{1,0:T(1,128)S(1)}) fusion(f32[1,1024]{1,0:T(1,128)S(1)} %get-tuple-element.265, f32[1,1024]{1,0:T(1,128)S(1)} %get-tuple-element.269, f32[]{:T(128)S(6)} %rsqrt.144, f32[]{:T(128)} %get-tuple-element.108, ...), kind=kLoop, calls=%fused_computation.80 | loop fusion | flops 41984 | bytes 49212 | tf_op jit(solution)/shard_map/mul | solution.py:44
  318.8 3.8 subtract_multiply_fusion.7
  322.6 6.0 %fusion.49 = f32[8,1024]{1,0:T(8,128)S(1)} fusion(f32[8,1024]{1,0:T(8,128)S(1)} %concatenate.40, f32[1024,1024]{1,0:T(8,128)} %copy-done), kind=kOutput, calls=%fused_computation.317 | convolution fusion | flops 100663296 | bytes 4259840 | tf_op jit(solution)/shard_map/kj,ij->ki/dot_general | solution.py:26
  328.7 5.7 %fusion.50 = f32[8,1024]{1,0:T(8,128)S(1)} fusion(f32[8,1024]{1,0:T(8,128)S(1)} %concatenate.40, f32[1024,1024]{1,0:T(8,128)} %copy-done.1), kind=kOutput, calls=%fused_computation.318 | convolution fusion | flops 100663296 | bytes 4259840 | tf_op jit(solution)/shard_map/kj,ij->ki/dot_general | solution.py:27
  339.5 3.0 add_reduce_fusion.4
  343.7 4.4 %add_reduce_fusion = f32[]{:T(128)} fusion(f32[1024]{0:T(1024)S(1)} %bitcast.261, f32[1024]{0:T(1024)S(1)} %bitcast.157, f32[1024]{0:T(1024)S(1)} %bitcast.163, f32[1024]{0:T(1024)S(1)} %bitcast.275, f32[1024]{0:T(1024)S(1)} %get-tuple-element.157, f32[1024]{0:T(1024)S(1)} %get-tuple-element.156, f32[1024]{0:T(1024)S(1)} %get-tuple-element.160, ...), kind=kLoop, calls=%fused_computation.55 | loop fusion | flops 32767 | bytes 32804 | tf_op jit(solution)/shard_map/reduce_sum | solution.py:42
  348.9 7.5 %subtract_multiply_fusion = (f32[1,1024]{1,0:T(1,128)S(1)}, f32[1,1024]{1,0:T(1,128)S(1)}, f32[1,1024]{1,0:T(1,128)S(1)}, f32[1,1024]{1,0:T(1,128)S(1)}, f32[1,1024]{1,0:T(1,128)S(1)}) fusion(f32[1,1024]{1,0:T(1,128)S(1)} %get-tuple-element.257, f32[1,1024]{1,0:T(1,128)S(1)} %get-tuple-element.261, f32[]{:T(128)S(6)} %rsqrt.148, f32[]{:T(128)} %get-tuple-element.102, ...), kind=kLoop, calls=%fused_computation.54 | loop fusion | flops 41984 | bytes 49212 | tf_op jit(solution)/shard_map/mul | solution.py:44
  356.4 3.8 subtract_multiply_fusion.1
  360.2 5.6 %fusion.51 = f32[8,1024]{1,0:T(8,128)S(1)} fusion(f32[8,1024]{1,0:T(8,128)S(1)} %concatenate.41, f32[1024,1024]{1,0:T(8,128)} %copy-done), kind=kOutput, calls=%fused_computation.319 | convolution fusion | flops 100663296 | bytes 4259840 | tf_op jit(solution)/shard_map/kj,ij->ki/dot_general | solution.py:26
  365.9 5.7 %fusion.52 = f32[8,1024]{1,0:T(8,128)S(1)} fusion(f32[8,1024]{1,0:T(8,128)S(1)} %concatenate.41, f32[1024,1024]{1,0:T(8,128)} %copy-done.1), kind=kOutput, calls=%fused_computation.320 | convolution fusion | flops 100663296 | bytes 4259840 | tf_op jit(solution)/shard_map/kj,ij->ki/dot_general | solution.py:27
  374.6 4.5 %fusion.3 = (bf16[128,8,8,128]{3,1,2,0:T(8,128)(2,1)S(1)}, bf16[128,8,8,128]{3,1,2,0:T(8,128)(2,1)S(1)}) fusion(f32[1024,1024]{1,0:T(8,128)} %copy-done, f32[1024]{0:T(1024)S(1)} %maximum_rsqrt_fusion, f32[1024,1024]{1,0:T(8,128)} %copy-done.1), kind=kLoop, calls=%fused_computation.10 | loop fusion | flops 5242880 | bytes 12587008
  381.5 2.3 pad_maximum_fusion
  383.8 5.2 %gather_fusion = bf16[64,2,128,128]{3,2,1,0:T(8,128)(2,1)} fusion(bf16[64,2,128,128]{3,2,1,0:T(8,128)(2,1)} %bitcast.132, s32[1024]{0:T(1024)S(1)} %pad_clamp_fusion), kind=kCustom, calls=%fused_computation | custom fusion | bytes 8388864 | tf_op jit(solution)/shard_map/jit(_take)/gather | solution.py:96
  389.1 2.6 broadcast_select_fusion
  391.7 50.8 %all_to_all.21 = bf16[1,1,2,32,2,128,128]{6,5,4,3,1,0,2:T(8,128)(2,1)S(1)} all-to-all(bf16[1,1,2,32,2,128,128]{6,5,4,3,1,0,2:T(8,128)(2,1)S(1)} %broadcast_select_fusion), channel_id=1, replica_groups=mesh['inp'=16,'chan'=2] {'chan'}, dimensions={2} | all-to-all | bytes 8388608 | tf_op jit(solution)/shard_map/all_to_all | solution.py:97
  (99 shorter events, 36.3 us)
Async XLA Ops:
  1.3 11.4 %copy-start.3 = (s32[64]{0:T(128)S(1)}, s32[64]{0:T(128)}, u32[]{:S(2)}) copy-start(s32[64]{0:T(128)} %param.5) | copy-start | bytes 772
  6.1 53.5 %all-to-all-start = ((bf16[16,64,2,512]{3,2,1,0:T(2,128)(2,1)}), bf16[16,64,2,512]{3,2,1,0:T(2,128)(2,1)S(1)}, u32[]{:S(2)}, u32[]{:S(2)}) async-start(bf16[16,64,2,512]{3,2,1,0:T(2,128)(2,1)} %broadcast_multiply_fusion), calls=%async_computation | async-start | bytes 4194304 | tf_op jit(solution)/shard_map/all_to_all | solution.py:89
  63.2 6.0 %copy-start = (f32[1024,1024]{1,0:T(8,128)}, f32[1024,1024]{1,0:T(8,128)S(1)}, u32[]{:S(2)}) copy-start(f32[1024,1024]{1,0:T(8,128)S(1)} %convolution_multiply_fusion.1) | copy-start | bytes 12582916
  65.6 7.2 %copy-start.1 = (f32[1024,1024]{1,0:T(8,128)}, f32[1024,1024]{1,0:T(8,128)S(1)}, u32[]{:S(2)}) copy-start(f32[1024,1024]{1,0:T(8,128)S(1)} %convolution_multiply_fusion) | copy-start | bytes 12582916
  374.6 4.5 %copy-start.2 = (f32[1024]{0:T(1024)}, f32[1024]{0:T(1024)S(1)}, u32[]{:S(2)}) copy-start(f32[1024]{0:T(1024)S(1)} %maximum_rsqrt_fusion) | copy-start | bytes 12292
where the time goes:
time: 449 us; the launch traced here: 444 us
  other arithmetic  201 us (45%)
  matrix products  106 us (24%)
  blocking collectives  50.8 us (11%)
  waiting for transfers between devices  46.7 us (10%)
  between operations  22.9 us (5%)
  local copies, waits for them, and re-layouts  10.1 us (2%)
  starting transfers between devices  6.51 us (1%)
    reduce_sum x32, other arithmetic, orthonormal(): scale = lax.rsqrt(jnp.sum(w_real * w_real + w_imag * w_imag) + 1e-06)  79 us
    mul x8, other arithmetic, orthonormal(): outs_imag.append(w_imag * scale)  60.1 us
    all_to_all x1, blocking collectives, body(): lax.all_to_all(outgoing, 'chan', split_axis=2, concat_axis=1, tiled=True)  50.8 us
    dot_general x9, matrix products, apply_gram(): jnp.einsum('kj,ij->ki', stacked, real_part, precision=lax.Precision.HIGHEST)  50.1 us
    dot_general x9, matrix products, apply_gram(): jnp.einsum('kj,ij->ki', stacked, imag_part, precision=lax.Precision.HIGHEST)  48.9 us
    all_to_all x1, waiting for transfers between devices, body(): lax.all_to_all(masked, 'inp', split_axis=0, concat_axis=1, tiled=True)  46.7 us
    mul x8, other arithmetic, orthonormal(): outs_real.append(w_real * scale)  30.4 us
    reduce_sum x24, other arithmetic, orthonormal(): c_real = jnp.sum(outs_real[l] * z_real[k] + outs_imag[l] * z_imag[k])  15.3 us
  transfers between devices with their start and end apart: 1, of which 1 were waited for; matrix products, arithmetic and copies ran while one was open for 0% of the time, Pallas kernels for 0%

commit v1 on v0

v1 whole, which is shorter than its diff:
```python
import functools
import math

import jax
import jax.numpy as jnp
import numpy as np
from jax import lax
from jax.experimental import pallas as pl
from jax.experimental.pallas import tpu as pltpu
from jax.sharding import PartitionSpec as P

TB = 128
RANK = 4
ITERS = 8
KPO = 4
EPS = 1e-06
SPLITS = 3

VMEM = pl.BlockSpec(memory_space=pltpu.VMEM)
SMEM = pl.BlockSpec(memory_space=pltpu.SMEM)


def first_basis(count):
    turns = np.outer(np.arange(RANK), np.arange(count)) % count
    angle = 2.0 * math.pi / count * turns
    both = np.concatenate([np.cos(angle), np.sin(angle)], axis=0)
    return (both / math.sqrt(count)).astype(np.float32)


def pieces(x):
    parts = []
    rest = x
    for k in range(SPLITS):
        part = rest.astype(jnp.bfloat16).astype(jnp.float32)
        parts.append(part)
        rest = rest - part
    return jnp.concatenate(parts, axis=0).astype(jnp.bfloat16)


def summed(y):
    rows = y.shape[0] // SPLITS
    total = y[(SPLITS - 1) * rows :]
    for k in range(SPLITS - 2, -1, -1):
        total = total + y[k * rows : (k + 1) * rows]
    return total


def swap(x):
    return jnp.concatenate([x[RANK:], x[:RANK]], axis=0)


def gram_times(v_ref, mask, sign, q):
    frames = v_ref.shape[1] // 2
    s = summed(lax.dot_general(pieces(q), v_ref[...], (((1,), (0,)), ((), ())), preferred_element_type=jnp.float32))
    left = s[:, :frames] + sign * swap(s[:, frames:])
    right = -sign * swap(left)
    y = jnp.concatenate([left, right], axis=1)
    z = summed(lax.dot_general(pieces(y), v_ref[...], (((1,), (1,)), ((), ())), preferred_element_type=jnp.float32))
    return z * (1.0 / frames) * mask


def inner(row_real, row_imag, z, sign):
    p = jnp.sum(z * row_real, axis=1, keepdims=True)
    m = jnp.sum(z * row_imag, axis=1, keepdims=True)
    return p + sign * swap(m)


def gram_schmidt(z, sign, order):
    w = z
    q = jnp.zeros_like(z)
    for l in range(RANK):
        row_real = w[l : l + 1]
        row_imag = w[RANK + l : RANK + l + 1]
        norm = jnp.sum(row_real * row_real + row_imag * row_imag, axis=1, keepdims=True)
        scale = lax.rsqrt(norm + EPS)
        q_real = row_real * scale
        q_imag = row_imag * scale
        q = jnp.where(order == l, jnp.where(sign > 0, q_real, q_imag), q)
        if l < RANK - 1:
            c = inner(q_real, q_imag, z, sign)
            c = jnp.where(order > l, c, 0.0)
            w = w - (q_real * c - q_imag * (sign * swap(c)))
    return q


def calibrate_kernel(v_ref, mask_ref, basis_ref, gains_ref, masked_ref):
    count = v_ref.shape[0]
    mask = mask_ref[...].astype(jnp.float32)
    rows = lax.broadcasted_iota(jnp.int32, (2 * RANK, 1), 0)
    sign = jnp.where(rows < RANK, 1.0, -1.0)
    order = jnp.where(rows < RANK, rows, rows - RANK)

    def step(_, q):
        return gram_schmidt(gram_times(v_ref, mask, sign, q), sign, order)

    q = lax.fori_loop(0, ITERS, step, basis_ref[...] * mask)
    z = gram_times(v_ref, mask, sign, q)
    u = jnp.zeros_like(q)
    for k in range(RANK):
        row_real = q[k : k + 1]
        row_imag = q[RANK + k : RANK + k + 1]
        h = inner(row_real, row_imag, z, sign)
        u = u + (row_real * h - row_imag * (sign * swap(h)))
    d = jnp.sum(u * q, axis=0, keepdims=True)
    floor = 0.1 * (jnp.sum(d, axis=1, keepdims=True) / count) + EPS
    gains = lax.rsqrt(jnp.maximum(d, floor))
    gains_ref[...] = gains
    masked = gains * mask
    for k in range(count // TB):
        masked_ref[k : k + 1, :] = masked[:, k * TB : (k + 1) * TB]


def tiles_kernel(owners, slots, table_ref, me_ref, v_ref, *out_refs):
    frames = v_ref.shape[1] // 2
    blocks = v_ref.shape[0] // TB
    dims = (((1,), (1,)), ((), ()))
    for d in range(owners):
        owner = lax.rem(me_ref[0] + d, owners)
        for s in range(KPO):
            tile = table_ref[owner * slots + s]
            row = pl.multiple_of((tile // blocks) * TB, TB)
            col = pl.multiple_of(lax.rem(tile, blocks) * TB, TB)
            lhs = v_ref[pl.ds(row, TB), :]
            rhs = v_ref[pl.ds(col, TB), :]
            other = jnp.concatenate([lhs[:, frames:], -lhs[:, :frames]], axis=1)
            out_refs[d][s, 0] = lax.dot_general(lhs, rhs, dims, preferred_element_type=jnp.float32) / frames
            out_refs[d][s, 1] = lax.dot_general(other, rhs, dims, preferred_element_type=jnp.float32) / frames


def scale_kernel(owners, slots, table_ref, me_ref, *refs):
    tile_refs, gain_refs, vis_ref = refs[:owners], refs[owners : 2 * owners], refs[2 * owners]
    blocks = gain_refs[0].shape[0]
    me = me_ref[0]
    for d in range(owners):
        source = lax.rem(me + owners - d, owners)
        for s in range(KPO):
            tile = table_ref[me * slots + s]
            row = gain_refs[d][pl.ds(tile // blocks, 1), :]
            col = gain_refs[d][pl.ds(lax.rem(tile, blocks), 1), :]
            outer = jnp.transpose(jnp.broadcast_to(row, (TB, TB))) * col
            for part in range(2):
                vis_ref[source, s, part] = (outer * tile_refs[d][s, part]).astype(jnp.bfloat16)


def body(volt, mask, table):
    owners = lax.axis_size("chan")
    slots = table.shape[0] // owners
    full_mask = lax.all_gather(mask, "inp", tiled=True)
    turned = lax.all_to_all(volt, "inp", split_axis=0, concat_axis=1, tiled=True)[0]
    count, _, frames = turned.shape
    flat = turned.reshape(count, 2 * frames)
    me = lax.axis_index("chan").reshape(1)
    blocks = count // TB

    def shift(x, d):
        return lax.ppermute(x, "chan", [(j, (j + d) % owners) for j in range(owners)])

    tile_shape = jax.ShapeDtypeStruct((KPO, 2, TB, TB), jnp.float32)
    tiles = pl.pallas_call(
        functools.partial(tiles_kernel, owners, slots),
        out_shape=[tile_shape] * owners,
        in_specs=[SMEM, SMEM, VMEM],
        out_specs=[VMEM] * owners,
        name="tiles",
    )(table, me, flat)
    arrived = [tiles[0]] + [shift(tiles[d], d) for d in range(1, owners)]

    gains, masked = pl.pallas_call(
        calibrate_kernel,
        out_shape=[
            jax.ShapeDtypeStruct((1, count), jnp.float32),
            jax.ShapeDtypeStruct((blocks, TB), jnp.float32),
        ],
        in_specs=[VMEM] * 3,
        out_specs=[VMEM] * 2,
        name="calibrate",
    )(flat, full_mask.reshape(1, count), first_basis(count))
    all_gains = [masked] + [shift(masked, d) for d in range(1, owners)]

    vis = pl.pallas_call(
        functools.partial(scale_kernel, owners, slots),
        out_shape=jax.ShapeDtypeStruct((owners, KPO, 2, TB, TB), jnp.bfloat16),
        in_specs=[SMEM, SMEM] + [VMEM] * (2 * owners),
        out_specs=VMEM,
        name="scale",
    )(table, me, *arrived, *all_gains)
    return (vis[None, :, None], gains.reshape(1, 1, count))


def solution(mesh):
    placed = (P("chan", "inp", None, None), P("inp"), P())
    return jax.shard_map(
        body,
        mesh=mesh,
        in_specs=placed,
        out_specs=(P("inp", None, "chan", None, None, None, None), P("chan", "inp", None)),
        check_vma=False,
    )
```

time: 449 us -> 103 us (0.23)
  the two profiles are of different devices: /device:TPU:10 before, /device:TPU:0 now
where the time goes in v1:
time: 103 us
  waiting for transfers between devices  44.4 us (43%)
  Pallas kernels  25.7 us (25%)
  blocking collectives  18.2 us (18%)
  starting transfers between devices  9.38 us (9%)
  local copies, waits for them, and re-layouts  3.56 us (3%)
  between operations  1.32 us (1%)
    all_to_all x1, waiting for transfers between devices, body(): lax.all_to_all(volt, 'inp', split_axis=0, concat_axis=1, tiled=True)[0]  41.1 us
    pallas_call x1, Pallas kernels, body(): pl.pallas_call(calibrate_kernel, out_shape=[jax.ShapeDtypeStruct((1, coun...  19.8 us
    unnamed x1, blocking collectives  18.2 us
    all_to_all x1, starting transfers between devices, body(): lax.all_to_all(volt, 'inp', split_axis=0, concat_axis=1, tiled=True)[0]  7.37 us
    pallas_call x1, Pallas kernels, body(): pl.pallas_call(functools.partial(tiles_kernel, owners, slots), out_shape=...  3.69 us
    unnamed x12, local copies, waits for them, and re-layouts  3.56 us
    ppermute x2, waiting for transfers between devices, shift(): lax.ppermute(x, 'chan', [(j, (j + d) % owners) for j in range(owners)])  3.33 us
    pallas_call x1, Pallas kernels, body(): pl.pallas_call(functools.partial(scale_kernel, owners, slots), out_shape=...  2.22 us
  transfers between devices with their start and end apart: 3, of which 2 were waited for; matrix products, arithmetic and copies ran while one was open for 1% of the time, Pallas kernels for 19%

profile of v1, /device:TPU:0, one launch (start us, length us, event | category | flops | bytes accessed | tf_op | source)
XLA Modules:
  0.0 102.5 jit_solution(15891347714697170433)
XLA Ops:
  0.6 7.4 %all-to-all-start = ((bf16[16,64,2,512]{3,2,1,0:T(2,128)(2,1)}), bf16[16,64,2,512]{3,2,1,0:T(2,128)(2,1)S(1)}, u32[]{:S(2)}, u32[]{:S(2)}) async-start(bf16[16,64,2,512]{3,2,1,0:T(2,128)(2,1)} %param.4), calls=%async_computation | async-start | bytes 4194304 | tf_op jit(solution)/shard_map/all_to_all | solution.py:149
  8.0 41.1 %all-to-all-done = bf16[16,64,2,512]{3,2,1,0:T(2,128)(2,1)S(1)} async-done(((bf16[16,64,2,512]{3,2,1,0:T(2,128)(2,1)}), bf16[16,64,2,512]{3,2,1,0:T(2,128)(2,1)S(1)}, u32[]{:S(2)}, u32[]{:S(2)}) %all-to-all-start) | async-done | bytes 2097184 | tf_op jit(solution)/shard_map/all_to_all | solution.py:149
  49.1 1.9 %copy.7 = bf16[128,8,2,512]{3,1,2,0:T(8,128)(2,1)} copy(bf16[128,8,2,512]{3,2,1,0:T(2,128)(2,1)S(1)} %bitcast.12) | data formatting | bytes 4194304
  51.0 0.0 copy-start.3
  51.0 0.0 copy-start.2
  51.0 3.7 %tiles.1 = (f32[4,2,128,128]{3,2,1,0:T(8,128)}, f32[4,2,128,128]{3,2,1,0:T(8,128)}) custom-call(s32[64]{0:T(128)} %table_ref.3, s32[1]{0:T(128)} %bitcast.me_ref, bf16[1024,1024]{1,0:T(8,128)(2,1)} %bitcast.10), custom_call_target="tpu_custom_call" | custom-call | tf_op jit(solution)/shard_map/tiles/pallas_call | solution.py:159
  54.7 1.5 %collective-permute-start = (f32[4,2,128,128]{3,2,1,0:T(8,128)}, f32[4,2,128,128]{3,2,1,0:T(8,128)S(1)}, u32[]{:S(2)}, u32[]{:S(2)}) collective-permute-start(f32[4,2,128,128]{3,2,1,0:T(8,128)} %get-tuple-element.7), channel_id=1, source_target_pairs={{0,1},{1,0},{2,3},{3,2},{4,5},{5,4},{6,7},{7,6},{8,9},{9,8},{10,11... | collective-permute-start | bytes 1572872 | tf_op jit(solution)/shard_map/ppermute | solution.py:156
  56.2 0.0 copy-done.3
  56.2 0.6 dynamic-slice
  57.5 0.0 copy-done.2
  57.5 0.2 dynamic-update-slice
  57.8 18.2 %all-reduce = s32[1024]{0:T(1024)} all-reduce(s32[1024]{0:T(1024)S(1)} %dynamic-update-slice), channel_id=1, replica_groups=mesh['inp'=16,'chan'=2] {'inp'}, use_global_device_ids=true, to_apply=%add | all-reduce | flops 1024 | bytes 8192
  75.9 19.8 %calibrate.1 = (f32[1,1024]{1,0:T(1,128)}, f32[8,128]{1,0:T(8,128)}) custom-call(bf16[1024,1024]{1,0:T(8,128)(2,1)} %bitcast.11, s32[1,1024]{1,0:T(1,128)} %bitcast.14, f32[8,1024]{1,0:T(8,128)} %constant.6.clone.basis_ref), custom_call_target="tpu_custom_call" | custom-call | tf_op jit(solution)/shard_map/calibrate/pallas_call | solution.py:168
  95.7 0.5 collective-permute-start.1
  96.2 3.3 %collective-permute-done.1.refs_3_ = f32[8,128]{1,0:T(8,128)S(1)} collective-permute-done((f32[8,128]{1,0:T(8,128)}, f32[8,128]{1,0:T(8,128)S(1)}, u32[]{:S(2)}, u32[]{:S(2)}) %collective-permute-start.1) | collective-permute-done | bytes 4128 | tf_op jit(solution)/shard_map/ppermute | solution.py:156
  99.5 0.0 copy-start.1
  99.5 0.0 collective-permute-done.refs_1_
  99.5 0.0 copy-start
  99.5 0.6 copy-done.1
  100.1 0.2 copy-done
  100.3 2.2 %scale.1 = bf16[2,4,2,128,128]{4,3,2,1,0:T(8,128)(2,1)} custom-call(s32[64]{0:T(128)} %table_ref.3, s32[1]{0:T(128)} %bitcast.me_ref, f32[4,2,128,128]{3,2,1,0:T(8,128)} %get-tuple-element.6.refs_0_, f32[4,2,128,128]{3,2,1,0:T(8,128)} %copy-done, f32[8,128]{1,0:T(8,128)} %get-tuple-element.8.refs_2_, f32[8,128]{1,0:T(8,128)} %copy-done.1), custom_call_target="tpu_custom_call" | custom-call | tf_op jit(solution)/shard_map/scale/pallas_call | solution.py:180
  (1 shorter events, 0.0 us)
Async XLA Ops:
  0.6 48.5 %all-to-all-start = ((bf16[16,64,2,512]{3,2,1,0:T(2,128)(2,1)}), bf16[16,64,2,512]{3,2,1,0:T(2,128)(2,1)S(1)}, u32[]{:S(2)}, u32[]{:S(2)}) async-start(bf16[16,64,2,512]{3,2,1,0:T(2,128)(2,1)} %param.4), calls=%async_computation | async-start | bytes 4194304 | tf_op jit(solution)/shard_map/all_to_all | solution.py:149
  51.0 5.2 %copy-start.3 = (u32[32]{0:T(128)S(1)}, u32[32]{0:T(128)}, u32[]{:S(2)}) copy-start(u32[32]{0:T(128)} %constant.9) | copy-start | bytes 388
  51.0 6.5 %copy-start.2 = (s32[64]{0:T(128)S(1)}, s32[64]{0:T(128)}, u32[]{:S(2)}) copy-start(s32[64]{0:T(128)} %param.5) | copy-start | bytes 772
  54.7 44.8 %collective-permute-start = (f32[4,2,128,128]{3,2,1,0:T(8,128)}, f32[4,2,128,128]{3,2,1,0:T(8,128)S(1)}, u32[]{:S(2)}, u32[]{:S(2)}) collective-permute-start(f32[4,2,128,128]{3,2,1,0:T(8,128)} %get-tuple-element.7), channel_id=1, source_target_pairs={{0,1},{1,0},{2,3},{3,2},{4,5},{5,4},{6,7},{7,6},{8,9},{9,8},{10,11... | collective-permute-start | bytes 1572872 | tf_op jit(solution)/shard_map/ppermute | solution.py:156
  95.7 3.8 %collective-permute-start.1 = (f32[8,128]{1,0:T(8,128)}, f32[8,128]{1,0:T(8,128)S(1)}, u32[]{:S(2)}, u32[]{:S(2)}) collective-permute-start(f32[8,128]{1,0:T(8,128)} %get-tuple-element.8.refs_2_), channel_id=1, source_target_pairs={{0,1},{1,0},{2,3},{3,2},{4,5},{5,4},{6,7},{7,6},{8,9},{9,8},{10,11... | collective-permute-start | bytes 12296 | tf_op jit(solution)/shard_map/ppermute | solution.py:156
  99.5 0.6 copy-start.1
  99.5 0.8 copy-start

commit v2 on v1

v2 whole, which is shorter than its diff:
```python
import functools
import math

import jax
import jax.numpy as jnp
import numpy as np
from jax import lax
from jax.experimental import pallas as pl
from jax.experimental.pallas import tpu as pltpu
from jax.sharding import PartitionSpec as P

TB = 128
RANK = 4
ITERS = 8
KPO = 4
EPS = 1e-06
SPLITS = 2

VMEM = pl.BlockSpec(memory_space=pltpu.VMEM)
ANY = pl.BlockSpec(memory_space=pl.ANY)
SMEM = pl.BlockSpec(memory_space=pltpu.SMEM)


def first_basis(count):
    turns = np.outer(np.arange(RANK), np.arange(count)) % count
    angle = 2.0 * math.pi / count * turns
    both = np.concatenate([np.cos(angle), np.sin(angle)], axis=0)
    return (both / math.sqrt(count)).astype(np.float32)


def pieces(x):
    parts = []
    rest = x
    for k in range(SPLITS):
        part = rest.astype(jnp.bfloat16).astype(jnp.float32)
        parts.append(part)
        rest = rest - part
    return jnp.concatenate(parts, axis=0).astype(jnp.bfloat16)


def summed(y):
    rows = y.shape[0] // SPLITS
    total = y[(SPLITS - 1) * rows :]
    for k in range(SPLITS - 2, -1, -1):
        total = total + y[k * rows : (k + 1) * rows]
    return total


def swap(x):
    return jnp.concatenate([x[RANK:], x[:RANK]], axis=0)


def gram_times(v_ref, mask, sign, q):
    frames = v_ref.shape[1] // 2
    s = summed(lax.dot_general(pieces(q), v_ref[...], (((1,), (0,)), ((), ())), preferred_element_type=jnp.float32))
    left = s[:, :frames] + sign * swap(s[:, frames:])
    right = -sign * swap(left)
    y = jnp.concatenate([left, right], axis=1)
    z = summed(lax.dot_general(pieces(y), v_ref[...], (((1,), (1,)), ((), ())), preferred_element_type=jnp.float32))
    return z * (1.0 / frames) * mask


def inner(row_real, row_imag, z, turned):
    first = jnp.sum(z * row_real + turned * row_imag, axis=1, keepdims=True)
    second = jnp.sum(z * row_imag - turned * row_real, axis=1, keepdims=True)
    return first, second


def gram_schmidt(z, sign, order):
    turned = sign * swap(z)
    w = z
    reals, imags = [], []
    for l in range(RANK):
        row_real = w[l : l + 1]
        row_imag = w[RANK + l : RANK + l + 1]
        norm = jnp.sum(row_real * row_real + row_imag * row_imag, axis=1, keepdims=True)
        scale = lax.rsqrt(norm + EPS)
        reals.append(row_real * scale)
        imags.append(row_imag * scale)
        if l < RANK - 1:
            first, second = inner(row_real, row_imag, z, turned)
            keep = jnp.where(order > l, scale * scale, 0.0)
            w = w - (row_real * (first * keep) + row_imag * (second * keep))
    return jnp.concatenate(reals + imags, axis=0)


def calibrate_kernel(v_ref, mask_ref, basis_ref, gains_ref, masked_ref):
    count = v_ref.shape[0]
    mask = mask_ref[...].astype(jnp.float32)
    rows = lax.broadcasted_iota(jnp.int32, (2 * RANK, 1), 0)
    sign = jnp.where(rows < RANK, 1.0, -1.0)
    order = jnp.where(rows < RANK, rows, rows - RANK)

    def step(_, q):
        return gram_schmidt(gram_times(v_ref, mask, sign, q), sign, order)

    q = lax.fori_loop(0, ITERS, step, basis_ref[...] * mask)
    z = gram_times(v_ref, mask, sign, q)
    turned = sign * swap(z)
    u = jnp.zeros_like(q)
    for k in range(RANK):
        row_real = q[k : k + 1]
        row_imag = q[RANK + k : RANK + k + 1]
        first, second = inner(row_real, row_imag, z, turned)
        u = u + (row_real * first + row_imag * second)
    d = jnp.sum(u * q, axis=0, keepdims=True)
    floor = 0.1 * (jnp.sum(d, axis=1, keepdims=True) / count) + EPS
    gains = lax.rsqrt(jnp.maximum(d, floor))
    gains_ref[...] = gains
    masked = gains * mask
    for k in range(count // TB):
        masked_ref[k : k + 1, :] = masked[:, k * TB : (k + 1) * TB]


def product(v_ref, tile):
    frames = v_ref.shape[1] // 2
    blocks = v_ref.shape[0] // TB
    lhs = v_ref[pl.ds(pl.multiple_of((tile // blocks) * TB, TB), TB), :]
    rhs = v_ref[pl.ds(pl.multiple_of(lax.rem(tile, blocks) * TB, TB), TB), :]
    other = jnp.concatenate([lhs[:, frames:], -lhs[:, :frames]], axis=1)
    both = jnp.concatenate([lhs, other], axis=0)
    dims = (((1,), (1,)), ((), ()))
    return lax.dot_general(both, rhs, dims, preferred_element_type=jnp.float32) * (1.0 / frames)


def outer(gains_ref, tile):
    blocks = gains_ref.shape[0]
    row = gains_ref[pl.ds(tile // blocks, 1), :]
    col = gains_ref[pl.ds(lax.rem(tile, blocks), 1), :]
    return jnp.transpose(jnp.broadcast_to(row, (TB, TB))) * col


def sent_kernel(owners, slots, table_ref, me_ref, v_ref, *out_refs):
    for d in range(1, owners):
        owner = lax.rem(me_ref[0] + d, owners)
        for s in range(KPO):
            both = product(v_ref, table_ref[owner * slots + s])
            out_refs[d - 1][s, 0] = both[:TB]
            out_refs[d - 1][s, 1] = both[TB:]


def own_kernel(slots, table_ref, me_ref, v_ref, gains_ref, vis_ref, held, sem):
    me = me_ref[0]
    for s in range(KPO):
        tile = table_ref[me * slots + s]
        both = product(v_ref, tile)
        scale = outer(gains_ref, tile)
        held[s, 0] = (scale * both[:TB]).astype(jnp.bfloat16)
        held[s, 1] = (scale * both[TB:]).astype(jnp.bfloat16)
    copy = pltpu.make_async_copy(held, vis_ref.at[me], sem)
    copy.start()
    copy.wait()


def others_kernel(owners, slots, table_ref, me_ref, *refs):
    tile_refs, gain_refs = refs[: owners - 1], refs[owners - 1 : 2 * owners - 2]
    vis_ref, held, sem = refs[-3:]
    me = me_ref[0]
    copies = []
    for d in range(1, owners):
        for s in range(KPO):
            scale = outer(gain_refs[d - 1], table_ref[me * slots + s])
            for part in range(2):
                held[d - 1, s, part] = (scale * tile_refs[d - 1][s, part]).astype(jnp.bfloat16)
        source = lax.rem(me + owners - d, owners)
        copies.append(pltpu.make_async_copy(held.at[d - 1], vis_ref.at[source], sem.at[d - 1]))
        copies[-1].start()
    for copy in copies:
        copy.wait()


def gather_mask(mask):
    parts = lax.axis_size("inp")
    size = mask.shape[0]
    whole = jnp.zeros((1, parts * size), mask.dtype)
    whole = lax.dynamic_update_slice(whole, mask.reshape(1, size), (0, lax.axis_index("inp") * size))
    if parts & (parts - 1):
        return lax.psum(whole, "inp")
    step = 1
    while step < parts:
        whole = whole + lax.ppermute(whole, "inp", [(j, (j + step) % parts) for j in range(parts)])
        step *= 2
    return whole


def in_vmem(x, owners=2):
    return x if owners > 2 else pltpu.with_memory_space_constraint(x, pltpu.VMEM)


def body(volt, mask, table):
    owners = lax.axis_size("chan")
    slots = table.shape[0] // owners
    full_mask = gather_mask(mask)
    turned = lax.all_to_all(volt, "inp", split_axis=0, concat_axis=1, tiled=True)[0]
    turned, full_mask = lax.optimization_barrier((turned, full_mask))
    count, _, frames = turned.shape
    flat = in_vmem(turned.reshape(count, 2 * frames))
    me = lax.axis_index("chan").reshape(1)
    blocks = count // TB

    def shift(x, d):
        return lax.ppermute(x, "chan", [(j, (j + d) % owners) for j in range(owners)])

    sent = pl.pallas_call(
        functools.partial(sent_kernel, owners, slots),
        out_shape=[(pltpu.VMEM if owners == 2 else jax.ShapeDtypeStruct)((KPO, 2, TB, TB), jnp.float32)] * (owners - 1),
        in_specs=[SMEM, SMEM, VMEM],
        out_specs=[VMEM] * (owners - 1),
        name="sent",
    )(table, me, flat)
    arrived = [in_vmem(shift(sent[d - 1], d), owners) for d in range(1, owners)]

    gains, masked = pl.pallas_call(
        calibrate_kernel,
        out_shape=[
            jax.ShapeDtypeStruct((1, count), jnp.float32),
            pltpu.VMEM((blocks, TB), jnp.float32),
        ],
        in_specs=[VMEM] * 3,
        out_specs=[VMEM] * 2,
        name="calibrate",
    )(flat, full_mask, first_basis(count))
    other_gains = [in_vmem(shift(masked, d), owners) for d in range(1, owners)]

    vis_shape = jax.ShapeDtypeStruct((owners, KPO, 2, TB, TB), jnp.bfloat16)
    vis = pl.pallas_call(
        functools.partial(own_kernel, slots),
        out_shape=vis_shape,
        in_specs=[SMEM, SMEM, VMEM, VMEM],
        out_specs=ANY,
        scratch_shapes=[pltpu.VMEM((KPO, 2, TB, TB), jnp.bfloat16), pltpu.SemaphoreType.DMA],
        name="own",
    )(table, me, flat, masked)
    vis = pl.pallas_call(
        functools.partial(others_kernel, owners, slots),
        out_shape=vis_shape,
        in_specs=[SMEM, SMEM] + [VMEM] * (2 * owners - 2) + [ANY],
        out_specs=ANY,
        scratch_shapes=[
            pltpu.VMEM((owners - 1, KPO, 2, TB, TB), jnp.bfloat16),
            pltpu.SemaphoreType.DMA((owners - 1,)),
        ],
        input_output_aliases={2 * owners: 0},
        name="others",
    )(table, me, *arrived, *other_gains, vis)
    return (vis[None, :, None], gains.reshape(1, 1, count))


def solution(mesh):
    placed = (P("chan", "inp", None, None), P("inp"), P())
    return jax.shard_map(
        body,
        mesh=mesh,
        in_specs=placed,
        out_specs=(P("inp", None, "chan", None, None, None, None), P("chan", "inp", None)),
        check_vma=False,
    )
```

time: 103 us -> 94.3 us (0.916)
  blocking collectives: 18.2 us -> 0 us
  waiting for transfers between devices: 44.4 us -> 53 us
  starting transfers between devices: 9.38 us -> 17 us
  Pallas kernels: 25.7 us -> 18.8 us
    ppermute x0 -> x4, waiting for transfers between devices: none -> 52.1 us  [gather_mask(): lax.ppermute(whole, 'inp', [(j, (j + step) % parts) for j in range(parts)])]
    all_to_all x1, waiting for transfers between devices: 41.1 us -> 0.01 us  [body(): lax.all_to_all(volt, 'inp', split_axis=0, concat_axis=1, tiled=True)[0]]
    unnamed x1 -> x0, blocking collectives: 18.2 us -> none
    ppermute x0 -> x4, starting transfers between devices: none -> 7.49 us  [gather_mask(): lax.ppermute(whole, 'inp', [(j, (j + step) % parts) for j in range(parts)])]
    pallas_call x1, Pallas kernels: 19.8 us -> 13.7 us  [body(): pl.pallas_call(calibrate_kernel, out_shape=[jax.ShapeDtypeStruct((1, coun...]
    ppermute x2, waiting for transfers between devices: 3.33 us -> 0.91 us  [shift(): lax.ppermute(x, 'chan', [(j, (j + d) % owners) for j in range(owners)])]
    pallas_call x2 -> x3, Pallas kernels: 5.91 us -> 5.02 us  [the longest x1 2.11 us: body(): pl.pallas_call(functools.partial(own_kernel, slots), out_shape=vis_shape,...]
    unnamed x12 -> x7, local copies, waits for them, and re-layouts: 3.56 us -> 3.56 us
  transfers between devices with their start and end apart: 3 -> 7, of which waited for: 2 -> 5; matrix products, arithmetic and copies ran while one was open for 1% -> 1% of each run, Pallas kernels for 19% -> 17%
where the time goes in v2:
time: 94.3 us; the launch traced here: 94 us
  waiting for transfers between devices  53 us (56%)
  Pallas kernels  18.8 us (20%)
  starting transfers between devices  17 us (18%)
  local copies, waits for them, and re-layouts  3.8 us (4%)
    ppermute x4, waiting for transfers between devices, gather_mask(): lax.ppermute(whole, 'inp', [(j, (j + step) % parts) for j in range(parts)])  52.1 us
    pallas_call x1, Pallas kernels, body(): pl.pallas_call(calibrate_kernel, out_shape=[jax.ShapeDtypeStruct((1, coun...  13.7 us
    ppermute x4, starting transfers between devices, gather_mask(): lax.ppermute(whole, 'inp', [(j, (j + step) % parts) for j in range(parts)])  7.49 us
    all_to_all x1, starting transfers between devices, body(): lax.all_to_all(volt, 'inp', split_axis=0, concat_axis=1, tiled=True)[0]  7.37 us
    unnamed x7, local copies, waits for them, and re-layouts  3.56 us
    pallas_call x1, Pallas kernels, body(): pl.pallas_call(functools.partial(own_kernel, slots), out_shape=vis_shape,...  2.11 us
    ppermute x2, starting transfers between devices, shift(): lax.ppermute(x, 'chan', [(j, (j + d) % owners) for j in range(owners)])  2.09 us
  transfers between devices with their start and end apart: 7, of which 5 were waited for; matrix products, arithmetic and copies ran while one was open for 1% of the time, Pallas kernels for 17%

profile of v2, /device:TPU:0, one launch (start us, length us, event | category | flops | bytes accessed | tf_op | source)
XLA Modules:
  0.0 94.0 jit_solution(1764919114869289145)
XLA Ops:
  0.6 0.0 copy-start.2
  0.6 7.4 %all-to-all-start = ((bf16[16,64,2,512]{3,2,1,0:T(2,128)(2,1)}), bf16[16,64,2,512]{3,2,1,0:T(2,128)(2,1)S(1)}, u32[]{:S(2)}, u32[]{:S(2)}) async-start(bf16[16,64,2,512]{3,2,1,0:T(2,128)(2,1)} %param.4), calls=%async_computation | async-start | bytes 4194304 | tf_op jit(solution)/shard_map/all_to_all | solution.py:194
  8.0 0.0 copy-done.2
  8.0 0.2 dynamic_update_slice.5
  8.2 0.5 collective-permute-start
  8.7 38.8 %collective-permute-done = s32[1,1024]{1,0:T(1,128)S(1)} collective-permute-done((s32[1,1024]{1,0:T(1,128)S(1)}, s32[1,1024]{1,0:T(1,128)S(1)}, u32[]{:S(2)}, u32[]{:S(2)}) %collective-permute-start) | collective-permute-done | bytes 4128 | tf_op jit(solution)/shard_map/ppermute | solution.py:181
  47.5 0.1 dynamic-slice_add_fusion
  47.6 0.1 add.17
  47.7 0.1 collective-permute-start.1
  47.7 6.4 %collective-permute-done.1 = s32[1,1024]{1,0:T(1,128)S(1)} collective-permute-done((s32[1,1024]{1,0:T(1,128)S(1)}, s32[1,1024]{1,0:T(1,128)S(1)}, u32[]{:S(2)}, u32[]{:S(2)}) %collective-permute-start.1) | collective-permute-done | bytes 4128 | tf_op jit(solution)/shard_map/ppermute | solution.py:181
  54.1 0.0 collective-permute-start.2
  54.1 5.4 %collective-permute-done.2 = s32[1,1024]{1,0:T(1,128)S(1)} collective-permute-done((s32[1,1024]{1,0:T(1,128)S(1)}, s32[1,1024]{1,0:T(1,128)S(1)}, u32[]{:S(2)}, u32[]{:S(2)}) %collective-permute-start.2) | collective-permute-done | bytes 4128 | tf_op jit(solution)/shard_map/ppermute | solution.py:181
  59.5 6.9 %collective-permute-start.3 = (s32[1,1024]{1,0:T(1,128)S(1)}, s32[1,1024]{1,0:T(1,128)S(1)}, u32[]{:S(2)}, u32[]{:S(2)}) collective-permute-start(s32[1,1024]{1,0:T(1,128)S(1)} %add.19), channel_id=1, source_target_pairs={{0,16},{2,18},{4,20},{6,22},{8,24},{10,26},{12,28},{14,30},{16,0},... | collective-permute-start | bytes 12296 | tf_op jit(solution)/shard_map/ppermute | solution.py:181
  66.4 1.6 %collective-permute-done.3 = s32[1,1024]{1,0:T(1,128)S(1)} collective-permute-done((s32[1,1024]{1,0:T(1,128)S(1)}, s32[1,1024]{1,0:T(1,128)S(1)}, u32[]{:S(2)}, u32[]{:S(2)}) %collective-permute-start.3) | collective-permute-done | bytes 4128 | tf_op jit(solution)/shard_map/ppermute | solution.py:181
  68.0 0.6 add.20.mask_ref
  68.6 0.0 all-to-all-done
  68.6 0.0 copy-start.1
  68.6 1.3 %copy-done.1 = bf16[16,64,2,512]{3,2,1,0:T(2,128)(2,1)} copy-done((bf16[16,64,2,512]{3,2,1,0:T(2,128)(2,1)}, bf16[16,64,2,512]{3,2,1,0:T(2,128)(2,1)S(1)}, u32[]{:S(2)}) %copy-start.1) | copy-done | bytes 2097176
  70.0 2.1 %copy.8 = bf16[128,8,2,512]{3,1,2,0:T(8,128)(2,1)S(1)} copy(bf16[128,8,2,512]{3,2,1,0:T(2,128)(2,1)} %bitcast.13) | data formatting | bytes 4194304
  72.1 1.4 %sent.1 = f32[4,2,128,128]{3,2,1,0:T(8,128)S(1)} custom-call(s32[64]{0:T(128)} %table_ref.5, s32[1]{0:T(128)} %bitcast.me_ref, bf16[1024,1024]{1,0:T(8,128)(2,1)S(1)} %bitcast.10), custom_call_target="tpu_custom_call" | custom-call | tf_op jit(solution)/shard_map/sent/pallas_call | solution.py:204
  73.5 1.6 %collective-permute-start.4 = (f32[4,2,128,128]{3,2,1,0:T(8,128)S(1)}, f32[4,2,128,128]{3,2,1,0:T(8,128)S(1)}, u32[]{:S(2)}, u32[]{:S(2)}) collective-permute-start(f32[4,2,128,128]{3,2,1,0:T(8,128)S(1)} %sent.1), channel_id=1, source_target_pairs={{0,1},{1,0},{2,3},{3,2},{4,5},{5,4},{6,7},{7,6},{8,9},{9,8},{10,11... | collective-permute-start | bytes 1572872 | tf_op jit(solution)/shard_map/ppermute | solution.py:202
  75.1 13.7 %calibrate.1 = (f32[1,1024]{1,0:T(1,128)}, f32[8,128]{1,0:T(8,128)S(1)}) custom-call(bf16[1024,1024]{1,0:T(8,128)(2,1)S(1)} %bitcast.11, s32[1,1024]{1,0:T(1,128)} %add.20.mask_ref, f32[8,1024]{1,0:T(8,128)} %constant.17.clone.basis_ref), custom_call_target="tpu_custom_call" | custom-call | tf_op jit(solution)/shard_map/calibrate/pallas_call | solution.py:213
  88.8 0.0 copy-start
  88.8 0.5 collective-permute-start.5
  89.3 0.1 copy-done
  89.4 2.1 %own.1.refs_2_ = bf16[2,4,2,128,128]{4,3,2,1,0:T(8,128)(2,1)} custom-call(s32[64]{0:T(128)} %table_ref.5, s32[1]{0:T(128)} %bitcast.me_ref, bf16[1024,1024]{1,0:T(8,128)(2,1)S(1)} %bitcast.12, f32[8,128]{1,0:T(8,128)} %copy-done), custom_call_target="tpu_custom_call" | custom-call | tf_op jit(solution)/shard_map/own/pallas_call | solution.py:226
  91.5 0.9 collective-permute-done.5.refs_1_
  92.4 0.0 collective-permute-done.4.refs_0_
  92.5 1.5 %others.1 = bf16[2,4,2,128,128]{4,3,2,1,0:T(8,128)(2,1)} custom-call(s32[64]{0:T(128)} %table_ref.5, s32[1]{0:T(128)} %bitcast.me_ref, f32[4,2,128,128]{3,2,1,0:T(8,128)S(1)} %collective-permute-done.4.refs_0_, f32[8,128]{1,0:T(8,128)S(1)} %collective-permute-done.5.refs_1_, bf16[2,4,2,128,128]{4,3,2,1,0:T(8,128)(2,1)} %own.1.refs_2_), custom_call_target="tpu_custom_call", output_to_operand_aliasing={{}: (4, {})} | custom-call | tf_op jit(solution)/shard_map/others/pallas_call | solution.py:234
  (3 shorter events, 0.0 us)
Async XLA Ops:
  0.6 7.4 %copy-start.2 = (s32[64]{0:T(128)S(1)}, s32[64]{0:T(128)}, u32[]{:S(2)}) copy-start(s32[64]{0:T(128)} %param.5) | copy-start | bytes 772
  0.6 68.0 %all-to-all-start = ((bf16[16,64,2,512]{3,2,1,0:T(2,128)(2,1)}), bf16[16,64,2,512]{3,2,1,0:T(2,128)(2,1)S(1)}, u32[]{:S(2)}, u32[]{:S(2)}) async-start(bf16[16,64,2,512]{3,2,1,0:T(2,128)(2,1)} %param.4), calls=%async_computation | async-start | bytes 4194304 | tf_op jit(solution)/shard_map/all_to_all | solution.py:194
  8.2 39.3 %collective-permute-start = (s32[1,1024]{1,0:T(1,128)S(1)}, s32[1,1024]{1,0:T(1,128)S(1)}, u32[]{:S(2)}, u32[]{:S(2)}) collective-permute-start(s32[1,1024]{1,0:T(1,128)S(1)} %dynamic_update_slice.5), channel_id=1, source_target_pairs={{0,2},{2,4},{4,6},{6,8},{8,10},{10,12},{12,14},{14,16},{16,18},{18... | collective-permute-start | bytes 12296 | tf_op jit(solution)/shard_map/ppermute | solution.py:181
  47.7 6.5 %collective-permute-start.1 = (s32[1,1024]{1,0:T(1,128)S(1)}, s32[1,1024]{1,0:T(1,128)S(1)}, u32[]{:S(2)}, u32[]{:S(2)}) collective-permute-start(s32[1,1024]{1,0:T(1,128)S(1)} %add.17), channel_id=1, source_target_pairs={{0,4},{2,6},{4,8},{6,10},{8,12},{10,14},{12,16},{14,18},{16,20},{1... | collective-permute-start | bytes 12296 | tf_op jit(solution)/shard_map/ppermute | solution.py:181
  54.1 5.4 %collective-permute-start.2 = (s32[1,1024]{1,0:T(1,128)S(1)}, s32[1,1024]{1,0:T(1,128)S(1)}, u32[]{:S(2)}, u32[]{:S(2)}) collective-permute-start(s32[1,1024]{1,0:T(1,128)S(1)} %add.18), channel_id=1, source_target_pairs={{0,8},{2,10},{4,12},{6,14},{8,16},{10,18},{12,20},{14,22},{16,24},... | collective-permute-start | bytes 12296 | tf_op jit(solution)/shard_map/ppermute | solution.py:181
  59.5 8.5 %collective-permute-start.3 = (s32[1,1024]{1,0:T(1,128)S(1)}, s32[1,1024]{1,0:T(1,128)S(1)}, u32[]{:S(2)}, u32[]{:S(2)}) collective-permute-start(s32[1,1024]{1,0:T(1,128)S(1)} %add.19), channel_id=1, source_target_pairs={{0,16},{2,18},{4,20},{6,22},{8,24},{10,26},{12,28},{14,30},{16,0},... | collective-permute-start | bytes 12296 | tf_op jit(solution)/shard_map/ppermute | solution.py:181
  68.6 1.3 %copy-start.1 = (bf16[16,64,2,512]{3,2,1,0:T(2,128)(2,1)}, bf16[16,64,2,512]{3,2,1,0:T(2,128)(2,1)S(1)}, u32[]{:S(2)}) copy-start(bf16[16,64,2,512]{3,2,1,0:T(2,128)(2,1)S(1)} %all-to-all-done) | copy-start | bytes 6291460
  73.5 18.9 %collective-permute-start.4 = (f32[4,2,128,128]{3,2,1,0:T(8,128)S(1)}, f32[4,2,128,128]{3,2,1,0:T(8,128)S(1)}, u32[]{:S(2)}, u32[]{:S(2)}) collective-permute-start(f32[4,2,128,128]{3,2,1,0:T(8,128)S(1)} %sent.1), channel_id=1, source_target_pairs={{0,1},{1,0},{2,3},{3,2},{4,5},{5,4},{6,7},{7,6},{8,9},{9,8},{10,11... | collective-permute-start | bytes 1572872 | tf_op jit(solution)/shard_map/ppermute | solution.py:202
  88.8 0.6 copy-start
  88.8 3.6 %collective-permute-start.5 = (f32[8,128]{1,0:T(8,128)S(1)}, f32[8,128]{1,0:T(8,128)S(1)}, u32[]{:S(2)}, u32[]{:S(2)}) collective-permute-start(f32[8,128]{1,0:T(8,128)S(1)} %get-tuple-element.8.gains_ref), channel_id=1, source_target_pairs={{0,1},{1,0},{2,3},{3,2},{4,5},{5,4},{6,7},{7,6},{8,9},{9,8},{10,11... | collective-permute-start | bytes 12296 | tf_op jit(solution)/shard_map/ppermute | solution.py:202

commit v3 on v2

--- a/solution.py
+++ b/solution.py
@@ -38,26 +38,17 @@
     return jnp.concatenate(parts, axis=0).astype(jnp.bfloat16)
 
 
-def summed(y):
-    rows = y.shape[0] // SPLITS
-    total = y[(SPLITS - 1) * rows :]
+def dot(x, y):
+    split = lax.dot_general(x, y, (((1,), (0,)), ((), ())), preferred_element_type=jnp.float32)
+    rows = split.shape[0] // SPLITS
+    total = split[(SPLITS - 1) * rows :]
     for k in range(SPLITS - 2, -1, -1):
-        total = total + y[k * rows : (k + 1) * rows]
+        total = total + split[k * rows : (k + 1) * rows]
     return total
 
 
 def swap(x):
     return jnp.concatenate([x[RANK:], x[:RANK]], axis=0)
-
-
-def gram_times(v_ref, mask, sign, q):
-    frames = v_ref.shape[1] // 2
-    s = summed(lax.dot_general(pieces(q), v_ref[...], (((1,), (0,)), ((), ())), preferred_element_type=jnp.float32))
-    left = s[:, :frames] + sign * swap(s[:, frames:])
-    right = -sign * swap(left)
-    y = jnp.concatenate([left, right], axis=1)
-    z = summed(lax.dot_general(pieces(y), v_ref[...], (((1,), (1,)), ((), ())), preferred_element_type=jnp.float32))
-    return z * (1.0 / frames) * mask
 
 
 def inner(row_real, row_imag, z, turned):
@@ -66,44 +57,57 @@
     return first, second
 
 
-def gram_schmidt(z, sign, order):
+def times(x, k, first, second):
+    return x[k : k + 1] * first + x[RANK + k : RANK + k + 1] * second
+
+
+def gram_schmidt(z, p, sign, order):
     turned = sign * swap(z)
     w = z
-    reals, imags = [], []
+    scales = jnp.zeros((2 * RANK, 1), jnp.float32)
     for l in range(RANK):
         row_real = w[l : l + 1]
         row_imag = w[RANK + l : RANK + l + 1]
         norm = jnp.sum(row_real * row_real + row_imag * row_imag, axis=1, keepdims=True)
         scale = lax.rsqrt(norm + EPS)
-        reals.append(row_real * scale)
-        imags.append(row_imag * scale)
+        scales = jnp.where(order == l, scale, scales)
         if l < RANK - 1:
             first, second = inner(row_real, row_imag, z, turned)
             keep = jnp.where(order > l, scale * scale, 0.0)
-            w = w - (row_real * (first * keep) + row_imag * (second * keep))
-    return jnp.concatenate(reals + imags, axis=0)
-
-
-def calibrate_kernel(v_ref, mask_ref, basis_ref, gains_ref, masked_ref):
-    count = v_ref.shape[0]
+            first, second = first * keep, second * keep
+            w = w - times(w, l, first, second)
+            p = p - times(p, l, first, second)
+    return w * scales, p * scales
+
+
+def calibrate_kernel(v_ref, mask_ref, basis_ref, gains_ref, masked_ref, vt_ref):
+    _, count, frames = v_ref.shape
     mask = mask_ref[...].astype(jnp.float32)
     rows = lax.broadcasted_iota(jnp.int32, (2 * RANK, 1), 0)
     sign = jnp.where(rows < RANK, 1.0, -1.0)
     order = jnp.where(rows < RANK, rows, rows - RANK)
-
-    def step(_, q):
-        return gram_schmidt(gram_times(v_ref, mask, sign, q), sign, order)
-
-    q = lax.fori_loop(0, ITERS, step, basis_ref[...] * mask)
-    z = gram_times(v_ref, mask, sign, q)
-    turned = sign * swap(z)
+    for part in range(2):
+        for k in range(0, count, 2 * TB):
+            vt_ref[part, :, k : k + 2 * TB] = jnp.transpose(v_ref[part, k : k + 2 * TB, :])
+
+    def project(q):
+        x = pieces(q)
+        return dot(x, v_ref[0]) + sign * swap(dot(x, v_ref[1]))
+
+    def expand(y):
+        z = dot(pieces(y), vt_ref[0]) - dot(pieces(sign * swap(y)), vt_ref[1])
+        return z * (mask * (1.0 / frames))
+
+    def step(_, z):
+        return expand(gram_schmidt(z, project(z), sign, order)[1])
+
+    z = lax.fori_loop(0, ITERS - 1, step, expand(project(basis_ref[...] * mask)))
+    q, y = gram_schmidt(z, project(z), sign, order)
+    turned = sign * swap(y)
     u = jnp.zeros_like(q)
     for k in range(RANK):
-        row_real = q[k : k + 1]
-        row_imag = q[RANK + k : RANK + k + 1]
-        first, second = inner(row_real, row_imag, z, turned)
-        u = u + (row_real * first + row_imag * second)
-    d = jnp.sum(u * q, axis=0, keepdims=True)
+        u = u + times(q, k, *inner(y[k : k + 1], y[RANK + k : RANK + k + 1], y, turned))
+    d = jnp.sum(u * q, axis=0, keepdims=True) * (1.0 / frames)
     floor = 0.1 * (jnp.sum(d, axis=1, keepdims=True) / count) + EPS
     gains = lax.rsqrt(jnp.maximum(d, floor))
     gains_ref[...] = gains
@@ -113,14 +117,19 @@
 
 
 def product(v_ref, tile):
-    frames = v_ref.shape[1] // 2
-    blocks = v_ref.shape[0] // TB
-    lhs = v_ref[pl.ds(pl.multiple_of((tile // blocks) * TB, TB), TB), :]
-    rhs = v_ref[pl.ds(pl.multiple_of(lax.rem(tile, blocks) * TB, TB), TB), :]
-    other = jnp.concatenate([lhs[:, frames:], -lhs[:, :frames]], axis=1)
-    both = jnp.concatenate([lhs, other], axis=0)
+    _, count, frames = v_ref.shape
+    blocks = count // TB
+    row = pl.ds(pl.multiple_of((tile // blocks) * TB, TB), TB)
+    col = pl.ds(pl.multiple_of(lax.rem(tile, blocks) * TB, TB), TB)
+    real, imag = v_ref[0, row, :], v_ref[1, row, :]
     dims = (((1,), (1,)), ((), ()))
-    return lax.dot_general(both, rhs, dims, preferred_element_type=jnp.float32) * (1.0 / frames)
+    both = lax.dot_general(
+        jnp.concatenate([real, imag], axis=0), v_ref[0, col, :], dims, preferred_element_type=jnp.float32
+    )
+    both = both + lax.dot_general(
+        jnp.concatenate([imag, -real], axis=0), v_ref[1, col, :], dims, preferred_element_type=jnp.float32
+    )
+    return both * (1.0 / frames)
 
 
 def outer(gains_ref, tile):
@@ -169,18 +178,22 @@
         copy.wait()
 
 
-def gather_mask(mask):
+def digits(parts):
+    stride = parts
+    while stride > 1:
+        radix = next(r for r in (4, 3, 2, stride) if stride % r == 0)
+        stride //= radix
+        yield stride, radix
+
+
+def sum_digit(x, stride, radix):
     parts = lax.axis_size("inp")
-    size = mask.shape[0]
-    whole = jnp.zeros((1, parts * size), mask.dtype)
-    whole = lax.dynamic_update_slice(whole, mask.reshape(1, size), (0, lax.axis_index("inp") * size))
-    if parts & (parts - 1):
-        return lax.psum(whole, "inp")
-    step = 1
-    while step < parts:
-        whole = whole + lax.ppermute(whole, "inp", [(j, (j + step) % parts) for j in range(parts)])
-        step *= 2
-    return whole
+    span = stride * radix
+    moved = []
+    for d in range(1, radix):
+        pairs = [(j, j // span * span + (j + d * stride) % span) for j in range(parts)]
+        moved.append(lax.ppermute(x, "inp", pairs))
+    return sum(moved, x)
 
 
 def in_vmem(x, owners=2):
@@ -190,11 +203,17 @@
 def body(volt, mask, table):
     owners = lax.axis_size("chan")
     slots = table.shape[0] // owners
-    full_mask = gather_mask(mask)
+    parts, size = lax.axis_size("inp"), mask.shape[0]
+    first, *later = digits(parts)
+    full_mask = jnp.zeros((1, parts * size), mask.dtype)
+    full_mask = lax.dynamic_update_slice(full_mask, mask.reshape(1, size), (0, lax.axis_index("inp") * size))
+    full_mask = sum_digit(full_mask, *first)
     turned = lax.all_to_all(volt, "inp", split_axis=0, concat_axis=1, tiled=True)[0]
     turned, full_mask = lax.optimization_barrier((turned, full_mask))
+    for digit in later:
+        full_mask = sum_digit(full_mask, *digit)
     count, _, frames = turned.shape
-    flat = in_vmem(turned.reshape(count, 2 * frames))
+    flat = in_vmem(jnp.transpose(turned, (1, 0, 2)))
     me = lax.axis_index("chan").reshape(1)
     blocks = count // TB
 
@@ -218,8 +237,9 @@
         ],
         in_specs=[VMEM] * 3,
         out_specs=[VMEM] * 2,
+        scratch_shapes=[pltpu.VMEM((2, frames, count), jnp.bfloat16)],
         name="calibrate",
-    )(flat, full_mask, first_basis(count))
+    )(flat, in_vmem(full_mask), first_basis(count))
     other_gains = [in_vmem(shift(masked, d), owners) for d in range(1, owners)]
 
     vis_shape = jax.ShapeDtypeStruct((owners, KPO, 2, TB, TB), jnp.bfloat16)

time: 94.3 us -> 80.7 us (0.86)
  Pallas kernels: 18.8 us -> 13.2 us
  waiting for transfers between devices: 53 us -> 47.9 us
  local copies, waits for them, and re-layouts: 3.8 us -> 2.36 us
    pallas_call x1, Pallas kernels: 13.7 us -> 8.2 us  [body(): pl.pallas_call(calibrate_kernel, out_shape=[jax.ShapeDtypeStruct((1, coun...]
    ppermute x4 -> x6, waiting for transfers between devices: 52.1 us -> 47 us  [sum_digit(): moved.append(lax.ppermute(x, 'inp', pairs))]
    unnamed x7 -> x4, local copies, waits for them, and re-layouts: 3.56 us -> 0.08 us
    all_to_all x0 -> x1, local copies, waits for them, and re-layouts: none -> 2.03 us  [body(): lax.all_to_all(volt, 'inp', split_axis=0, concat_axis=1, tiled=True)[0]]
    ppermute x4 -> x6, starting transfers between devices: 7.49 us -> 6.59 us  [sum_digit(): moved.append(lax.ppermute(x, 'inp', pairs))]
  transfers between devices with their start and end apart: 7 -> 9, of which waited for: 5 -> 5; matrix products, arithmetic and copies ran while one was open for 1% -> 0% of each run, Pallas kernels for 17% -> 13%
where the time goes in v3:
time: 80.7 us; the launch traced here: 80.4 us
  waiting for transfers between devices  47.9 us (59%)
  starting transfers between devices  16.1 us (20%)
  Pallas kernels  13.2 us (16%)
  local copies, waits for them, and re-layouts  2.36 us (3%)
    ppermute x6, waiting for transfers between devices, sum_digit(): moved.append(lax.ppermute(x, 'inp', pairs))  47 us
    pallas_call x1, Pallas kernels, body(): pl.pallas_call(calibrate_kernel, out_shape=[jax.ShapeDtypeStruct((1, coun...  8.2 us
    all_to_all x1, starting transfers between devices, body(): lax.all_to_all(volt, 'inp', split_axis=0, concat_axis=1, tiled=True)[0]  7.42 us
    ppermute x6, starting transfers between devices, sum_digit(): moved.append(lax.ppermute(x, 'inp', pairs))  6.59 us
    pallas_call x1, Pallas kernels, body(): pl.pallas_call(functools.partial(own_kernel, slots), out_shape=vis_shape,...  2.11 us
    ppermute x2, starting transfers between devices, shift(): lax.ppermute(x, 'chan', [(j, (j + d) % owners) for j in range(owners)])  2.09 us
    all_to_all x1, local copies, waits for them, and re-layouts, body(): lax.all_to_all(volt, 'inp', split_axis=0, concat_axis=1, tiled=True)[0]  2.03 us
  transfers between devices with their start and end apart: 9, of which 5 were waited for; matrix products, arithmetic and copies ran while one was open for 0% of the time, Pallas kernels for 13%

profile of v3, /device:TPU:0, one launch (start us, length us, event | category | flops | bytes accessed | tf_op | source)
XLA Modules:
  0.0 80.4 jit_solution(10154494115388774025)
XLA Ops:
  0.6 0.0 copy-start.1
  0.6 7.4 %all-to-all-start = ((bf16[16,64,2,512]{3,2,1,0:T(2,128)(2,1)}), bf16[16,64,2,512]{3,2,1,0:T(2,128)(2,1)}, u32[]{:S(2)}, u32[]{:S(2)}) async-start(bf16[16,64,2,512]{3,2,1,0:T(2,128)(2,1)} %param.4), calls=%async_computation | async-start | bytes 4194304 | tf_op jit(solution)/shard_map/all_to_all | solution.py:211
  8.1 0.0 copy-done.1
  8.1 0.2 dynamic_update_slice.5
  8.3 1.9 %collective-permute-start = (s32[1,1024]{1,0:T(1,128)S(1)}, s32[1,1024]{1,0:T(1,128)S(1)}, u32[]{:S(2)}, u32[]{:S(2)}) collective-permute-start(s32[1,1024]{1,0:T(1,128)S(1)} %dynamic_update_slice.5), channel_id=1, source_target_pairs={{0,8},{2,10},{4,12},{6,14},{8,16},{10,18},{12,20},{14,22},{16,24},... | collective-permute-start | bytes 12296 | tf_op jit(solution)/shard_map/ppermute | solution.py:195
  10.2 2.0 %collective-permute-start.2 = (s32[1,1024]{1,0:T(1,128)S(1)}, s32[1,1024]{1,0:T(1,128)S(1)}, u32[]{:S(2)}, u32[]{:S(2)}) collective-permute-start(s32[1,1024]{1,0:T(1,128)S(1)} %dynamic_update_slice.5), channel_id=1, source_target_pairs={{0,24},{2,26},{4,28},{6,30},{8,0},{10,2},{12,4},{14,6},{16,8},{18,... | collective-permute-start | bytes 12296 | tf_op jit(solution)/shard_map/ppermute | solution.py:195
  12.1 1.0 %collective-permute-start.1 = (s32[1,1024]{1,0:T(1,128)S(1)}, s32[1,1024]{1,0:T(1,128)S(1)}, u32[]{:S(2)}, u32[]{:S(2)}) collective-permute-start(s32[1,1024]{1,0:T(1,128)S(1)} %dynamic_update_slice.5), channel_id=1, source_target_pairs={{0,16},{2,18},{4,20},{6,22},{8,24},{10,26},{12,28},{14,30},{16,0},... | collective-permute-start | bytes 12296 | tf_op jit(solution)/shard_map/ppermute | solution.py:195
  13.1 34.0 %collective-permute-done = s32[1,1024]{1,0:T(1,128)S(1)} collective-permute-done((s32[1,1024]{1,0:T(1,128)S(1)}, s32[1,1024]{1,0:T(1,128)S(1)}, u32[]{:S(2)}, u32[]{:S(2)}) %collective-permute-start) | collective-permute-done | bytes 4128 | tf_op jit(solution)/shard_map/ppermute | solution.py:195
  47.1 0.1 dynamic-slice_add_fusion
  47.1 0.1 add.23
  47.2 0.0 collective-permute-done.2
  47.2 10.2 %collective-permute-done.1 = s32[1,1024]{1,0:T(1,128)S(1)} collective-permute-done((s32[1,1024]{1,0:T(1,128)S(1)}, s32[1,1024]{1,0:T(1,128)S(1)}, u32[]{:S(2)}, u32[]{:S(2)}) %collective-permute-start.1) | collective-permute-done | bytes 4128 | tf_op jit(solution)/shard_map/ppermute | solution.py:195
  57.4 0.0 all-to-all-done
  57.5 2.0 %copy.7 = bf16[16,64,2,512]{3,1,0,2:T(8,128)(2,1)S(1)} copy(bf16[16,64,2,512]{3,2,1,0:T(2,128)(2,1)} %all-to-all-done) | data formatting | bytes 4194304 | tf_op jit(solution)/shard_map/all_to_all | solution.py:211
  59.5 1.4 %sent.1 = f32[4,2,128,128]{3,2,1,0:T(8,128)S(1)} custom-call(s32[64]{0:T(128)} %table_ref.5, s32[1]{0:T(128)} %bitcast.me_ref, bf16[2,1024,512]{2,1,0:T(8,128)(2,1)S(1)} %bitcast.9), custom_call_target="tpu_custom_call" | custom-call | tf_op jit(solution)/shard_map/sent/pallas_call | solution.py:223
  60.9 1.6 %collective-permute-start.3 = (f32[4,2,128,128]{3,2,1,0:T(8,128)S(1)}, f32[4,2,128,128]{3,2,1,0:T(8,128)S(1)}, u32[]{:S(2)}, u32[]{:S(2)}) collective-permute-start(f32[4,2,128,128]{3,2,1,0:T(8,128)S(1)} %sent.1), channel_id=1, source_target_pairs={{0,1},{1,0},{2,3},{3,2},{4,5},{5,4},{6,7},{7,6},{8,9},{9,8},{10,11... | collective-permute-start | bytes 1572872 | tf_op jit(solution)/shard_map/ppermute | solution.py:221
  62.5 0.2 collective-permute-start.6
  62.6 1.3 %collective-permute-start.5 = (s32[1,1024]{1,0:T(1,128)S(1)}, s32[1,1024]{1,0:T(1,128)S(1)}, u32[]{:S(2)}, u32[]{:S(2)}) collective-permute-start(s32[1,1024]{1,0:T(1,128)S(1)} %add_add_fusion.1), channel_id=1, source_target_pairs={{0,4},{2,6},{4,0},{6,2},{8,12},{10,14},{12,8},{14,10},{16,20},{18,... | collective-permute-start | bytes 12296 | tf_op jit(solution)/shard_map/ppermute | solution.py:195
  64.0 0.2 collective-permute-start.4
  64.2 0.0 collective-permute-done.6
  64.2 2.0 %collective-permute-done.5 = s32[1,1024]{1,0:T(1,128)S(1)} collective-permute-done((s32[1,1024]{1,0:T(1,128)S(1)}, s32[1,1024]{1,0:T(1,128)S(1)}, u32[]{:S(2)}, u32[]{:S(2)}) %collective-permute-start.5) | collective-permute-done | bytes 4128 | tf_op jit(solution)/shard_map/ppermute | solution.py:195
  66.3 0.8 collective-permute-done.4
  67.0 8.2 %calibrate.1 = (f32[1,1024]{1,0:T(1,128)}, f32[8,128]{1,0:T(8,128)S(1)}) custom-call(bf16[2,1024,512]{2,1,0:T(8,128)(2,1)S(1)} %bitcast.10, s32[1,1024]{1,0:T(1,128)S(1)} %add_add_fusion.mask_ref, f32[8,1024]{1,0:T(8,128)} %constant.17.clone.basis_ref), custom_call_target="tpu_custom_call" | custom-call | tf_op jit(solution)/shard_map/calibrate/pallas_call | solution.py:232
  75.2 0.0 copy-start
  75.2 0.5 collective-permute-start.7
  75.7 0.1 copy-done
  75.8 2.1 %own.1.refs_2_ = bf16[2,4,2,128,128]{4,3,2,1,0:T(8,128)(2,1)} custom-call(s32[64]{0:T(128)} %table_ref.5, s32[1]{0:T(128)} %bitcast.me_ref, bf16[2,1024,512]{2,1,0:T(8,128)(2,1)S(1)} %bitcast.11, f32[8,128]{1,0:T(8,128)} %copy-done), custom_call_target="tpu_custom_call" | custom-call | tf_op jit(solution)/shard_map/own/pallas_call | solution.py:246
  77.9 0.9 %collective-permute-done.7.refs_1_ = f32[8,128]{1,0:T(8,128)S(1)} collective-permute-done((f32[8,128]{1,0:T(8,128)S(1)}, f32[8,128]{1,0:T(8,128)S(1)}, u32[]{:S(2)}, u32[]{:S(2)}) %collective-permute-start.7) | collective-permute-done | bytes 4128 | tf_op jit(solution)/shard_map/ppermute | solution.py:221
  78.8 0.0 collective-permute-done.3.refs_0_
  78.8 1.5 %others.1 = bf16[2,4,2,128,128]{4,3,2,1,0:T(8,128)(2,1)} custom-call(s32[64]{0:T(128)} %table_ref.5, s32[1]{0:T(128)} %bitcast.me_ref, f32[4,2,128,128]{3,2,1,0:T(8,128)S(1)} %collective-permute-done.3.refs_0_, f32[8,128]{1,0:T(8,128)S(1)} %collective-permute-done.7.refs_1_, bf16[2,4,2,128,128]{4,3,2,1,0:T(8,128)(2,1)} %own.1.refs_2_), custom_call_target="tpu_custom_call", output_to_operand_aliasing={{}: (4, {})} | custom-call | tf_op jit(solution)/shard_map/others/pallas_call | solution.py:254
  (3 shorter events, 0.0 us)
Async XLA Ops:
  0.6 7.5 %copy-start.1 = (s32[64]{0:T(128)S(1)}, s32[64]{0:T(128)}, u32[]{:S(2)}) copy-start(s32[64]{0:T(128)} %param.5) | copy-start | bytes 772
  0.6 56.8 %all-to-all-start = ((bf16[16,64,2,512]{3,2,1,0:T(2,128)(2,1)}), bf16[16,64,2,512]{3,2,1,0:T(2,128)(2,1)}, u32[]{:S(2)}, u32[]{:S(2)}) async-start(bf16[16,64,2,512]{3,2,1,0:T(2,128)(2,1)} %param.4), calls=%async_computation | async-start | bytes 4194304 | tf_op jit(solution)/shard_map/all_to_all | solution.py:211
  8.3 38.8 %collective-permute-start = (s32[1,1024]{1,0:T(1,128)S(1)}, s32[1,1024]{1,0:T(1,128)S(1)}, u32[]{:S(2)}, u32[]{:S(2)}) collective-permute-start(s32[1,1024]{1,0:T(1,128)S(1)} %dynamic_update_slice.5), channel_id=1, source_target_pairs={{0,8},{2,10},{4,12},{6,14},{8,16},{10,18},{12,20},{14,22},{16,24},... | collective-permute-start | bytes 12296 | tf_op jit(solution)/shard_map/ppermute | solution.py:195
  10.2 37.1 %collective-permute-start.2 = (s32[1,1024]{1,0:T(1,128)S(1)}, s32[1,1024]{1,0:T(1,128)S(1)}, u32[]{:S(2)}, u32[]{:S(2)}) collective-permute-start(s32[1,1024]{1,0:T(1,128)S(1)} %dynamic_update_slice.5), channel_id=1, source_target_pairs={{0,24},{2,26},{4,28},{6,30},{8,0},{10,2},{12,4},{14,6},{16,8},{18,... | collective-permute-start | bytes 12296 | tf_op jit(solution)/shard_map/ppermute | solution.py:195
  12.1 45.3 %collective-permute-start.1 = (s32[1,1024]{1,0:T(1,128)S(1)}, s32[1,1024]{1,0:T(1,128)S(1)}, u32[]{:S(2)}, u32[]{:S(2)}) collective-permute-start(s32[1,1024]{1,0:T(1,128)S(1)} %dynamic_update_slice.5), channel_id=1, source_target_pairs={{0,16},{2,18},{4,20},{6,22},{8,24},{10,26},{12,28},{14,30},{16,0},... | collective-permute-start | bytes 12296 | tf_op jit(solution)/shard_map/ppermute | solution.py:195
  60.9 18.0 %collective-permute-start.3 = (f32[4,2,128,128]{3,2,1,0:T(8,128)S(1)}, f32[4,2,128,128]{3,2,1,0:T(8,128)S(1)}, u32[]{:S(2)}, u32[]{:S(2)}) collective-permute-start(f32[4,2,128,128]{3,2,1,0:T(8,128)S(1)} %sent.1), channel_id=1, source_target_pairs={{0,1},{1,0},{2,3},{3,2},{4,5},{5,4},{6,7},{7,6},{8,9},{9,8},{10,11... | collective-permute-start | bytes 1572872 | tf_op jit(solution)/shard_map/ppermute | solution.py:221
  62.5 1.7 %collective-permute-start.6 = (s32[1,1024]{1,0:T(1,128)S(1)}, s32[1,1024]{1,0:T(1,128)S(1)}, u32[]{:S(2)}, u32[]{:S(2)}) collective-permute-start(s32[1,1024]{1,0:T(1,128)S(1)} %add_add_fusion.1), channel_id=1, source_target_pairs={{0,6},{2,0},{4,2},{6,4},{8,14},{10,8},{12,10},{14,12},{16,22},{18,... | collective-permute-start | bytes 12296 | tf_op jit(solution)/shard_map/ppermute | solution.py:195
  62.6 3.6 %collective-permute-start.5 = (s32[1,1024]{1,0:T(1,128)S(1)}, s32[1,1024]{1,0:T(1,128)S(1)}, u32[]{:S(2)}, u32[]{:S(2)}) collective-permute-start(s32[1,1024]{1,0:T(1,128)S(1)} %add_add_fusion.1), channel_id=1, source_target_pairs={{0,4},{2,6},{4,0},{6,2},{8,12},{10,14},{12,8},{14,10},{16,20},{18,... | collective-permute-start | bytes 12296 | tf_op jit(solution)/shard_map/ppermute | solution.py:195
  64.0 3.0 %collective-permute-start.4 = (s32[1,1024]{1,0:T(1,128)S(1)}, s32[1,1024]{1,0:T(1,128)S(1)}, u32[]{:S(2)}, u32[]{:S(2)}) collective-permute-start(s32[1,1024]{1,0:T(1,128)S(1)} %add_add_fusion.1), channel_id=1, source_target_pairs={{0,2},{2,4},{4,6},{6,0},{8,10},{10,12},{12,14},{14,8},{16,18},{18,... | collective-permute-start | bytes 12296 | tf_op jit(solution)/shard_map/ppermute | solution.py:195
  75.2 0.6 copy-start
  75.2 3.6 %collective-permute-start.7 = (f32[8,128]{1,0:T(8,128)S(1)}, f32[8,128]{1,0:T(8,128)S(1)}, u32[]{:S(2)}, u32[]{:S(2)}) collective-permute-start(f32[8,128]{1,0:T(8,128)S(1)} %get-tuple-element.8.gains_ref), channel_id=1, source_target_pairs={{0,1},{1,0},{2,3},{3,2},{4,5},{5,4},{6,7},{7,6},{8,9},{9,8},{10,11... | collective-permute-start | bytes 12296 | tf_op jit(solution)/shard_map/ppermute | solution.py:221

commit v4 on v3

--- a/solution.py
+++ b/solution.py
@@ -80,28 +80,31 @@
     return w * scales, p * scales
 
 
-def calibrate_kernel(v_ref, mask_ref, basis_ref, gains_ref, masked_ref, vt_ref):
-    _, count, frames = v_ref.shape
-    mask = mask_ref[...].astype(jnp.float32)
+def calibrate_kernel(v_ref, basis_ref, gains_ref, blocks_ref, vt_ref):
+    parts, _, size, frames = v_ref.shape
+    count = parts * size
     rows = lax.broadcasted_iota(jnp.int32, (2 * RANK, 1), 0)
     sign = jnp.where(rows < RANK, 1.0, -1.0)
     order = jnp.where(rows < RANK, rows, rows - RANK)
+    group = 2 * TB // size
     for part in range(2):
-        for k in range(0, count, 2 * TB):
-            vt_ref[part, :, k : k + 2 * TB] = jnp.transpose(v_ref[part, k : k + 2 * TB, :])
+        for k in range(0, parts, group):
+            rows_k = v_ref[k : k + group, part].reshape(group * size, frames)
+            vt_ref[part, :, k * size : (k + group) * size] = jnp.transpose(rows_k)
 
     def project(q):
         x = pieces(q)
-        return dot(x, v_ref[0]) + sign * swap(dot(x, v_ref[1]))
+        real, imag = (v_ref[:, part].reshape(count, frames) for part in range(2))
+        return dot(x, real) + sign * swap(dot(x, imag))
 
     def expand(y):
         z = dot(pieces(y), vt_ref[0]) - dot(pieces(sign * swap(y)), vt_ref[1])
-        return z * (mask * (1.0 / frames))
+        return z * (1.0 / frames)
 
     def step(_, z):
         return expand(gram_schmidt(z, project(z), sign, order)[1])
 
-    z = lax.fori_loop(0, ITERS - 1, step, expand(project(basis_ref[...] * mask)))
+    z = lax.fori_loop(0, ITERS - 1, step, expand(project(basis_ref[...])))
     q, y = gram_schmidt(z, project(z), sign, order)
     turned = sign * swap(y)
     u = jnp.zeros_like(q)
@@ -111,23 +114,23 @@
     floor = 0.1 * (jnp.sum(d, axis=1, keepdims=True) / count) + EPS
     gains = lax.rsqrt(jnp.maximum(d, floor))
     gains_ref[...] = gains
-    masked = gains * mask
     for k in range(count // TB):
-        masked_ref[k : k + 1, :] = masked[:, k * TB : (k + 1) * TB]
+        blocks_ref[k : k + 1, :] = gains[:, k * TB : (k + 1) * TB]
 
 
 def product(v_ref, tile):
-    _, count, frames = v_ref.shape
-    blocks = count // TB
-    row = pl.ds(pl.multiple_of((tile // blocks) * TB, TB), TB)
-    col = pl.ds(pl.multiple_of(lax.rem(tile, blocks) * TB, TB), TB)
-    real, imag = v_ref[0, row, :], v_ref[1, row, :]
+    parts, _, size, frames = v_ref.shape
+    blocks = parts * size // TB
+    group = TB // size
+    row = pl.ds((tile // blocks) * group, group)
+    col = pl.ds(lax.rem(tile, blocks) * group, group)
+    real, imag, col_real, col_imag = (v_ref[k, part].reshape(TB, frames) for k in (row, col) for part in range(2))
     dims = (((1,), (1,)), ((), ()))
     both = lax.dot_general(
-        jnp.concatenate([real, imag], axis=0), v_ref[0, col, :], dims, preferred_element_type=jnp.float32
+        jnp.concatenate([real, imag], axis=0), col_real, dims, preferred_element_type=jnp.float32
     )
     both = both + lax.dot_general(
-        jnp.concatenate([imag, -real], axis=0), v_ref[1, col, :], dims, preferred_element_type=jnp.float32
+        jnp.concatenate([imag, -real], axis=0), col_imag, dims, preferred_element_type=jnp.float32
     )
     return both * (1.0 / frames)
 
@@ -178,24 +181,6 @@
         copy.wait()
 
 
-def digits(parts):
-    stride = parts
-    while stride > 1:
-        radix = next(r for r in (4, 3, 2, stride) if stride % r == 0)
-        stride //= radix
-        yield stride, radix
-
-
-def sum_digit(x, stride, radix):
-    parts = lax.axis_size("inp")
-    span = stride * radix
-    moved = []
-    for d in range(1, radix):
-        pairs = [(j, j // span * span + (j + d * stride) % span) for j in range(parts)]
-        moved.append(lax.ppermute(x, "inp", pairs))
-    return sum(moved, x)
-
-
 def in_vmem(x, owners=2):
     return x if owners > 2 else pltpu.with_memory_space_constraint(x, pltpu.VMEM)
 
@@ -203,17 +188,11 @@
 def body(volt, mask, table):
     owners = lax.axis_size("chan")
     slots = table.shape[0] // owners
-    parts, size = lax.axis_size("inp"), mask.shape[0]
-    first, *later = digits(parts)
-    full_mask = jnp.zeros((1, parts * size), mask.dtype)
-    full_mask = lax.dynamic_update_slice(full_mask, mask.reshape(1, size), (0, lax.axis_index("inp") * size))
-    full_mask = sum_digit(full_mask, *first)
-    turned = lax.all_to_all(volt, "inp", split_axis=0, concat_axis=1, tiled=True)[0]
-    turned, full_mask = lax.optimization_barrier((turned, full_mask))
-    for digit in later:
-        full_mask = sum_digit(full_mask, *digit)
-    count, _, frames = turned.shape
-    flat = in_vmem(jnp.transpose(turned, (1, 0, 2)))
+    masked = jnp.transpose(volt, (0, 2, 1, 3)) * mask.astype(jnp.bfloat16)[None, None, :, None]
+    turned = lax.all_to_all(masked, "inp", split_axis=0, concat_axis=0, tiled=True)
+    parts, _, size, frames = turned.shape
+    count = parts * size
+    flat = in_vmem(turned)
     me = lax.axis_index("chan").reshape(1)
     blocks = count // TB
 
@@ -229,18 +208,18 @@
     )(table, me, flat)
     arrived = [in_vmem(shift(sent[d - 1], d), owners) for d in range(1, owners)]
 
-    gains, masked = pl.pallas_call(
+    gains, by_block = pl.pallas_call(
         calibrate_kernel,
         out_shape=[
             jax.ShapeDtypeStruct((1, count), jnp.float32),
             pltpu.VMEM((blocks, TB), jnp.float32),
         ],
-        in_specs=[VMEM] * 3,
+        in_specs=[VMEM] * 2,
         out_specs=[VMEM] * 2,
         scratch_shapes=[pltpu.VMEM((2, frames, count), jnp.bfloat16)],
         name="calibrate",
-    )(flat, in_vmem(full_mask), first_basis(count))
-    other_gains = [in_vmem(shift(masked, d), owners) for d in range(1, owners)]
+    )(flat, first_basis(count))
+    other_gains = [in_vmem(shift(by_block, d), owners) for d in range(1, owners)]
 
     vis_shape = jax.ShapeDtypeStruct((owners, KPO, 2, TB, TB), jnp.bfloat16)
     vis = pl.pallas_call(
@@ -250,7 +229,7 @@
         out_specs=ANY,
         scratch_shapes=[pltpu.VMEM((KPO, 2, TB, TB), jnp.bfloat16), pltpu.SemaphoreType.DMA],
         name="own",
-    )(table, me, flat, masked)
+    )(table, me, flat, by_block)
     vis = pl.pallas_call(
         functools.partial(others_kernel, owners, slots),
         out_shape=vis_shape,

time: 80.7 us -> 75.5 us (0.936)
  the two profiles are of different devices: /device:TPU:0 before, /device:TPU:10 now
where the time goes in v4:
time: 75.5 us; the launch traced here: 75.2 us
  waiting for transfers between devices  49 us (65%)
  Pallas kernels  13.2 us (17%)
  starting transfers between devices  8.33 us (11%)
  other arithmetic  3.88 us (5%)
    all_to_all x1, waiting for transfers between devices, body(): lax.all_to_all(masked, 'inp', split_axis=0, concat_axis=0, tiled=True)  47.3 us
    pallas_call x1, Pallas kernels, body(): pl.pallas_call(calibrate_kernel, out_shape=[jax.ShapeDtypeStruct((1, coun...  8.2 us
    all_to_all x1, starting transfers between devices, body(): lax.all_to_all(masked, 'inp', split_axis=0, concat_axis=0, tiled=True)  6.24 us
    mul x1, other arithmetic, body(): jnp.transpose(volt, (0, 2, 1, 3))  3.22 us
    pallas_call x1, Pallas kernels, body(): pl.pallas_call(functools.partial(own_kernel, slots), out_shape=vis_shape,...  2.12 us
    ppermute x2, starting transfers between devices, shift(): lax.ppermute(x, 'chan', [(j, (j + d) % owners) for j in range(owners)])  2.09 us
    ppermute x2, waiting for transfers between devices, shift(): lax.ppermute(x, 'chan', [(j, (j + d) % owners) for j in range(owners)])  1.77 us
    pallas_call x1, Pallas kernels, body(): pl.pallas_call(functools.partial(others_kernel, owners, slots), out_shape...  1.53 us
  transfers between devices with their start and end apart: 3, of which 2 were waited for; matrix products, arithmetic and copies ran while one was open for 0% of the time, Pallas kernels for 14%

profile of v4, /device:TPU:10, one launch (start us, length us, event | category | flops | bytes accessed | tf_op | source)
XLA Modules:
  0.0 75.2 jit_solution(4326153506865850784)
XLA Ops:
  0.6 0.7 convert_element_type.3
  1.3 3.2 %fusion = bf16[16,2,64,512]{3,2,1,0:T(8,128)(2,1)} fusion(bf16[16,64,2,512]{3,2,1,0:T(2,128)(2,1)} %param.4, bf16[64]{0:T(256)(128)(2,1)S(1)} %convert_element_type.3), kind=kLoop, calls=%fused_computation.1 | loop fusion | flops 1048576 | bytes 4194432 | tf_op jit(solution)/shard_map/mul | solution.py:191
  4.5 6.2 %all-to-all-start = ((bf16[16,2,64,512]{3,2,1,0:T(8,128)(2,1)}), bf16[16,2,64,512]{3,2,1,0:T(8,128)(2,1)S(1)}, u32[]{:S(2)}, u32[]{:S(2)}) async-start(bf16[16,2,64,512]{3,2,1,0:T(8,128)(2,1)} %fusion), calls=%async_computation | async-start | bytes 4194304 | tf_op jit(solution)/shard_map/all_to_all | solution.py:192
  10.8 47.3 %all-to-all-done.v_ref = bf16[16,2,64,512]{3,2,1,0:T(8,128)(2,1)S(1)} async-done(((bf16[16,2,64,512]{3,2,1,0:T(8,128)(2,1)}), bf16[16,2,64,512]{3,2,1,0:T(8,128)(2,1)S(1)}, u32[]{:S(2)}, u32[]{:S(2)}) %all-to-all-start) | async-done | bytes 2097184 | tf_op jit(solution)/shard_map/all_to_all | solution.py:192
  58.0 1.4 %sent.1 = f32[4,2,128,128]{3,2,1,0:T(8,128)S(1)} custom-call(s32[64]{0:T(128)} %table_ref.5, s32[1]{0:T(128)} %bitcast.me_ref, bf16[16,2,64,512]{3,2,1,0:T(8,128)(2,1)S(1)} %all-to-all-done.v_ref), custom_call_target="tpu_custom_call" | custom-call | tf_op jit(solution)/shard_map/sent/pallas_call | solution.py:202
  59.4 1.6 %collective-permute-start = (f32[4,2,128,128]{3,2,1,0:T(8,128)S(1)}, f32[4,2,128,128]{3,2,1,0:T(8,128)S(1)}, u32[]{:S(2)}, u32[]{:S(2)}) collective-permute-start(f32[4,2,128,128]{3,2,1,0:T(8,128)S(1)} %sent.1), channel_id=1, source_target_pairs={{0,1},{1,0},{2,3},{3,2},{4,5},{5,4},{6,7},{7,6},{8,9},{9,8},{10,11... | collective-permute-start | bytes 1572872 | tf_op jit(solution)/shard_map/ppermute | solution.py:200
  61.0 8.2 %calibrate.1 = (f32[1,1024]{1,0:T(1,128)}, f32[8,128]{1,0:T(8,128)S(1)}) custom-call(bf16[16,2,64,512]{3,2,1,0:T(8,128)(2,1)S(1)} %all-to-all-done.v_ref, f32[8,1024]{1,0:T(8,128)} %constant.6.clone.basis_ref), custom_call_target="tpu_custom_call" | custom-call | tf_op jit(solution)/shard_map/calibrate/pallas_call | solution.py:211
  69.2 0.0 copy-start
  69.2 0.5 collective-permute-start.1
  69.7 0.1 copy-done
  69.8 2.1 %own.1.refs_2_ = bf16[2,4,2,128,128]{4,3,2,1,0:T(8,128)(2,1)} custom-call(s32[64]{0:T(128)} %table_ref.5, s32[1]{0:T(128)} %bitcast.me_ref, bf16[16,2,64,512]{3,2,1,0:T(8,128)(2,1)S(1)} %all-to-all-done.v_ref, f32[8,128]{1,0:T(8,128)} %copy-done), custom_call_target="tpu_custom_call" | custom-call | tf_op jit(solution)/shard_map/own/pallas_call | solution.py:225
  71.9 1.8 %collective-permute-done.1.refs_1_ = f32[8,128]{1,0:T(8,128)S(1)} collective-permute-done((f32[8,128]{1,0:T(8,128)S(1)}, f32[8,128]{1,0:T(8,128)S(1)}, u32[]{:S(2)}, u32[]{:S(2)}) %collective-permute-start.1) | collective-permute-done | bytes 4128 | tf_op jit(solution)/shard_map/ppermute | solution.py:200
  73.7 0.0 collective-permute-done.refs_0_
  73.7 1.5 %others.1 = bf16[2,4,2,128,128]{4,3,2,1,0:T(8,128)(2,1)} custom-call(s32[64]{0:T(128)} %table_ref.5, s32[1]{0:T(128)} %bitcast.me_ref, f32[4,2,128,128]{3,2,1,0:T(8,128)S(1)} %collective-permute-done.refs_0_, f32[8,128]{1,0:T(8,128)S(1)} %collective-permute-done.1.refs_1_, bf16[2,4,2,128,128]{4,3,2,1,0:T(8,128)(2,1)} %own.1.refs_2_), custom_call_target="tpu_custom_call", output_to_operand_aliasing={{}: (4, {})} | custom-call | tf_op jit(solution)/shard_map/others/pallas_call | solution.py:233
Async XLA Ops:
  4.5 53.5 %all-to-all-start = ((bf16[16,2,64,512]{3,2,1,0:T(8,128)(2,1)}), bf16[16,2,64,512]{3,2,1,0:T(8,128)(2,1)S(1)}, u32[]{:S(2)}, u32[]{:S(2)}) async-start(bf16[16,2,64,512]{3,2,1,0:T(8,128)(2,1)} %fusion), calls=%async_computation | async-start | bytes 4194304 | tf_op jit(solution)/shard_map/all_to_all | solution.py:192
  59.4 14.3 %collective-permute-start = (f32[4,2,128,128]{3,2,1,0:T(8,128)S(1)}, f32[4,2,128,128]{3,2,1,0:T(8,128)S(1)}, u32[]{:S(2)}, u32[]{:S(2)}) collective-permute-start(f32[4,2,128,128]{3,2,1,0:T(8,128)S(1)} %sent.1), channel_id=1, source_target_pairs={{0,1},{1,0},{2,3},{3,2},{4,5},{5,4},{6,7},{7,6},{8,9},{9,8},{10,11... | collective-permute-start | bytes 1572872 | tf_op jit(solution)/shard_map/ppermute | solution.py:200
  69.2 0.6 copy-start
  69.2 4.5 %collective-permute-start.1 = (f32[8,128]{1,0:T(8,128)S(1)}, f32[8,128]{1,0:T(8,128)S(1)}, u32[]{:S(2)}, u32[]{:S(2)}) collective-permute-start(f32[8,128]{1,0:T(8,128)S(1)} %get-tuple-element.4.gains_ref), channel_id=1, source_target_pairs={{0,1},{1,0},{2,3},{3,2},{4,5},{5,4},{6,7},{7,6},{8,9},{9,8},{10,11... | collective-permute-start | bytes 12296 | tf_op jit(solution)/shard_map/ppermute | solution.py:200

commit v5 on v4

--- a/solution.py
+++ b/solution.py
@@ -14,10 +14,13 @@
 ITERS = 8
 KPO = 4
 EPS = 1e-06
+LANES = 128
+GROUP = 4
 SPLITS = 2
 
 VMEM = pl.BlockSpec(memory_space=pltpu.VMEM)
 ANY = pl.BlockSpec(memory_space=pl.ANY)
+HBM = pl.BlockSpec(memory_space=pltpu.HBM)
 SMEM = pl.BlockSpec(memory_space=pltpu.SMEM)
 
 
@@ -80,22 +83,20 @@
     return w * scales, p * scales
 
 
-def calibrate_kernel(v_ref, basis_ref, gains_ref, blocks_ref, vt_ref):
-    parts, _, size, frames = v_ref.shape
-    count = parts * size
+def calibrate_kernel(v_ref, basis_ref, gains_ref, blocks_ref, vt_ref, first, sem):
+    _, count, frames = v_ref.shape
+    copy = pltpu.make_async_copy(basis_ref, first, sem)
+    copy.start()
     rows = lax.broadcasted_iota(jnp.int32, (2 * RANK, 1), 0)
     sign = jnp.where(rows < RANK, 1.0, -1.0)
     order = jnp.where(rows < RANK, rows, rows - RANK)
-    group = 2 * TB // size
     for part in range(2):
-        for k in range(0, parts, group):
-            rows_k = v_ref[k : k + group, part].reshape(group * size, frames)
-            vt_ref[part, :, k * size : (k + group) * size] = jnp.transpose(rows_k)
+        for k in range(0, count, 2 * TB):
+            vt_ref[part, :, k : k + 2 * TB] = jnp.transpose(v_ref[part, k : k + 2 * TB, :])
 
     def project(q):
         x = pieces(q)
-        real, imag = (v_ref[:, part].reshape(count, frames) for part in range(2))
-        return dot(x, real) + sign * swap(dot(x, imag))
+        return dot(x, v_ref[0]) + sign * swap(dot(x, v_ref[1]))
 
     def expand(y):
         z = dot(pieces(y), vt_ref[0]) - dot(pieces(sign * swap(y)), vt_ref[1])
@@ -104,7 +105,8 @@
     def step(_, z):
         return expand(gram_schmidt(z, project(z), sign, order)[1])
 
-    z = lax.fori_loop(0, ITERS - 1, step, expand(project(basis_ref[...])))
+    copy.wait()
+    z = lax.fori_loop(0, ITERS - 1, step, expand(project(first[...])))
     q, y = gram_schmidt(z, project(z), sign, order)
     turned = sign * swap(y)
     u = jnp.zeros_like(q)
@@ -119,12 +121,11 @@
 
 
 def product(v_ref, tile):
-    parts, _, size, frames = v_ref.shape
-    blocks = parts * size // TB
-    group = TB // size
-    row = pl.ds((tile // blocks) * group, group)
-    col = pl.ds(lax.rem(tile, blocks) * group, group)
-    real, imag, col_real, col_imag = (v_ref[k, part].reshape(TB, frames) for k in (row, col) for part in range(2))
+    _, count, frames = v_ref.shape
+    blocks = count // TB
+    row = pl.ds(pl.multiple_of((tile // blocks) * TB, TB), TB)
+    col = pl.ds(pl.multiple_of(lax.rem(tile, blocks) * TB, TB), TB)
+    real, imag, col_real, col_imag = (v_ref[part, k, :] for k in (row, col) for part in range(2))
     dims = (((1,), (1,)), ((), ()))
     both = lax.dot_general(
         jnp.concatenate([real, imag], axis=0), col_real, dims, preferred_element_type=jnp.float32
@@ -140,6 +141,105 @@
     row = gains_ref[pl.ds(tile // blocks, 1), :]
     col = gains_ref[pl.ds(lax.rem(tile, blocks), 1), :]
     return jnp.transpose(jnp.broadcast_to(row, (TB, TB))) * col
+
+
+def front_kernel(targets, per, me_ref, mask_ref, volt_ref, *refs):
+    out_refs, (taken, flags, sem) = refs[: len(targets)], refs[len(targets) :]
+    parts, size, frames = out_refs[0].shape
+    cols = frames // LANES
+    rows = per * cols * parts
+    chunk = taken.shape[1]
+    copies = []
+    for k, d in enumerate(targets):
+        start = pl.multiple_of(lax.bitwise_xor(me_ref[0], d) * chunk, chunk)
+        copies.append(pltpu.make_async_copy(volt_ref.at[pl.ds(start, chunk)], taken.at[k], sem.at[k]))
+        copies[-1].start()
+    flag_copy = pltpu.make_async_copy(mask_ref, flags, sem.at[len(targets)])
+    flag_copy.start()
+    row = lax.broadcasted_iota(jnp.int32, (rows, rows), 0)
+    col = lax.broadcasted_iota(jnp.int32, (rows, rows), 1)
+    block = lax.div(row, per)
+    source = (lax.rem(row, per) * cols + lax.rem(block, cols)) * parts + lax.div(block, cols)
+    lane = lax.broadcasted_iota(jnp.int32, (size, rows), 1)
+    place = lax.broadcasted_iota(jnp.int32, (size, rows), 0)
+    flag_copy.wait()
+    mask = flags[...].astype(jnp.bfloat16)
+    selects = []
+    for g in range(0, size, per):
+        spread = (lax.div(lane, cols * parts) + g == place).astype(jnp.bfloat16)
+        kept = jnp.dot(mask, spread, preferred_element_type=jnp.float32)
+        selects.append(jnp.where(col == source, kept, 0.0).astype(jnp.bfloat16))
+    for copy in copies:
+        copy.wait()
+    for k in range(len(targets)):
+        for g, select in enumerate(selects):
+            x = taken[k, g * rows : (g + 1) * rows, :]
+            y = jnp.dot(select, x, preferred_element_type=jnp.float32).astype(jnp.bfloat16)
+            for p in range(parts):
+                for c in range(cols):
+                    at = (p * cols + c) * per
+                    out_refs[k][p, g * per : (g + 1) * per, c * LANES : (c + 1) * LANES] = y[at : at + per]
+
+
+def join_kernel(order, me_ref, *refs):
+    v_ref = refs[-1]
+    size = refs[0].shape[1]
+    for d, block_ref in zip(order, refs[:-1]):
+        start = pl.multiple_of(lax.bitwise_xor(me_ref[0], d) * size, size)
+        v_ref[:, pl.ds(start, size), :] = block_ref[...]
+
+
+def corner_turn(volt, mask):
+    parts = lax.axis_size("inp")
+    _, size, both, frames = volt.shape
+    me = lax.axis_index("inp").reshape(1)
+    cols = frames // LANES
+    chunk = size * cols * both
+    rows = volt.reshape(parts, size, both, cols, LANES).transpose(0, 1, 3, 2, 4).reshape(parts * chunk, LANES)
+    near = list(range(1, parts // 2))
+    far = list(range(parts // 2, parts))
+    order = [far[0]]
+    for k in range(len(near)):
+        order += [far[k + 1], near[k]]
+    order.append(0)
+    shape = (both, size, frames)
+    blocks = []
+    groups = [order[at : at + GROUP] for at in range(0, parts, GROUP)]
+    order = sum(reversed(groups), [])
+    for at in range(0, parts, GROUP):
+        targets = order[at : at + GROUP]
+        fronts = pl.pallas_call(
+            functools.partial(front_kernel, targets, min(size, 16)),
+            out_shape=[small(parts)(shape, volt.dtype)] * len(targets),
+            in_specs=[SMEM, HBM, HBM],
+            out_specs=[VMEM] * len(targets),
+            scratch_shapes=[
+                pltpu.VMEM((len(targets), chunk, LANES), volt.dtype),
+                pltpu.VMEM((1, size), mask.dtype),
+                pltpu.SemaphoreType.DMA((len(targets) + 1,)),
+            ],
+            compiler_params=pltpu.CompilerParams(vmem_limit_bytes=8 << 20),
+            name="front",
+        )(me, in_hbm(mask.reshape(1, size)), in_hbm(rows))
+        for d, block in zip(targets, fronts):
+            pairs = [(j, j ^ d) for j in range(parts)]
+            blocks.append(lax.ppermute(block, "inp", pairs) if d else block)
+    return pl.pallas_call(
+        functools.partial(join_kernel, order),
+        out_shape=pltpu.VMEM((both, parts * size, frames), volt.dtype),
+        in_specs=[SMEM] + [VMEM] * parts,
+        out_specs=VMEM,
+        compiler_params=pltpu.CompilerParams(vmem_limit_bytes=4 << 20),
+        name="join",
+    )(me, *[in_vmem(block, parts // 8) for block in blocks])
+
+
+def in_hbm(x):
+    return pltpu.with_memory_space_constraint(x, pltpu.HBM)
+
+
+def small(parts):
+    return pltpu.VMEM if parts <= 16 else jax.ShapeDtypeStruct
 
 
 def sent_kernel(owners, slots, table_ref, me_ref, v_ref, *out_refs):
@@ -188,11 +288,8 @@
 def body(volt, mask, table):
     owners = lax.axis_size("chan")
     slots = table.shape[0] // owners
-    masked = jnp.transpose(volt, (0, 2, 1, 3)) * mask.astype(jnp.bfloat16)[None, None, :, None]
-    turned = lax.all_to_all(masked, "inp", split_axis=0, concat_axis=0, tiled=True)
-    parts, _, size, frames = turned.shape
-    count = parts * size
-    flat = in_vmem(turned)
+    flat = in_vmem(corner_turn(volt, mask))
+    _, count, frames = flat.shape
     me = lax.axis_index("chan").reshape(1)
     blocks = count // TB
 
@@ -204,6 +301,7 @@
         out_shape=[(pltpu.VMEM if owners == 2 else jax.ShapeDtypeStruct)((KPO, 2, TB, TB), jnp.float32)] * (owners - 1),
         in_specs=[SMEM, SMEM, VMEM],
         out_specs=[VMEM] * (owners - 1),
+        compiler_params=pltpu.CompilerParams(vmem_limit_bytes=12 << 20),
         name="sent",
     )(table, me, flat)
     arrived = [in_vmem(shift(sent[d - 1], d), owners) for d in range(1, owners)]
@@ -214,11 +312,16 @@
             jax.ShapeDtypeStruct((1, count), jnp.float32),
             pltpu.VMEM((blocks, TB), jnp.float32),
         ],
-        in_specs=[VMEM] * 2,
+        in_specs=[VMEM, HBM],
         out_specs=[VMEM] * 2,
-        scratch_shapes=[pltpu.VMEM((2, frames, count), jnp.bfloat16)],
+        scratch_shapes=[
+            pltpu.VMEM((2, frames, count), jnp.bfloat16),
+            pltpu.VMEM((2 * RANK, count), jnp.float32),
+            pltpu.SemaphoreType.DMA,
+        ],
+        compiler_params=pltpu.CompilerParams(vmem_limit_bytes=12 << 20),
         name="calibrate",
-    )(flat, first_basis(count))
+    )(flat, in_hbm(jnp.asarray(first_basis(count))))
     other_gains = [in_vmem(shift(by_block, d), owners) for d in range(1, owners)]
 
     vis_shape = jax.ShapeDtypeStruct((owners, KPO, 2, TB, TB), jnp.bfloat16)
@@ -228,6 +331,7 @@
         in_specs=[SMEM, SMEM, VMEM, VMEM],
         out_specs=ANY,
         scratch_shapes=[pltpu.VMEM((KPO, 2, TB, TB), jnp.bfloat16), pltpu.SemaphoreType.DMA],
+        compiler_params=pltpu.CompilerParams(vmem_limit_bytes=12 << 20),
         name="own",
     )(table, me, flat, by_block)
     vis = pl.pallas_call(
@@ -240,6 +344,7 @@
             pltpu.SemaphoreType.DMA((owners - 1,)),
         ],
         input_output_aliases={2 * owners: 0},
+        compiler_params=pltpu.CompilerParams(vmem_limit_bytes=12 << 20),
         name="others",
     )(table, me, *arrived, *other_gains, vis)
     return (vis[None, :, None], gains.reshape(1, 1, count))

time: 75.5 us -> 70.6 us (0.935)
  the two profiles are of different devices: /device:TPU:10 before, /device:TPU:0 now
where the time goes in v5:
time: 70.6 us; the launch traced here: 70.2 us
  starting transfers between devices  34.9 us (49%)
  Pallas kernels  18.8 us (27%)
  waiting for transfers between devices  15.3 us (22%)
  between operations  0.72 us (1%)
    ppermute x15, starting transfers between devices, corner_turn(): blocks.append(lax.ppermute(block, 'inp', pairs) if d else block)  32.7 us
    ppermute x15, waiting for transfers between devices, corner_turn(): blocks.append(lax.ppermute(block, 'inp', pairs) if d else block)  13.7 us
    pallas_call x1, Pallas kernels, body(): pl.pallas_call(calibrate_kernel, out_shape=[jax.ShapeDtypeStruct((1, coun...  8.29 us
    pallas_call x4, Pallas kernels, corner_turn(): pl.pallas_call(functools.partial(front_kernel, targets, min(size, 16)), o...  5.74 us
    ppermute x2, starting transfers between devices, shift(): lax.ppermute(x, 'chan', [(j, (j + d) % owners) for j in range(owners)])  2.16 us
    pallas_call x1, Pallas kernels, body(): pl.pallas_call(functools.partial(own_kernel, slots), out_shape=vis_shape,...  1.97 us
    ppermute x2, waiting for transfers between devices, shift(): lax.ppermute(x, 'chan', [(j, (j + d) % owners) for j in range(owners)])  1.6 us
  transfers between devices with their start and end apart: 17, of which 7 were waited for; matrix products, arithmetic and copies ran while one was open for 0% of the time, Pallas kernels for 21%

profile of v5, /device:TPU:0, one launch (start us, length us, event | category | flops | bytes accessed | tf_op | source)
XLA Modules:
  0.0 70.2 jit_solution(5080092861113844599)
XLA Ops:
  0.6 1.4 %front.7 = (bf16[2,64,512]{2,1,0:T(8,128)(2,1)S(1)}, bf16[2,64,512]{2,1,0:T(8,128)(2,1)S(1)}, bf16[2,64,512]{2,1,0:T(8,128)(2,1)S(1)}, bf16[2,64,512]{2,1,0:T(8,128)(2,1)S(1)}) custom-call(s32[1]{0:T(128)} %bitcast.1.me_ref, s32[1,64]{1,0:T(1,128)} %bitcast.17, bf16[8192,128]{1,0:T(8,128)(2,1)} %bitcast.12), custom_call_target="tpu_custom_call" | custom-call | tf_op jit(solution)/shard_map/front/pallas_call | solution.py:211
  2.1 4.1 %collective-permute-start.11 = (bf16[2,64,512]{2,1,0:T(8,128)(2,1)S(1)}, bf16[2,64,512]{2,1,0:T(8,128)(2,1)S(1)}, u32[]{:S(2)}, u32[]{:S(2)}) collective-permute-start(bf16[2,64,512]{2,1,0:T(8,128)(2,1)S(1)} %get-tuple-element.32), channel_id=1, source_target_pairs={{0,16},{2,18},{4,20},{6,22},{8,24},{10,26},{12,28},{14,30},{16,0},... | collective-permute-start | bytes 393224 | tf_op jit(solution)/shard_map/ppermute | solution.py:226
  6.2 0.0 collective-permute-start.12
  6.2 0.2 collective-permute-start.13
  6.4 3.8 %collective-permute-start.14 = (bf16[2,64,512]{2,1,0:T(8,128)(2,1)S(1)}, bf16[2,64,512]{2,1,0:T(8,128)(2,1)S(1)}, u32[]{:S(2)}, u32[]{:S(2)}) collective-permute-start(bf16[2,64,512]{2,1,0:T(8,128)(2,1)S(1)} %get-tuple-element.35), channel_id=1, source_target_pairs={{0,20},{2,22},{4,16},{6,18},{8,28},{10,30},{12,24},{14,26},{16,4},... | collective-permute-start | bytes 393224 | tf_op jit(solution)/shard_map/ppermute | solution.py:226
  10.1 1.4 %front.6 = (bf16[2,64,512]{2,1,0:T(8,128)(2,1)S(1)}, bf16[2,64,512]{2,1,0:T(8,128)(2,1)S(1)}, bf16[2,64,512]{2,1,0:T(8,128)(2,1)S(1)}, bf16[2,64,512]{2,1,0:T(8,128)(2,1)S(1)}) custom-call(s32[1]{0:T(128)} %bitcast.1.me_ref, s32[1,64]{1,0:T(1,128)} %bitcast.18, bf16[8192,128]{1,0:T(8,128)(2,1)} %bitcast.13), custom_call_target="tpu_custom_call" | custom-call | tf_op jit(solution)/shard_map/front/pallas_call | solution.py:211
  11.6 0.6 collective-permute-start.7
  12.2 1.4 %front.5 = (bf16[2,64,512]{2,1,0:T(8,128)(2,1)S(1)}, bf16[2,64,512]{2,1,0:T(8,128)(2,1)S(1)}, bf16[2,64,512]{2,1,0:T(8,128)(2,1)S(1)}, bf16[2,64,512]{2,1,0:T(8,128)(2,1)S(1)}) custom-call(s32[1]{0:T(128)} %bitcast.1.me_ref, s32[1,64]{1,0:T(1,128)} %bitcast.19, bf16[8192,128]{1,0:T(8,128)(2,1)} %bitcast.14), custom_call_target="tpu_custom_call" | custom-call | tf_op jit(solution)/shard_map/front/pallas_call | solution.py:211
  13.6 5.3 %collective-permute-done.11.refs_12_ = bf16[2,64,512]{2,1,0:T(8,128)(2,1)S(1)} collective-permute-done((bf16[2,64,512]{2,1,0:T(8,128)(2,1)S(1)}, bf16[2,64,512]{2,1,0:T(8,128)(2,1)S(1)}, u32[]{:S(2)}, u32[]{:S(2)}) %collective-permute-start.11) | collective-permute-done | bytes 131104 | tf_op jit(solution)/shard_map/ppermute | solution.py:226
  18.9 0.0 collective-permute-start.8
  18.9 1.1 %collective-permute-done.12.refs_13_ = bf16[2,64,512]{2,1,0:T(8,128)(2,1)S(1)} collective-permute-done((bf16[2,64,512]{2,1,0:T(8,128)(2,1)S(1)}, bf16[2,64,512]{2,1,0:T(8,128)(2,1)S(1)}, u32[]{:S(2)}, u32[]{:S(2)}) %collective-permute-start.12) | collective-permute-done | bytes 131104 | tf_op jit(solution)/shard_map/ppermute | solution.py:226
  20.1 3.2 %collective-permute-start.9 = (bf16[2,64,512]{2,1,0:T(8,128)(2,1)S(1)}, bf16[2,64,512]{2,1,0:T(8,128)(2,1)S(1)}, u32[]{:S(2)}, u32[]{:S(2)}) collective-permute-start(bf16[2,64,512]{2,1,0:T(8,128)(2,1)S(1)} %get-tuple-element.30), channel_id=1, source_target_pairs={{0,6},{2,4},{4,2},{6,0},{8,14},{10,12},{12,10},{14,8},{16,22},{18,... | collective-permute-start | bytes 393224 | tf_op jit(solution)/shard_map/ppermute | solution.py:226
  23.3 0.0 collective-permute-done.13.refs_14_
  23.3 5.3 %collective-permute-start.10 = (bf16[2,64,512]{2,1,0:T(8,128)(2,1)S(1)}, bf16[2,64,512]{2,1,0:T(8,128)(2,1)S(1)}, u32[]{:S(2)}, u32[]{:S(2)}) collective-permute-start(bf16[2,64,512]{2,1,0:T(8,128)(2,1)S(1)} %get-tuple-element.31), channel_id=1, source_target_pairs={{0,24},{2,26},{4,28},{6,30},{8,16},{10,18},{12,20},{14,22},{16,8},... | collective-permute-start | bytes 393224 | tf_op jit(solution)/shard_map/ppermute | solution.py:226
  28.6 0.2 collective-permute-done.14.refs_15_
  28.7 0.0 collective-permute-start.3
  28.7 0.0 collective-permute-done.7.refs_8_
  28.7 1.9 %collective-permute-start.4 = (bf16[2,64,512]{2,1,0:T(8,128)(2,1)S(1)}, bf16[2,64,512]{2,1,0:T(8,128)(2,1)S(1)}, u32[]{:S(2)}, u32[]{:S(2)}) collective-permute-start(bf16[2,64,512]{2,1,0:T(8,128)(2,1)S(1)} %get-tuple-element.25), channel_id=1, source_target_pairs={{0,26},{2,24},{4,30},{6,28},{8,18},{10,16},{12,22},{14,20},{16,10}... | collective-permute-start | bytes 393224 | tf_op jit(solution)/shard_map/ppermute | solution.py:226
  30.6 1.4 %front.4 = (bf16[2,64,512]{2,1,0:T(8,128)(2,1)S(1)}, bf16[2,64,512]{2,1,0:T(8,128)(2,1)S(1)}, bf16[2,64,512]{2,1,0:T(8,128)(2,1)S(1)}, bf16[2,64,512]{2,1,0:T(8,128)(2,1)S(1)}) custom-call(s32[1]{0:T(128)} %bitcast.1.me_ref, s32[1,64]{1,0:T(1,128)} %bitcast.20, bf16[8192,128]{1,0:T(8,128)(2,1)} %bitcast.15), custom_call_target="tpu_custom_call" | custom-call | tf_op jit(solution)/shard_map/front/pallas_call | solution.py:211
  32.1 0.0 collective-permute-done.8.refs_9_
  32.1 1.5 %collective-permute-start.5 = (bf16[2,64,512]{2,1,0:T(8,128)(2,1)S(1)}, bf16[2,64,512]{2,1,0:T(8,128)(2,1)S(1)}, u32[]{:S(2)}, u32[]{:S(2)}) collective-permute-start(bf16[2,64,512]{2,1,0:T(8,128)(2,1)S(1)} %get-tuple-element.26), channel_id=1, source_target_pairs={{0,10},{2,8},{4,14},{6,12},{8,2},{10,0},{12,6},{14,4},{16,26},{18,... | collective-permute-start | bytes 393224 | tf_op jit(solution)/shard_map/ppermute | solution.py:226
  33.6 0.0 collective-permute-done.9.refs_10_
  33.6 3.0 %collective-permute-start.6 = (bf16[2,64,512]{2,1,0:T(8,128)(2,1)S(1)}, bf16[2,64,512]{2,1,0:T(8,128)(2,1)S(1)}, u32[]{:S(2)}, u32[]{:S(2)}) collective-permute-start(bf16[2,64,512]{2,1,0:T(8,128)(2,1)S(1)} %get-tuple-element.27), channel_id=1, source_target_pairs={{0,28},{2,30},{4,24},{6,26},{8,20},{10,22},{12,16},{14,18},{16,12}... | collective-permute-start | bytes 393224 | tf_op jit(solution)/shard_map/ppermute | solution.py:226
  36.5 0.0 collective-permute-done.10.refs_11_
  36.5 3.9 %collective-permute-start = (bf16[2,64,512]{2,1,0:T(8,128)(2,1)S(1)}, bf16[2,64,512]{2,1,0:T(8,128)(2,1)S(1)}, u32[]{:S(2)}, u32[]{:S(2)}) collective-permute-start(bf16[2,64,512]{2,1,0:T(8,128)(2,1)S(1)} %get-tuple-element.20), channel_id=1, source_target_pairs={{0,12},{2,14},{4,8},{6,10},{8,4},{10,6},{12,0},{14,2},{16,28},{18,... | collective-permute-start | bytes 393224 | tf_op jit(solution)/shard_map/ppermute | solution.py:226
  40.4 0.0 collective-permute-done.3.refs_4_
  40.4 1.5 %collective-permute-start.1 = (bf16[2,64,512]{2,1,0:T(8,128)(2,1)S(1)}, bf16[2,64,512]{2,1,0:T(8,128)(2,1)S(1)}, u32[]{:S(2)}, u32[]{:S(2)}) collective-permute-start(bf16[2,64,512]{2,1,0:T(8,128)(2,1)S(1)} %get-tuple-element.21), channel_id=1, source_target_pairs={{0,30},{2,28},{4,26},{6,24},{8,22},{10,20},{12,18},{14,16},{16,14}... | collective-permute-start | bytes 393224 | tf_op jit(solution)/shard_map/ppermute | solution.py:226
  41.9 0.0 collective-permute-done.4.refs_5_
  41.9 3.9 %collective-permute-start.2 = (bf16[2,64,512]{2,1,0:T(8,128)(2,1)S(1)}, bf16[2,64,512]{2,1,0:T(8,128)(2,1)S(1)}, u32[]{:S(2)}, u32[]{:S(2)}) collective-permute-start(bf16[2,64,512]{2,1,0:T(8,128)(2,1)S(1)} %get-tuple-element.22), channel_id=1, source_target_pairs={{0,14},{2,12},{4,10},{6,8},{8,6},{10,4},{12,2},{14,0},{16,30},{18,... | collective-permute-start | bytes 393224 | tf_op jit(solution)/shard_map/ppermute | solution.py:226
  45.8 0.0 collective-permute-done.5.refs_6_
  45.8 0.0 collective-permute-done.6.refs_7_
  45.8 4.4 %collective-permute-done.refs_0_ = bf16[2,64,512]{2,1,0:T(8,128)(2,1)S(1)} collective-permute-done((bf16[2,64,512]{2,1,0:T(8,128)(2,1)S(1)}, bf16[2,64,512]{2,1,0:T(8,128)(2,1)S(1)}, u32[]{:S(2)}, u32[]{:S(2)}) %collective-permute-start) | collective-permute-done | bytes 131104 | tf_op jit(solution)/shard_map/ppermute | solution.py:226
  50.2 0.1 collective-permute-done.1.refs_1_
  50.2 2.6 %collective-permute-done.2.refs_2_ = bf16[2,64,512]{2,1,0:T(8,128)(2,1)S(1)} collective-permute-done((bf16[2,64,512]{2,1,0:T(8,128)(2,1)S(1)}, bf16[2,64,512]{2,1,0:T(8,128)(2,1)S(1)}, u32[]{:S(2)}, u32[]{:S(2)}) %collective-permute-start.2) | collective-permute-done | bytes 131104 | tf_op jit(solution)/shard_map/ppermute | solution.py:226
  52.8 0.0 copy-start
  52.8 0.2 join.1.v_ref
  53.0 0.5 copy-done
  53.5 1.3 %sent.1 = f32[4,2,128,128]{3,2,1,0:T(8,128)S(1)} custom-call(s32[64]{0:T(128)S(1)} %copy-done, s32[1]{0:T(128)} %bitcast.me_ref, bf16[2,1024,512]{2,1,0:T(8,128)(2,1)S(1)} %join.1.v_ref), custom_call_target="tpu_custom_call" | custom-call | tf_op jit(solution)/shard_map/sent/pallas_call | solution.py:299
  54.8 1.6 %collective-permute-start.15 = (f32[4,2,128,128]{3,2,1,0:T(8,128)S(1)}, f32[4,2,128,128]{3,2,1,0:T(8,128)S(1)}, u32[]{:S(2)}, u32[]{:S(2)}) collective-permute-start(f32[4,2,128,128]{3,2,1,0:T(8,128)S(1)} %sent.1), channel_id=1, source_target_pairs={{0,1},{1,0},{2,3},{3,2},{4,5},{5,4},{6,7},{7,6},{8,9},{9,8},{10,11... | collective-permute-start | bytes 1572872 | tf_op jit(solution)/shard_map/ppermute | solution.py:297
  56.4 8.3 %calibrate.1 = (f32[1,1024]{1,0:T(1,128)}, f32[8,128]{1,0:T(8,128)S(1)}) custom-call(bf16[2,1024,512]{2,1,0:T(8,128)(2,1)S(1)} %join.1.v_ref, f32[8,1024]{1,0:T(8,128)} %constant.10.clone.basis_ref), custom_call_target="tpu_custom_call" | custom-call | tf_op jit(solution)/shard_map/calibrate/pallas_call | solution.py:309
  64.7 0.5 collective-permute-start.16
  65.2 2.0 %own.1.refs_2_ = bf16[2,4,2,128,128]{4,3,2,1,0:T(8,128)(2,1)} custom-call(s32[64]{0:T(128)S(1)} %copy-done, s32[1]{0:T(128)} %bitcast.me_ref, bf16[2,1024,512]{2,1,0:T(8,128)(2,1)S(1)} %join.1.v_ref, f32[8,128]{1,0:T(8,128)S(1)} %get-tuple-element.36.gains_ref), custom_call_target="tpu_custom_call" | custom-call | tf_op jit(solution)/shard_map/own/pallas_call | solution.py:328
  67.2 1.6 %collective-permute-done.16.refs_1_ = f32[8,128]{1,0:T(8,128)S(1)} collective-permute-done((f32[8,128]{1,0:T(8,128)S(1)}, f32[8,128]{1,0:T(8,128)S(1)}, u32[]{:S(2)}, u32[]{:S(2)}) %collective-permute-start.16) | collective-permute-done | bytes 4128 | tf_op jit(solution)/shard_map/ppermute | solution.py:297
  68.8 0.0 collective-permute-done.15.refs_0_
  68.8 1.4 %others.1 = bf16[2,4,2,128,128]{4,3,2,1,0:T(8,128)(2,1)} custom-call(s32[64]{0:T(128)S(1)} %copy-done, s32[1]{0:T(128)} %bitcast.me_ref, f32[4,2,128,128]{3,2,1,0:T(8,128)S(1)} %collective-permute-done.15.refs_0_, f32[8,128]{1,0:T(8,128)S(1)} %collective-permute-done.16.refs_1_, bf16[2,4,2,128,128]{4,3,2,1,0:T(8,128)(2,1)} %own.1.refs_2_), custom_call_target="tpu_custom_call", output_to_operand_aliasing={{}: (4, {})} | custom-call | tf_op jit(solution)/shard_map/others/pallas_call | solution.py:337
Async XLA Ops:
  2.1 16.9 %collective-permute-start.11 = (bf16[2,64,512]{2,1,0:T(8,128)(2,1)S(1)}, bf16[2,64,512]{2,1,0:T(8,128)(2,1)S(1)}, u32[]{:S(2)}, u32[]{:S(2)}) collective-permute-start(bf16[2,64,512]{2,1,0:T(8,128)(2,1)S(1)} %get-tuple-element.32), channel_id=1, source_target_pairs={{0,16},{2,18},{4,20},{6,22},{8,24},{10,26},{12,28},{14,30},{16,0},... | collective-permute-start | bytes 393224 | tf_op jit(solution)/shard_map/ppermute | solution.py:226
  6.2 13.9 %collective-permute-start.12 = (bf16[2,64,512]{2,1,0:T(8,128)(2,1)S(1)}, bf16[2,64,512]{2,1,0:T(8,128)(2,1)S(1)}, u32[]{:S(2)}, u32[]{:S(2)}) collective-permute-start(bf16[2,64,512]{2,1,0:T(8,128)(2,1)S(1)} %get-tuple-element.33), channel_id=1, source_target_pairs={{0,18},{2,16},{4,22},{6,20},{8,26},{10,24},{12,30},{14,28},{16,2},... | collective-permute-start | bytes 393224 | tf_op jit(solution)/shard_map/ppermute | solution.py:226
  6.2 17.1 %collective-permute-start.13 = (bf16[2,64,512]{2,1,0:T(8,128)(2,1)S(1)}, bf16[2,64,512]{2,1,0:T(8,128)(2,1)S(1)}, u32[]{:S(2)}, u32[]{:S(2)}) collective-permute-start(bf16[2,64,512]{2,1,0:T(8,128)(2,1)S(1)} %get-tuple-element.34), channel_id=1, source_target_pairs={{0,2},{2,0},{4,6},{6,4},{8,10},{10,8},{12,14},{14,12},{16,18},{18,... | collective-permute-start | bytes 393224 | tf_op jit(solution)/shard_map/ppermute | solution.py:226
  6.4 22.4 %collective-permute-start.14 = (bf16[2,64,512]{2,1,0:T(8,128)(2,1)S(1)}, bf16[2,64,512]{2,1,0:T(8,128)(2,1)S(1)}, u32[]{:S(2)}, u32[]{:S(2)}) collective-permute-start(bf16[2,64,512]{2,1,0:T(8,128)(2,1)S(1)} %get-tuple-element.35), channel_id=1, source_target_pairs={{0,20},{2,22},{4,16},{6,18},{8,28},{10,30},{12,24},{14,26},{16,4},... | collective-permute-start | bytes 393224 | tf_op jit(solution)/shard_map/ppermute | solution.py:226
  11.6 17.1 %collective-permute-start.7 = (bf16[2,64,512]{2,1,0:T(8,128)(2,1)S(1)}, bf16[2,64,512]{2,1,0:T(8,128)(2,1)S(1)}, u32[]{:S(2)}, u32[]{:S(2)}) collective-permute-start(bf16[2,64,512]{2,1,0:T(8,128)(2,1)S(1)} %get-tuple-element.28), channel_id=1, source_target_pairs={{0,4},{2,6},{4,0},{6,2},{8,12},{10,14},{12,8},{14,10},{16,20},{18,... | collective-permute-start | bytes 393224 | tf_op jit(solution)/shard_map/ppermute | solution.py:226
  18.9 13.1 %collective-permute-start.8 = (bf16[2,64,512]{2,1,0:T(8,128)(2,1)S(1)}, bf16[2,64,512]{2,1,0:T(8,128)(2,1)S(1)}, u32[]{:S(2)}, u32[]{:S(2)}) collective-permute-start(bf16[2,64,512]{2,1,0:T(8,128)(2,1)S(1)} %get-tuple-element.29), channel_id=1, source_target_pairs={{0,22},{2,20},{4,18},{6,16},{8,30},{10,28},{12,26},{14,24},{16,6},... | collective-permute-start | bytes 393224 | tf_op jit(solution)/shard_map/ppermute | solution.py:226
  20.1 13.5 %collective-permute-start.9 = (bf16[2,64,512]{2,1,0:T(8,128)(2,1)S(1)}, bf16[2,64,512]{2,1,0:T(8,128)(2,1)S(1)}, u32[]{:S(2)}, u32[]{:S(2)}) collective-permute-start(bf16[2,64,512]{2,1,0:T(8,128)(2,1)S(1)} %get-tuple-element.30), channel_id=1, source_target_pairs={{0,6},{2,4},{4,2},{6,0},{8,14},{10,12},{12,10},{14,8},{16,22},{18,... | collective-permute-start | bytes 393224 | tf_op jit(solution)/shard_map/ppermute | solution.py:226
  23.3 13.2 %collective-permute-start.10 = (bf16[2,64,512]{2,1,0:T(8,128)(2,1)S(1)}, bf16[2,64,512]{2,1,0:T(8,128)(2,1)S(1)}, u32[]{:S(2)}, u32[]{:S(2)}) collective-permute-start(bf16[2,64,512]{2,1,0:T(8,128)(2,1)S(1)} %get-tuple-element.31), channel_id=1, source_target_pairs={{0,24},{2,26},{4,28},{6,30},{8,16},{10,18},{12,20},{14,22},{16,8},... | collective-permute-start | bytes 393224 | tf_op jit(solution)/shard_map/ppermute | solution.py:226
  28.7 11.7 %collective-permute-start.3 = (bf16[2,64,512]{2,1,0:T(8,128)(2,1)S(1)}, bf16[2,64,512]{2,1,0:T(8,128)(2,1)S(1)}, u32[]{:S(2)}, u32[]{:S(2)}) collective-permute-start(bf16[2,64,512]{2,1,0:T(8,128)(2,1)S(1)} %get-tuple-element.24), channel_id=1, source_target_pairs={{0,8},{2,10},{4,12},{6,14},{8,0},{10,2},{12,4},{14,6},{16,24},{18,... | collective-permute-start | bytes 393224 | tf_op jit(solution)/shard_map/ppermute | solution.py:226
  28.7 13.2 %collective-permute-start.4 = (bf16[2,64,512]{2,1,0:T(8,128)(2,1)S(1)}, bf16[2,64,512]{2,1,0:T(8,128)(2,1)S(1)}, u32[]{:S(2)}, u32[]{:S(2)}) collective-permute-start(bf16[2,64,512]{2,1,0:T(8,128)(2,1)S(1)} %get-tuple-element.25), channel_id=1, source_target_pairs={{0,26},{2,24},{4,30},{6,28},{8,18},{10,16},{12,22},{14,20},{16,10}... | collective-permute-start | bytes 393224 | tf_op jit(solution)/shard_map/ppermute | solution.py:226
  32.1 13.7 %collective-permute-start.5 = (bf16[2,64,512]{2,1,0:T(8,128)(2,1)S(1)}, bf16[2,64,512]{2,1,0:T(8,128)(2,1)S(1)}, u32[]{:S(2)}, u32[]{:S(2)}) collective-permute-start(bf16[2,64,512]{2,1,0:T(8,128)(2,1)S(1)} %get-tuple-element.26), channel_id=1, source_target_pairs={{0,10},{2,8},{4,14},{6,12},{8,2},{10,0},{12,6},{14,4},{16,26},{18,... | collective-permute-start | bytes 393224 | tf_op jit(solution)/shard_map/ppermute | solution.py:226
  33.6 12.2 %collective-permute-start.6 = (bf16[2,64,512]{2,1,0:T(8,128)(2,1)S(1)}, bf16[2,64,512]{2,1,0:T(8,128)(2,1)S(1)}, u32[]{:S(2)}, u32[]{:S(2)}) collective-permute-start(bf16[2,64,512]{2,1,0:T(8,128)(2,1)S(1)} %get-tuple-element.27), channel_id=1, source_target_pairs={{0,28},{2,30},{4,24},{6,26},{8,20},{10,22},{12,16},{14,18},{16,12}... | collective-permute-start | bytes 393224 | tf_op jit(solution)/shard_map/ppermute | solution.py:226
  36.5 13.6 %collective-permute-start = (bf16[2,64,512]{2,1,0:T(8,128)(2,1)S(1)}, bf16[2,64,512]{2,1,0:T(8,128)(2,1)S(1)}, u32[]{:S(2)}, u32[]{:S(2)}) collective-permute-start(bf16[2,64,512]{2,1,0:T(8,128)(2,1)S(1)} %get-tuple-element.20), channel_id=1, source_target_pairs={{0,12},{2,14},{4,8},{6,10},{8,4},{10,6},{12,0},{14,2},{16,28},{18,... | collective-permute-start | bytes 393224 | tf_op jit(solution)/shard_map/ppermute | solution.py:226
  40.4 9.8 %collective-permute-start.1 = (bf16[2,64,512]{2,1,0:T(8,128)(2,1)S(1)}, bf16[2,64,512]{2,1,0:T(8,128)(2,1)S(1)}, u32[]{:S(2)}, u32[]{:S(2)}) collective-permute-start(bf16[2,64,512]{2,1,0:T(8,128)(2,1)S(1)} %get-tuple-element.21), channel_id=1, source_target_pairs={{0,30},{2,28},{4,26},{6,24},{8,22},{10,20},{12,18},{14,16},{16,14}... | collective-permute-start | bytes 393224 | tf_op jit(solution)/shard_map/ppermute | solution.py:226
  41.9 10.9 %collective-permute-start.2 = (bf16[2,64,512]{2,1,0:T(8,128)(2,1)S(1)}, bf16[2,64,512]{2,1,0:T(8,128)(2,1)S(1)}, u32[]{:S(2)}, u32[]{:S(2)}) collective-permute-start(bf16[2,64,512]{2,1,0:T(8,128)(2,1)S(1)} %get-tuple-element.22), channel_id=1, source_target_pairs={{0,14},{2,12},{4,10},{6,8},{8,6},{10,4},{12,2},{14,0},{16,30},{18,... | collective-permute-start | bytes 393224 | tf_op jit(solution)/shard_map/ppermute | solution.py:226
  52.8 0.7 copy-start
  54.8 14.0 %collective-permute-start.15 = (f32[4,2,128,128]{3,2,1,0:T(8,128)S(1)}, f32[4,2,128,128]{3,2,1,0:T(8,128)S(1)}, u32[]{:S(2)}, u32[]{:S(2)}) collective-permute-start(f32[4,2,128,128]{3,2,1,0:T(8,128)S(1)} %sent.1), channel_id=1, source_target_pairs={{0,1},{1,0},{2,3},{3,2},{4,5},{5,4},{6,7},{7,6},{8,9},{9,8},{10,11... | collective-permute-start | bytes 1572872 | tf_op jit(solution)/shard_map/ppermute | solution.py:297
  64.7 4.1 %collective-permute-start.16 = (f32[8,128]{1,0:T(8,128)S(1)}, f32[8,128]{1,0:T(8,128)S(1)}, u32[]{:S(2)}, u32[]{:S(2)}) collective-permute-start(f32[8,128]{1,0:T(8,128)S(1)} %get-tuple-element.36.gains_ref), channel_id=1, source_target_pairs={{0,1},{1,0},{2,3},{3,2},{4,5},{5,4},{6,7},{7,6},{8,9},{9,8},{10,11... | collective-permute-start | bytes 12296 | tf_op jit(solution)/shard_map/ppermute | solution.py:297

commit v6 on v5

--- a/solution.py
+++ b/solution.py
@@ -16,6 +16,7 @@
 EPS = 1e-06
 LANES = 128
 GROUP = 4
+FIRST = 2
 SPLITS = 2
 
 VMEM = pl.BlockSpec(memory_space=pltpu.VMEM)
@@ -83,10 +84,8 @@
     return w * scales, p * scales
 
 
-def calibrate_kernel(v_ref, basis_ref, gains_ref, blocks_ref, vt_ref, first, sem):
+def calibrate_kernel(v_ref, first, gains_ref, blocks_ref, vt_ref):
     _, count, frames = v_ref.shape
-    copy = pltpu.make_async_copy(basis_ref, first, sem)
-    copy.start()
     rows = lax.broadcasted_iota(jnp.int32, (2 * RANK, 1), 0)
     sign = jnp.where(rows < RANK, 1.0, -1.0)
     order = jnp.where(rows < RANK, rows, rows - RANK)
@@ -105,7 +104,6 @@
     def step(_, z):
         return expand(gram_schmidt(z, project(z), sign, order)[1])
 
-    copy.wait()
     z = lax.fori_loop(0, ITERS - 1, step, expand(project(first[...])))
     q, y = gram_schmidt(z, project(z), sign, order)
     turned = sign * swap(y)
@@ -196,18 +194,17 @@
     cols = frames // LANES
     chunk = size * cols * both
     rows = volt.reshape(parts, size, both, cols, LANES).transpose(0, 1, 3, 2, 4).reshape(parts * chunk, LANES)
-    near = list(range(1, parts // 2))
     far = list(range(parts // 2, parts))
-    order = [far[0]]
-    for k in range(len(near)):
-        order += [far[k + 1], near[k]]
+    near = sorted(range(1, parts // 2), key=lambda d: (-d.bit_length(), d))
+    order = far[:1]
+    for d, other in zip(near, far[1:]):
+        order += [other, d]
     order.append(0)
     shape = (both, size, frames)
     blocks = []
-    groups = [order[at : at + GROUP] for at in range(0, parts, GROUP)]
-    order = sum(reversed(groups), [])
-    for at in range(0, parts, GROUP):
-        targets = order[at : at + GROUP]
+    cuts = [0, *range(FIRST, GROUP, FIRST), *range(GROUP, parts, GROUP), parts]
+    groups = [order[start:stop] for start, stop in zip(cuts, cuts[1:])][::-1]
+    for targets in groups:
         fronts = pl.pallas_call(
             functools.partial(front_kernel, targets, min(size, 16)),
             out_shape=[small(parts)(shape, volt.dtype)] * len(targets),
@@ -225,7 +222,7 @@
             pairs = [(j, j ^ d) for j in range(parts)]
             blocks.append(lax.ppermute(block, "inp", pairs) if d else block)
     return pl.pallas_call(
-        functools.partial(join_kernel, order),
+        functools.partial(join_kernel, sum(groups, [])),
         out_shape=pltpu.VMEM((both, parts * size, frames), volt.dtype),
         in_specs=[SMEM] + [VMEM] * parts,
         out_specs=VMEM,
@@ -270,13 +267,13 @@
     me = me_ref[0]
     copies = []
     for d in range(1, owners):
+        source = lax.rem(me + owners - d, owners)
         for s in range(KPO):
             scale = outer(gain_refs[d - 1], table_ref[me * slots + s])
             for part in range(2):
                 held[d - 1, s, part] = (scale * tile_refs[d - 1][s, part]).astype(jnp.bfloat16)
-        source = lax.rem(me + owners - d, owners)
-        copies.append(pltpu.make_async_copy(held.at[d - 1], vis_ref.at[source], sem.at[d - 1]))
-        copies[-1].start()
+            copies.append(pltpu.make_async_copy(held.at[d - 1, s], vis_ref.at[source, s], sem.at[d - 1, s]))
+            copies[-1].start()
     for copy in copies:
         copy.wait()
 
@@ -291,6 +288,7 @@
     flat = in_vmem(corner_turn(volt, mask))
     _, count, frames = flat.shape
     me = lax.axis_index("chan").reshape(1)
+    table = in_hbm(table)
     blocks = count // TB
 
     def shift(x, d):
@@ -312,16 +310,12 @@
             jax.ShapeDtypeStruct((1, count), jnp.float32),
             pltpu.VMEM((blocks, TB), jnp.float32),
         ],
-        in_specs=[VMEM, HBM],
+        in_specs=[VMEM, VMEM],
         out_specs=[VMEM] * 2,
-        scratch_shapes=[
-            pltpu.VMEM((2, frames, count), jnp.bfloat16),
-            pltpu.VMEM((2 * RANK, count), jnp.float32),
-            pltpu.SemaphoreType.DMA,
-        ],
+        scratch_shapes=[pltpu.VMEM((2, frames, count), jnp.bfloat16)],
         compiler_params=pltpu.CompilerParams(vmem_limit_bytes=12 << 20),
         name="calibrate",
-    )(flat, in_hbm(jnp.asarray(first_basis(count))))
+    )(flat, in_vmem(jnp.asarray(first_basis(count))))
     other_gains = [in_vmem(shift(by_block, d), owners) for d in range(1, owners)]
 
     vis_shape = jax.ShapeDtypeStruct((owners, KPO, 2, TB, TB), jnp.bfloat16)
@@ -341,7 +335,7 @@
         out_specs=ANY,
         scratch_shapes=[
             pltpu.VMEM((owners - 1, KPO, 2, TB, TB), jnp.bfloat16),
-            pltpu.SemaphoreType.DMA((owners - 1,)),
+            pltpu.SemaphoreType.DMA((owners - 1, KPO)),
         ],
         input_output_aliases={2 * owners: 0},
         compiler_params=pltpu.CompilerParams(vmem_limit_bytes=12 << 20),

time: 70.6 us -> 68.8 us (0.975)
  starting transfers between devices: 34.9 us -> 29.3 us
  waiting for transfers between devices: 15.3 us -> 18.9 us
    ppermute x15, starting transfers between devices: 32.7 us -> 27.2 us  [corner_turn(): blocks.append(lax.ppermute(block, 'inp', pairs) if d else block)]
    ppermute x15, waiting for transfers between devices: 13.7 us -> 15.8 us  [corner_turn(): blocks.append(lax.ppermute(block, 'inp', pairs) if d else block)]
    ppermute x2, waiting for transfers between devices: 1.6 us -> 3.14 us  [shift(): lax.ppermute(x, 'chan', [(j, (j + d) % owners) for j in range(owners)])]
    pallas_call x4 -> x5, Pallas kernels: 5.74 us -> 6.74 us  [corner_turn(): pl.pallas_call(functools.partial(front_kernel, targets, min(size, 16)), o...]
    pallas_call x1, Pallas kernels: 8.29 us -> 7.5 us  [body(): pl.pallas_call(calibrate_kernel, out_shape=[jax.ShapeDtypeStruct((1, coun...]
  transfers between devices with their start and end apart: 17 -> 17, of which waited for: 7 -> 8; matrix products, arithmetic and copies ran while one was open for 0% -> 0% of each run, Pallas kernels for 21% -> 22%
where the time goes in v6:
time: 68.8 us; the launch traced here: 68.5 us
  starting transfers between devices  29.3 us (43%)
  Pallas kernels  19.5 us (28%)
  waiting for transfers between devices  18.9 us (27%)
  between operations  0.73 us (1%)
    ppermute x15, starting transfers between devices, corner_turn(): blocks.append(lax.ppermute(block, 'inp', pairs) if d else block)  27.2 us
    ppermute x15, waiting for transfers between devices, corner_turn(): blocks.append(lax.ppermute(block, 'inp', pairs) if d else block)  15.8 us
    pallas_call x1, Pallas kernels, body(): pl.pallas_call(calibrate_kernel, out_shape=[jax.ShapeDtypeStruct((1, coun...  7.5 us
    pallas_call x5, Pallas kernels, corner_turn(): pl.pallas_call(functools.partial(front_kernel, targets, min(size, 16)), o...  6.74 us
    ppermute x2, waiting for transfers between devices, shift(): lax.ppermute(x, 'chan', [(j, (j + d) % owners) for j in range(owners)])  3.14 us
    ppermute x2, starting transfers between devices, shift(): lax.ppermute(x, 'chan', [(j, (j + d) % owners) for j in range(owners)])  2.09 us
    pallas_call x1, Pallas kernels, body(): pl.pallas_call(functools.partial(own_kernel, slots), out_shape=vis_shape,...  2.09 us
    pallas_call x1, Pallas kernels, body(): pl.pallas_call(functools.partial(sent_kernel, owners, slots), out_shape=[...  1.51 us
  transfers between devices with their start and end apart: 17, of which 8 were waited for; matrix products, arithmetic and copies ran while one was open for 0% of the time, Pallas kernels for 22%

profile of v6, /device:TPU:0, one launch (start us, length us, event | category | flops | bytes accessed | tf_op | source)
XLA Modules:
  0.0 68.5 jit_solution(1637634049796347868)
XLA Ops:
  0.6 1.2 %front.9 = (bf16[2,64,512]{2,1,0:T(8,128)(2,1)S(1)}, bf16[2,64,512]{2,1,0:T(8,128)(2,1)S(1)}) custom-call(s32[1]{0:T(128)} %bitcast.1.me_ref, s32[1,64]{1,0:T(1,128)} %bitcast.18, bf16[8192,128]{1,0:T(8,128)(2,1)} %bitcast.12), custom_call_target="tpu_custom_call" | custom-call | tf_op jit(solution)/shard_map/front/pallas_call | solution.py:208
  1.9 4.1 %collective-permute-start.13 = (bf16[2,64,512]{2,1,0:T(8,128)(2,1)S(1)}, bf16[2,64,512]{2,1,0:T(8,128)(2,1)S(1)}, u32[]{:S(2)}, u32[]{:S(2)}) collective-permute-start(bf16[2,64,512]{2,1,0:T(8,128)(2,1)S(1)} %get-tuple-element.34), channel_id=1, source_target_pairs={{0,16},{2,18},{4,20},{6,22},{8,24},{10,26},{12,28},{14,30},{16,0},... | collective-permute-start | bytes 393224 | tf_op jit(solution)/shard_map/ppermute | solution.py:223
  6.0 0.0 collective-permute-start.14
  6.0 1.2 %front.8 = (bf16[2,64,512]{2,1,0:T(8,128)(2,1)S(1)}, bf16[2,64,512]{2,1,0:T(8,128)(2,1)S(1)}) custom-call(s32[1]{0:T(128)} %bitcast.1.me_ref, s32[1,64]{1,0:T(1,128)} %bitcast.19, bf16[8192,128]{1,0:T(8,128)(2,1)} %bitcast.13), custom_call_target="tpu_custom_call" | custom-call | tf_op jit(solution)/shard_map/front/pallas_call | solution.py:208
  7.2 1.6 %collective-permute-start.11 = (bf16[2,64,512]{2,1,0:T(8,128)(2,1)S(1)}, bf16[2,64,512]{2,1,0:T(8,128)(2,1)S(1)}, u32[]{:S(2)}, u32[]{:S(2)}) collective-permute-start(bf16[2,64,512]{2,1,0:T(8,128)(2,1)S(1)} %get-tuple-element.32), channel_id=1, source_target_pairs={{0,8},{2,10},{4,12},{6,14},{8,0},{10,2},{12,4},{14,6},{16,24},{18,... | collective-permute-start | bytes 393224 | tf_op jit(solution)/shard_map/ppermute | solution.py:223
  8.8 3.0 %collective-permute-start.12 = (bf16[2,64,512]{2,1,0:T(8,128)(2,1)S(1)}, bf16[2,64,512]{2,1,0:T(8,128)(2,1)S(1)}, u32[]{:S(2)}, u32[]{:S(2)}) collective-permute-start(bf16[2,64,512]{2,1,0:T(8,128)(2,1)S(1)} %get-tuple-element.33), channel_id=1, source_target_pairs={{0,20},{2,22},{4,16},{6,18},{8,28},{10,30},{12,24},{14,26},{16,4},... | collective-permute-start | bytes 393224 | tf_op jit(solution)/shard_map/ppermute | solution.py:223
  11.8 1.4 %front.7 = (bf16[2,64,512]{2,1,0:T(8,128)(2,1)S(1)}, bf16[2,64,512]{2,1,0:T(8,128)(2,1)S(1)}, bf16[2,64,512]{2,1,0:T(8,128)(2,1)S(1)}, bf16[2,64,512]{2,1,0:T(8,128)(2,1)S(1)}) custom-call(s32[1]{0:T(128)} %bitcast.1.me_ref, s32[1,64]{1,0:T(1,128)} %bitcast.20, bf16[8192,128]{1,0:T(8,128)(2,1)} %bitcast.14), custom_call_target="tpu_custom_call" | custom-call | tf_op jit(solution)/shard_map/front/pallas_call | solution.py:208
  13.3 0.5 collective-permute-start.7
  13.8 1.4 %front.6 = (bf16[2,64,512]{2,1,0:T(8,128)(2,1)S(1)}, bf16[2,64,512]{2,1,0:T(8,128)(2,1)S(1)}, bf16[2,64,512]{2,1,0:T(8,128)(2,1)S(1)}, bf16[2,64,512]{2,1,0:T(8,128)(2,1)S(1)}) custom-call(s32[1]{0:T(128)} %bitcast.1.me_ref, s32[1,64]{1,0:T(1,128)} %bitcast.21, bf16[8192,128]{1,0:T(8,128)(2,1)} %bitcast.15), custom_call_target="tpu_custom_call" | custom-call | tf_op jit(solution)/shard_map/front/pallas_call | solution.py:208
  15.3 0.6 collective-permute-done.13.refs_14_
  15.9 0.0 collective-permute-start.8
  15.9 4.1 %collective-permute-done.14.refs_15_ = bf16[2,64,512]{2,1,0:T(8,128)(2,1)S(1)} collective-permute-done((bf16[2,64,512]{2,1,0:T(8,128)(2,1)S(1)}, bf16[2,64,512]{2,1,0:T(8,128)(2,1)S(1)}, u32[]{:S(2)}, u32[]{:S(2)}) %collective-permute-start.14) | collective-permute-done | bytes 131104 | tf_op jit(solution)/shard_map/ppermute | solution.py:223
  20.0 3.3 %collective-permute-start.9 = (bf16[2,64,512]{2,1,0:T(8,128)(2,1)S(1)}, bf16[2,64,512]{2,1,0:T(8,128)(2,1)S(1)}, u32[]{:S(2)}, u32[]{:S(2)}) collective-permute-start(bf16[2,64,512]{2,1,0:T(8,128)(2,1)S(1)} %get-tuple-element.30), channel_id=1, source_target_pairs={{0,12},{2,14},{4,8},{6,10},{8,4},{10,6},{12,0},{14,2},{16,28},{18,... | collective-permute-start | bytes 393224 | tf_op jit(solution)/shard_map/ppermute | solution.py:223
  23.3 0.0 collective-permute-done.11.refs_12_
  23.3 1.8 %collective-permute-start.10 = (bf16[2,64,512]{2,1,0:T(8,128)(2,1)S(1)}, bf16[2,64,512]{2,1,0:T(8,128)(2,1)S(1)}, u32[]{:S(2)}, u32[]{:S(2)}) collective-permute-start(bf16[2,64,512]{2,1,0:T(8,128)(2,1)S(1)} %get-tuple-element.31), channel_id=1, source_target_pairs={{0,24},{2,26},{4,28},{6,30},{8,16},{10,18},{12,20},{14,22},{16,8},... | collective-permute-start | bytes 393224 | tf_op jit(solution)/shard_map/ppermute | solution.py:223
  25.1 3.4 %collective-permute-done.12.refs_13_ = bf16[2,64,512]{2,1,0:T(8,128)(2,1)S(1)} collective-permute-done((bf16[2,64,512]{2,1,0:T(8,128)(2,1)S(1)}, bf16[2,64,512]{2,1,0:T(8,128)(2,1)S(1)}, u32[]{:S(2)}, u32[]{:S(2)}) %collective-permute-start.12) | collective-permute-done | bytes 131104 | tf_op jit(solution)/shard_map/ppermute | solution.py:223
  28.5 0.0 collective-permute-start.3
  28.5 0.0 collective-permute-done.7.refs_8_
  28.5 1.9 %collective-permute-start.4 = (bf16[2,64,512]{2,1,0:T(8,128)(2,1)S(1)}, bf16[2,64,512]{2,1,0:T(8,128)(2,1)S(1)}, u32[]{:S(2)}, u32[]{:S(2)}) collective-permute-start(bf16[2,64,512]{2,1,0:T(8,128)(2,1)S(1)} %get-tuple-element.25), channel_id=1, source_target_pairs={{0,26},{2,24},{4,30},{6,28},{8,18},{10,16},{12,22},{14,20},{16,10}... | collective-permute-start | bytes 393224 | tf_op jit(solution)/shard_map/ppermute | solution.py:223
  30.4 1.4 %front.5 = (bf16[2,64,512]{2,1,0:T(8,128)(2,1)S(1)}, bf16[2,64,512]{2,1,0:T(8,128)(2,1)S(1)}, bf16[2,64,512]{2,1,0:T(8,128)(2,1)S(1)}, bf16[2,64,512]{2,1,0:T(8,128)(2,1)S(1)}) custom-call(s32[1]{0:T(128)} %bitcast.1.me_ref, s32[1,64]{1,0:T(1,128)} %bitcast.22, bf16[8192,128]{1,0:T(8,128)(2,1)} %bitcast.16), custom_call_target="tpu_custom_call" | custom-call | tf_op jit(solution)/shard_map/front/pallas_call | solution.py:208
  31.9 0.0 collective-permute-done.8.refs_9_
  31.9 0.6 collective-permute-start.5
  32.5 2.3 %collective-permute-done.9.refs_10_ = bf16[2,64,512]{2,1,0:T(8,128)(2,1)S(1)} collective-permute-done((bf16[2,64,512]{2,1,0:T(8,128)(2,1)S(1)}, bf16[2,64,512]{2,1,0:T(8,128)(2,1)S(1)}, u32[]{:S(2)}, u32[]{:S(2)}) %collective-permute-start.9) | collective-permute-done | bytes 131104 | tf_op jit(solution)/shard_map/ppermute | solution.py:223
  34.8 7.4 %collective-permute-start.6 = (bf16[2,64,512]{2,1,0:T(8,128)(2,1)S(1)}, bf16[2,64,512]{2,1,0:T(8,128)(2,1)S(1)}, u32[]{:S(2)}, u32[]{:S(2)}) collective-permute-start(bf16[2,64,512]{2,1,0:T(8,128)(2,1)S(1)} %get-tuple-element.27), channel_id=1, source_target_pairs={{0,28},{2,30},{4,24},{6,26},{8,20},{10,22},{12,16},{14,18},{16,12}... | collective-permute-start | bytes 393224 | tf_op jit(solution)/shard_map/ppermute | solution.py:223
  42.1 0.0 collective-permute-done.10.refs_11_
  42.1 0.8 %collective-permute-start = (bf16[2,64,512]{2,1,0:T(8,128)(2,1)S(1)}, bf16[2,64,512]{2,1,0:T(8,128)(2,1)S(1)}, u32[]{:S(2)}, u32[]{:S(2)}) collective-permute-start(bf16[2,64,512]{2,1,0:T(8,128)(2,1)S(1)} %get-tuple-element.20), channel_id=1, source_target_pairs={{0,6},{2,4},{4,2},{6,0},{8,14},{10,12},{12,10},{14,8},{16,22},{18,... | collective-permute-start | bytes 393224 | tf_op jit(solution)/shard_map/ppermute | solution.py:223
  42.9 0.0 collective-permute-done.3.refs_4_
  42.9 1.6 %collective-permute-start.1 = (bf16[2,64,512]{2,1,0:T(8,128)(2,1)S(1)}, bf16[2,64,512]{2,1,0:T(8,128)(2,1)S(1)}, u32[]{:S(2)}, u32[]{:S(2)}) collective-permute-start(bf16[2,64,512]{2,1,0:T(8,128)(2,1)S(1)} %get-tuple-element.21), channel_id=1, source_target_pairs={{0,30},{2,28},{4,26},{6,24},{8,22},{10,20},{12,18},{14,16},{16,14}... | collective-permute-start | bytes 393224 | tf_op jit(solution)/shard_map/ppermute | solution.py:223
  44.5 0.0 collective-permute-done.4.refs_5_
  44.5 0.5 collective-permute-start.2
  45.0 0.0 collective-permute-done.5.refs_6_
  45.0 1.0 %collective-permute-done.6.refs_7_ = bf16[2,64,512]{2,1,0:T(8,128)(2,1)S(1)} collective-permute-done((bf16[2,64,512]{2,1,0:T(8,128)(2,1)S(1)}, bf16[2,64,512]{2,1,0:T(8,128)(2,1)S(1)}, u32[]{:S(2)}, u32[]{:S(2)}) %collective-permute-start.6) | collective-permute-done | bytes 131104 | tf_op jit(solution)/shard_map/ppermute | solution.py:223
  45.9 4.4 %collective-permute-done.refs_0_ = bf16[2,64,512]{2,1,0:T(8,128)(2,1)S(1)} collective-permute-done((bf16[2,64,512]{2,1,0:T(8,128)(2,1)S(1)}, bf16[2,64,512]{2,1,0:T(8,128)(2,1)S(1)}, u32[]{:S(2)}, u32[]{:S(2)}) %collective-permute-start) | collective-permute-done | bytes 131104 | tf_op jit(solution)/shard_map/ppermute | solution.py:223
  50.3 0.1 collective-permute-done.1.refs_1_
  50.5 0.0 collective-permute-done.2.refs_2_
  50.5 0.2 join.1.v_ref
  50.6 0.0 copy-start
  50.6 1.5 %sent.1 = f32[4,2,128,128]{3,2,1,0:T(8,128)S(1)} custom-call(s32[64]{0:T(128)} %table_ref.5, s32[1]{0:T(128)} %bitcast.me_ref, bf16[2,1024,512]{2,1,0:T(8,128)(2,1)S(1)} %join.1.v_ref), custom_call_target="tpu_custom_call" | custom-call | tf_op jit(solution)/shard_map/sent/pallas_call | solution.py:297
  52.1 1.6 %collective-permute-start.15 = (f32[4,2,128,128]{3,2,1,0:T(8,128)S(1)}, f32[4,2,128,128]{3,2,1,0:T(8,128)S(1)}, u32[]{:S(2)}, u32[]{:S(2)}) collective-permute-start(f32[4,2,128,128]{3,2,1,0:T(8,128)S(1)} %sent.1), channel_id=1, source_target_pairs={{0,1},{1,0},{2,3},{3,2},{4,5},{5,4},{6,7},{7,6},{8,9},{9,8},{10,11... | collective-permute-start | bytes 1572872 | tf_op jit(solution)/shard_map/ppermute | solution.py:295
  53.7 0.0 copy-done
  53.7 7.5 %calibrate.1 = (f32[1,1024]{1,0:T(1,128)}, f32[8,128]{1,0:T(8,128)S(1)}) custom-call(bf16[2,1024,512]{2,1,0:T(8,128)(2,1)S(1)} %join.1.v_ref, f32[8,1024]{1,0:T(8,128)S(1)} %copy-done), custom_call_target="tpu_custom_call" | custom-call | tf_op jit(solution)/shard_map/calibrate/pallas_call | solution.py:307
  61.3 0.5 collective-permute-start.16
  61.7 2.1 %own.1.refs_2_ = bf16[2,4,2,128,128]{4,3,2,1,0:T(8,128)(2,1)} custom-call(s32[64]{0:T(128)} %table_ref.5, s32[1]{0:T(128)} %bitcast.me_ref, bf16[2,1024,512]{2,1,0:T(8,128)(2,1)S(1)} %join.1.v_ref, f32[8,128]{1,0:T(8,128)S(1)} %get-tuple-element.36.gains_ref), custom_call_target="tpu_custom_call" | custom-call | tf_op jit(solution)/shard_map/own/pallas_call | solution.py:322
  63.8 3.1 %collective-permute-done.16.refs_1_ = f32[8,128]{1,0:T(8,128)S(1)} collective-permute-done((f32[8,128]{1,0:T(8,128)S(1)}, f32[8,128]{1,0:T(8,128)S(1)}, u32[]{:S(2)}, u32[]{:S(2)}) %collective-permute-start.16) | collective-permute-done | bytes 4128 | tf_op jit(solution)/shard_map/ppermute | solution.py:295
  67.0 0.0 collective-permute-done.15.refs_0_
  67.0 1.5 %others.1 = bf16[2,4,2,128,128]{4,3,2,1,0:T(8,128)(2,1)} custom-call(s32[64]{0:T(128)} %table_ref.5, s32[1]{0:T(128)} %bitcast.me_ref, f32[4,2,128,128]{3,2,1,0:T(8,128)S(1)} %collective-permute-done.15.refs_0_, f32[8,128]{1,0:T(8,128)S(1)} %collective-permute-done.16.refs_1_, bf16[2,4,2,128,128]{4,3,2,1,0:T(8,128)(2,1)} %own.1.refs_2_), custom_call_target="tpu_custom_call", output_to_operand_aliasing={{}: (4, {})} | custom-call | tf_op jit(solution)/shard_map/others/pallas_call | solution.py:331
Async XLA Ops:
  1.9 14.0 %collective-permute-start.13 = (bf16[2,64,512]{2,1,0:T(8,128)(2,1)S(1)}, bf16[2,64,512]{2,1,0:T(8,128)(2,1)S(1)}, u32[]{:S(2)}, u32[]{:S(2)}) collective-permute-start(bf16[2,64,512]{2,1,0:T(8,128)(2,1)S(1)} %get-tuple-element.34), channel_id=1, source_target_pairs={{0,16},{2,18},{4,20},{6,22},{8,24},{10,26},{12,28},{14,30},{16,0},... | collective-permute-start | bytes 393224 | tf_op jit(solution)/shard_map/ppermute | solution.py:223
  6.0 14.0 %collective-permute-start.14 = (bf16[2,64,512]{2,1,0:T(8,128)(2,1)S(1)}, bf16[2,64,512]{2,1,0:T(8,128)(2,1)S(1)}, u32[]{:S(2)}, u32[]{:S(2)}) collective-permute-start(bf16[2,64,512]{2,1,0:T(8,128)(2,1)S(1)} %get-tuple-element.35), channel_id=1, source_target_pairs={{0,18},{2,16},{4,22},{6,20},{8,26},{10,24},{12,30},{14,28},{16,2},... | collective-permute-start | bytes 393224 | tf_op jit(solution)/shard_map/ppermute | solution.py:223
  7.2 16.1 %collective-permute-start.11 = (bf16[2,64,512]{2,1,0:T(8,128)(2,1)S(1)}, bf16[2,64,512]{2,1,0:T(8,128)(2,1)S(1)}, u32[]{:S(2)}, u32[]{:S(2)}) collective-permute-start(bf16[2,64,512]{2,1,0:T(8,128)(2,1)S(1)} %get-tuple-element.32), channel_id=1, source_target_pairs={{0,8},{2,10},{4,12},{6,14},{8,0},{10,2},{12,4},{14,6},{16,24},{18,... | collective-permute-start | bytes 393224 | tf_op jit(solution)/shard_map/ppermute | solution.py:223
  8.8 19.7 %collective-permute-start.12 = (bf16[2,64,512]{2,1,0:T(8,128)(2,1)S(1)}, bf16[2,64,512]{2,1,0:T(8,128)(2,1)S(1)}, u32[]{:S(2)}, u32[]{:S(2)}) collective-permute-start(bf16[2,64,512]{2,1,0:T(8,128)(2,1)S(1)} %get-tuple-element.33), channel_id=1, source_target_pairs={{0,20},{2,22},{4,16},{6,18},{8,28},{10,30},{12,24},{14,26},{16,4},... | collective-permute-start | bytes 393224 | tf_op jit(solution)/shard_map/ppermute | solution.py:223
  13.3 15.2 %collective-permute-start.7 = (bf16[2,64,512]{2,1,0:T(8,128)(2,1)S(1)}, bf16[2,64,512]{2,1,0:T(8,128)(2,1)S(1)}, u32[]{:S(2)}, u32[]{:S(2)}) collective-permute-start(bf16[2,64,512]{2,1,0:T(8,128)(2,1)S(1)} %get-tuple-element.28), channel_id=1, source_target_pairs={{0,10},{2,8},{4,14},{6,12},{8,2},{10,0},{12,6},{14,4},{16,26},{18,... | collective-permute-start | bytes 393224 | tf_op jit(solution)/shard_map/ppermute | solution.py:223
  15.9 16.0 %collective-permute-start.8 = (bf16[2,64,512]{2,1,0:T(8,128)(2,1)S(1)}, bf16[2,64,512]{2,1,0:T(8,128)(2,1)S(1)}, u32[]{:S(2)}, u32[]{:S(2)}) collective-permute-start(bf16[2,64,512]{2,1,0:T(8,128)(2,1)S(1)} %get-tuple-element.29), channel_id=1, source_target_pairs={{0,22},{2,20},{4,18},{6,16},{8,30},{10,28},{12,26},{14,24},{16,6},... | collective-permute-start | bytes 393224 | tf_op jit(solution)/shard_map/ppermute | solution.py:223
  20.0 14.8 %collective-permute-start.9 = (bf16[2,64,512]{2,1,0:T(8,128)(2,1)S(1)}, bf16[2,64,512]{2,1,0:T(8,128)(2,1)S(1)}, u32[]{:S(2)}, u32[]{:S(2)}) collective-permute-start(bf16[2,64,512]{2,1,0:T(8,128)(2,1)S(1)} %get-tuple-element.30), channel_id=1, source_target_pairs={{0,12},{2,14},{4,8},{6,10},{8,4},{10,6},{12,0},{14,2},{16,28},{18,... | collective-permute-start | bytes 393224 | tf_op jit(solution)/shard_map/ppermute | solution.py:223
  23.3 18.8 %collective-permute-start.10 = (bf16[2,64,512]{2,1,0:T(8,128)(2,1)S(1)}, bf16[2,64,512]{2,1,0:T(8,128)(2,1)S(1)}, u32[]{:S(2)}, u32[]{:S(2)}) collective-permute-start(bf16[2,64,512]{2,1,0:T(8,128)(2,1)S(1)} %get-tuple-element.31), channel_id=1, source_target_pairs={{0,24},{2,26},{4,28},{6,30},{8,16},{10,18},{12,20},{14,22},{16,8},... | collective-permute-start | bytes 393224 | tf_op jit(solution)/shard_map/ppermute | solution.py:223
  28.5 14.4 %collective-permute-start.3 = (bf16[2,64,512]{2,1,0:T(8,128)(2,1)S(1)}, bf16[2,64,512]{2,1,0:T(8,128)(2,1)S(1)}, u32[]{:S(2)}, u32[]{:S(2)}) collective-permute-start(bf16[2,64,512]{2,1,0:T(8,128)(2,1)S(1)} %get-tuple-element.24), channel_id=1, source_target_pairs={{0,14},{2,12},{4,10},{6,8},{8,6},{10,4},{12,2},{14,0},{16,30},{18,... | collective-permute-start | bytes 393224 | tf_op jit(solution)/shard_map/ppermute | solution.py:223
  28.5 16.0 %collective-permute-start.4 = (bf16[2,64,512]{2,1,0:T(8,128)(2,1)S(1)}, bf16[2,64,512]{2,1,0:T(8,128)(2,1)S(1)}, u32[]{:S(2)}, u32[]{:S(2)}) collective-permute-start(bf16[2,64,512]{2,1,0:T(8,128)(2,1)S(1)} %get-tuple-element.25), channel_id=1, source_target_pairs={{0,26},{2,24},{4,30},{6,28},{8,18},{10,16},{12,22},{14,20},{16,10}... | collective-permute-start | bytes 393224 | tf_op jit(solution)/shard_map/ppermute | solution.py:223
  31.9 13.1 %collective-permute-start.5 = (bf16[2,64,512]{2,1,0:T(8,128)(2,1)S(1)}, bf16[2,64,512]{2,1,0:T(8,128)(2,1)S(1)}, u32[]{:S(2)}, u32[]{:S(2)}) collective-permute-start(bf16[2,64,512]{2,1,0:T(8,128)(2,1)S(1)} %get-tuple-element.26), channel_id=1, source_target_pairs={{0,4},{2,6},{4,0},{6,2},{8,12},{10,14},{12,8},{14,10},{16,20},{18,... | collective-permute-start | bytes 393224 | tf_op jit(solution)/shard_map/ppermute | solution.py:223
  34.8 11.2 %collective-permute-start.6 = (bf16[2,64,512]{2,1,0:T(8,128)(2,1)S(1)}, bf16[2,64,512]{2,1,0:T(8,128)(2,1)S(1)}, u32[]{:S(2)}, u32[]{:S(2)}) collective-permute-start(bf16[2,64,512]{2,1,0:T(8,128)(2,1)S(1)} %get-tuple-element.27), channel_id=1, source_target_pairs={{0,28},{2,30},{4,24},{6,26},{8,20},{10,22},{12,16},{14,18},{16,12}... | collective-permute-start | bytes 393224 | tf_op jit(solution)/shard_map/ppermute | solution.py:223
  42.1 8.2 %collective-permute-start = (bf16[2,64,512]{2,1,0:T(8,128)(2,1)S(1)}, bf16[2,64,512]{2,1,0:T(8,128)(2,1)S(1)}, u32[]{:S(2)}, u32[]{:S(2)}) collective-permute-start(bf16[2,64,512]{2,1,0:T(8,128)(2,1)S(1)} %get-tuple-element.20), channel_id=1, source_target_pairs={{0,6},{2,4},{4,2},{6,0},{8,14},{10,12},{12,10},{14,8},{16,22},{18,... | collective-permute-start | bytes 393224 | tf_op jit(solution)/shard_map/ppermute | solution.py:223
  42.9 7.6 %collective-permute-start.1 = (bf16[2,64,512]{2,1,0:T(8,128)(2,1)S(1)}, bf16[2,64,512]{2,1,0:T(8,128)(2,1)S(1)}, u32[]{:S(2)}, u32[]{:S(2)}) collective-permute-start(bf16[2,64,512]{2,1,0:T(8,128)(2,1)S(1)} %get-tuple-element.21), channel_id=1, source_target_pairs={{0,30},{2,28},{4,26},{6,24},{8,22},{10,20},{12,18},{14,16},{16,14}... | collective-permute-start | bytes 393224 | tf_op jit(solution)/shard_map/ppermute | solution.py:223
  44.5 5.9 %collective-permute-start.2 = (bf16[2,64,512]{2,1,0:T(8,128)(2,1)S(1)}, bf16[2,64,512]{2,1,0:T(8,128)(2,1)S(1)}, u32[]{:S(2)}, u32[]{:S(2)}) collective-permute-start(bf16[2,64,512]{2,1,0:T(8,128)(2,1)S(1)} %get-tuple-element.22), channel_id=1, source_target_pairs={{0,2},{2,0},{4,6},{6,4},{8,10},{10,8},{12,14},{14,12},{16,18},{18,... | collective-permute-start | bytes 393224 | tf_op jit(solution)/shard_map/ppermute | solution.py:223
  50.6 3.1 %copy-start = (f32[8,1024]{1,0:T(8,128)S(1)}, f32[8,1024]{1,0:T(8,128)}, u32[]{:S(2)}) copy-start(f32[8,1024]{1,0:T(8,128)} %constant.10.clone.first) | copy-start | bytes 98308
  52.1 14.8 %collective-permute-start.15 = (f32[4,2,128,128]{3,2,1,0:T(8,128)S(1)}, f32[4,2,128,128]{3,2,1,0:T(8,128)S(1)}, u32[]{:S(2)}, u32[]{:S(2)}) collective-permute-start(f32[4,2,128,128]{3,2,1,0:T(8,128)S(1)} %sent.1), channel_id=1, source_target_pairs={{0,1},{1,0},{2,3},{3,2},{4,5},{5,4},{6,7},{7,6},{8,9},{9,8},{10,11... | collective-permute-start | bytes 1572872 | tf_op jit(solution)/shard_map/ppermute | solution.py:295
  61.3 5.7 %collective-permute-start.16 = (f32[8,128]{1,0:T(8,128)S(1)}, f32[8,128]{1,0:T(8,128)S(1)}, u32[]{:S(2)}, u32[]{:S(2)}) collective-permute-start(f32[8,128]{1,0:T(8,128)S(1)} %get-tuple-element.36.gains_ref), channel_id=1, source_target_pairs={{0,1},{1,0},{2,3},{3,2},{4,5},{5,4},{6,7},{7,6},{8,9},{9,8},{10,11... | collective-permute-start | bytes 12296 | tf_op jit(solution)/shard_map/ppermute | solution.py:295

commit v7 on v6

--- a/solution.py
+++ b/solution.py
@@ -17,6 +17,7 @@
 LANES = 128
 GROUP = 4
 FIRST = 2
+RAW = 3
 SPLITS = 2
 
 VMEM = pl.BlockSpec(memory_space=pltpu.VMEM)
@@ -84,7 +85,8 @@
     return w * scales, p * scales
 
 
-def calibrate_kernel(v_ref, first, gains_ref, blocks_ref, vt_ref):
+def calibrate_kernel(owners, slots, table_ref, me_ref, v_ref, first, gains_ref, blocks_ref, *refs):
+    ready_refs, vt_ref = refs[:-1], refs[-1]
     _, count, frames = v_ref.shape
     rows = lax.broadcasted_iota(jnp.int32, (2 * RANK, 1), 0)
     sign = jnp.where(rows < RANK, 1.0, -1.0)
@@ -116,6 +118,14 @@
     gains_ref[...] = gains
     for k in range(count // TB):
         blocks_ref[k : k + 1, :] = gains[:, k * TB : (k + 1) * TB]
+    for d in range(1, owners):
+        owner = lax.rem(me_ref[0] + d, owners)
+        for s in range(RAW, KPO):
+            tile = table_ref[owner * slots + s]
+            both = product(v_ref, tile)
+            scale = outer(blocks_ref, tile)
+            ready_refs[d - 1][s - RAW, 0] = (scale * both[:TB]).astype(jnp.bfloat16)
+            ready_refs[d - 1][s - RAW, 1] = (scale * both[TB:]).astype(jnp.bfloat16)
 
 
 def product(v_ref, tile):
@@ -142,6 +152,9 @@
 
 
 def front_kernel(targets, per, me_ref, mask_ref, volt_ref, *refs):
+    if 0 in targets:
+        table_ref, *refs = refs
+        staged_ref = refs.pop(len(targets))
     out_refs, (taken, flags, sem) = refs[: len(targets)], refs[len(targets) :]
     parts, size, frames = out_refs[0].shape
     cols = frames // LANES
@@ -154,6 +167,9 @@
         copies[-1].start()
     flag_copy = pltpu.make_async_copy(mask_ref, flags, sem.at[len(targets)])
     flag_copy.start()
+    if 0 in targets:
+        copies.append(pltpu.make_async_copy(table_ref, staged_ref, sem.at[len(targets) + 1]))
+        copies[-1].start()
     row = lax.broadcasted_iota(jnp.int32, (rows, rows), 0)
     col = lax.broadcasted_iota(jnp.int32, (rows, rows), 1)
     block = lax.div(row, per)
@@ -187,7 +203,7 @@
         v_ref[:, pl.ds(start, size), :] = block_ref[...]
 
 
-def corner_turn(volt, mask):
+def corner_turn(volt, mask, table):
     parts = lax.axis_size("inp")
     _, size, both, frames = volt.shape
     me = lax.axis_index("inp").reshape(1)
@@ -205,23 +221,27 @@
     cuts = [0, *range(FIRST, GROUP, FIRST), *range(GROUP, parts, GROUP), parts]
     groups = [order[start:stop] for start, stop in zip(cuts, cuts[1:])][::-1]
     for targets in groups:
+        extra = [in_hbm(table)] if 0 in targets else []
         fronts = pl.pallas_call(
             functools.partial(front_kernel, targets, min(size, 16)),
-            out_shape=[small(parts)(shape, volt.dtype)] * len(targets),
-            in_specs=[SMEM, HBM, HBM],
-            out_specs=[VMEM] * len(targets),
+            out_shape=[small(parts)(shape, volt.dtype)] * len(targets)
+            + [pltpu.VMEM(x.shape, x.dtype) for x in extra],
+            in_specs=[SMEM, HBM, HBM] + [HBM] * len(extra),
+            out_specs=[VMEM] * (len(targets) + len(extra)),
             scratch_shapes=[
                 pltpu.VMEM((len(targets), chunk, LANES), volt.dtype),
                 pltpu.VMEM((1, size), mask.dtype),
-                pltpu.SemaphoreType.DMA((len(targets) + 1,)),
+                pltpu.SemaphoreType.DMA((len(targets) + 2,)),
             ],
             compiler_params=pltpu.CompilerParams(vmem_limit_bytes=8 << 20),
             name="front",
-        )(me, in_hbm(mask.reshape(1, size)), in_hbm(rows))
+        )(me, in_hbm(mask.reshape(1, size)), in_hbm(rows), *extra)
+        if 0 in targets:
+            staged_table = fronts[-1]
         for d, block in zip(targets, fronts):
             pairs = [(j, j ^ d) for j in range(parts)]
             blocks.append(lax.ppermute(block, "inp", pairs) if d else block)
-    return pl.pallas_call(
+    joined = pl.pallas_call(
         functools.partial(join_kernel, sum(groups, [])),
         out_shape=pltpu.VMEM((both, parts * size, frames), volt.dtype),
         in_specs=[SMEM] + [VMEM] * parts,
@@ -229,6 +249,7 @@
         compiler_params=pltpu.CompilerParams(vmem_limit_bytes=4 << 20),
         name="join",
     )(me, *[in_vmem(block, parts // 8) for block in blocks])
+    return joined, staged_table
 
 
 def in_hbm(x):
@@ -242,7 +263,7 @@
 def sent_kernel(owners, slots, table_ref, me_ref, v_ref, *out_refs):
     for d in range(1, owners):
         owner = lax.rem(me_ref[0] + d, owners)
-        for s in range(KPO):
+        for s in range(RAW):
             both = product(v_ref, table_ref[owner * slots + s])
             out_refs[d - 1][s, 0] = both[:TB]
             out_refs[d - 1][s, 1] = both[TB:]
@@ -262,17 +283,20 @@
 
 
 def others_kernel(owners, slots, table_ref, me_ref, *refs):
-    tile_refs, gain_refs = refs[: owners - 1], refs[owners - 1 : 2 * owners - 2]
+    away = owners - 1
+    tile_refs, ready_refs, gain_refs = refs[:away], refs[away : 2 * away], refs[2 * away : 3 * away]
     vis_ref, held, sem = refs[-3:]
     me = me_ref[0]
     copies = []
     for d in range(1, owners):
-        source = lax.rem(me + owners - d, owners)
-        for s in range(KPO):
+        to = vis_ref.at[lax.rem(me + owners - d, owners)]
+        copies.append(pltpu.make_async_copy(ready_refs[d - 1], to.at[pl.ds(RAW, KPO - RAW)], sem.at[d - 1, RAW]))
+        copies[-1].start()
+        for s in range(RAW):
             scale = outer(gain_refs[d - 1], table_ref[me * slots + s])
             for part in range(2):
                 held[d - 1, s, part] = (scale * tile_refs[d - 1][s, part]).astype(jnp.bfloat16)
-            copies.append(pltpu.make_async_copy(held.at[d - 1, s], vis_ref.at[source, s], sem.at[d - 1, s]))
+            copies.append(pltpu.make_async_copy(held.at[d - 1, s], to.at[s], sem.at[d - 1, s]))
             copies[-1].start()
     for copy in copies:
         copy.wait()
@@ -285,10 +309,9 @@
 def body(volt, mask, table):
     owners = lax.axis_size("chan")
     slots = table.shape[0] // owners
-    flat = in_vmem(corner_turn(volt, mask))
+    flat, table = (in_vmem(x) for x in corner_turn(volt, mask, table))
     _, count, frames = flat.shape
     me = lax.axis_index("chan").reshape(1)
-    table = in_hbm(table)
     blocks = count // TB
 
     def shift(x, d):
@@ -296,7 +319,7 @@
 
     sent = pl.pallas_call(
         functools.partial(sent_kernel, owners, slots),
-        out_shape=[(pltpu.VMEM if owners == 2 else jax.ShapeDtypeStruct)((KPO, 2, TB, TB), jnp.float32)] * (owners - 1),
+        out_shape=[(pltpu.VMEM if owners == 2 else jax.ShapeDtypeStruct)((RAW, 2, TB, TB), jnp.float32)] * (owners - 1),
         in_specs=[SMEM, SMEM, VMEM],
         out_specs=[VMEM] * (owners - 1),
         compiler_params=pltpu.CompilerParams(vmem_limit_bytes=12 << 20),
@@ -304,19 +327,21 @@
     )(table, me, flat)
     arrived = [in_vmem(shift(sent[d - 1], d), owners) for d in range(1, owners)]
 
-    gains, by_block = pl.pallas_call(
-        calibrate_kernel,
+    gains, by_block, *ready = pl.pallas_call(
+        functools.partial(calibrate_kernel, owners, slots),
         out_shape=[
             jax.ShapeDtypeStruct((1, count), jnp.float32),
             pltpu.VMEM((blocks, TB), jnp.float32),
-        ],
-        in_specs=[VMEM, VMEM],
-        out_specs=[VMEM] * 2,
+        ]
+        + [small(8 * owners)((KPO - RAW, 2, TB, TB), jnp.bfloat16)] * (owners - 1),
+        in_specs=[SMEM, SMEM, VMEM, VMEM],
+        out_specs=[VMEM] * (owners + 1),
         scratch_shapes=[pltpu.VMEM((2, frames, count), jnp.bfloat16)],
         compiler_params=pltpu.CompilerParams(vmem_limit_bytes=12 << 20),
         name="calibrate",
-    )(flat, in_vmem(jnp.asarray(first_basis(count))))
+    )(table, me, flat, in_vmem(jnp.asarray(first_basis(count))))
     other_gains = [in_vmem(shift(by_block, d), owners) for d in range(1, owners)]
+    ready = [in_vmem(shift(ready[d - 1], d), owners) for d in range(1, owners)]
 
     vis_shape = jax.ShapeDtypeStruct((owners, KPO, 2, TB, TB), jnp.bfloat16)
     vis = pl.pallas_call(
@@ -331,16 +356,16 @@
     vis = pl.pallas_call(
         functools.partial(others_kernel, owners, slots),
         out_shape=vis_shape,
-        in_specs=[SMEM, SMEM] + [VMEM] * (2 * owners - 2) + [ANY],
+        in_specs=[SMEM, SMEM] + [VMEM] * (3 * owners - 3) + [ANY],
         out_specs=ANY,
         scratch_shapes=[
-            pltpu.VMEM((owners - 1, KPO, 2, TB, TB), jnp.bfloat16),
-            pltpu.SemaphoreType.DMA((owners - 1, KPO)),
+            pltpu.VMEM((owners - 1, RAW, 2, TB, TB), jnp.bfloat16),
+            pltpu.SemaphoreType.DMA((owners - 1, RAW + 1)),
         ],
-        input_output_aliases={2 * owners: 0},
+        input_output_aliases={3 * owners - 1: 0},
         compiler_params=pltpu.CompilerParams(vmem_limit_bytes=12 << 20),
         name="others",
-    )(table, me, *arrived, *other_gains, vis)
+    )(table, me, *arrived, *ready, *other_gains, vis)
     return (vis[None, :, None], gains.reshape(1, 1, count))
 
 

time: 68.8 us -> 67.9 us (0.987)
  waiting for transfers between devices: 18.9 us -> 16.5 us
  starting transfers between devices: 29.3 us -> 30.8 us
    ppermute x2 -> x3, waiting for transfers between devices: 3.14 us -> 0.65 us  [shift(): lax.ppermute(x, 'chan', [(j, (j + d) % owners) for j in range(owners)])]
    ppermute x2 -> x3, starting transfers between devices: 2.09 us -> 3.62 us  [shift(): lax.ppermute(x, 'chan', [(j, (j + d) % owners) for j in range(owners)])]
  transfers between devices with their start and end apart: 17 -> 18, of which waited for: 8 -> 8; matrix products, arithmetic and copies ran while one was open for 0% -> 0% of each run, Pallas kernels for 22% -> 23%
where the time goes in v7:
time: 67.9 us; the launch traced here: 67.4 us
  starting transfers between devices  30.8 us (45%)
  Pallas kernels  19.4 us (29%)
  waiting for transfers between devices  16.5 us (24%)
  between operations  0.73 us (1%)
    ppermute x15, starting transfers between devices, corner_turn(): blocks.append(lax.ppermute(block, 'inp', pairs) if d else block)  27.2 us
    ppermute x15, waiting for transfers between devices, corner_turn(): blocks.append(lax.ppermute(block, 'inp', pairs) if d else block)  15.8 us
    pallas_call x1, Pallas kernels, body(): pl.pallas_call(functools.partial(calibrate_kernel, owners, slots), out_sh...  8.01 us
    pallas_call x5, Pallas kernels, corner_turn(): pl.pallas_call(functools.partial(front_kernel, targets, min(size, 16)), o...  6.79 us
    ppermute x3, starting transfers between devices, shift(): lax.ppermute(x, 'chan', [(j, (j + d) % owners) for j in range(owners)])  3.62 us
    pallas_call x1, Pallas kernels, body(): pl.pallas_call(functools.partial(own_kernel, slots), out_shape=vis_shape,...  1.97 us
    pallas_call x1, Pallas kernels, body(): pl.pallas_call(functools.partial(others_kernel, owners, slots), out_shape...  1.36 us
  transfers between devices with their start and end apart: 18, of which 8 were waited for; matrix products, arithmetic and copies ran while one was open for 0% of the time, Pallas kernels for 23%

profile of v7, /device:TPU:0, one launch (start us, length us, event | category | flops | bytes accessed | tf_op | source)
XLA Modules:
  0.0 67.4 jit_solution(8416356592573510005)
XLA Ops:
  0.6 1.2 %front.9 = (bf16[2,64,512]{2,1,0:T(8,128)(2,1)S(1)}, bf16[2,64,512]{2,1,0:T(8,128)(2,1)S(1)}) custom-call(s32[1]{0:T(128)} %bitcast.me_ref, s32[1,64]{1,0:T(1,128)} %bitcast.18, bf16[8192,128]{1,0:T(8,128)(2,1)} %bitcast.12), custom_call_target="tpu_custom_call" | custom-call | tf_op jit(solution)/shard_map/front/pallas_call | solution.py:225
  1.9 4.1 %collective-permute-start.13 = (bf16[2,64,512]{2,1,0:T(8,128)(2,1)S(1)}, bf16[2,64,512]{2,1,0:T(8,128)(2,1)S(1)}, u32[]{:S(2)}, u32[]{:S(2)}) collective-permute-start(bf16[2,64,512]{2,1,0:T(8,128)(2,1)S(1)} %get-tuple-element.37), channel_id=1, source_target_pairs={{0,16},{2,18},{4,20},{6,22},{8,24},{10,26},{12,28},{14,30},{16,0},... | collective-permute-start | bytes 393224 | tf_op jit(solution)/shard_map/ppermute | solution.py:243
  6.0 0.0 collective-permute-start.14
  6.0 1.2 %front.8 = (bf16[2,64,512]{2,1,0:T(8,128)(2,1)S(1)}, bf16[2,64,512]{2,1,0:T(8,128)(2,1)S(1)}) custom-call(s32[1]{0:T(128)} %bitcast.me_ref, s32[1,64]{1,0:T(1,128)} %bitcast.19, bf16[8192,128]{1,0:T(8,128)(2,1)} %bitcast.13), custom_call_target="tpu_custom_call" | custom-call | tf_op jit(solution)/shard_map/front/pallas_call | solution.py:225
  7.2 1.6 %collective-permute-start.11 = (bf16[2,64,512]{2,1,0:T(8,128)(2,1)S(1)}, bf16[2,64,512]{2,1,0:T(8,128)(2,1)S(1)}, u32[]{:S(2)}, u32[]{:S(2)}) collective-permute-start(bf16[2,64,512]{2,1,0:T(8,128)(2,1)S(1)} %get-tuple-element.35), channel_id=1, source_target_pairs={{0,8},{2,10},{4,12},{6,14},{8,0},{10,2},{12,4},{14,6},{16,24},{18,... | collective-permute-start | bytes 393224 | tf_op jit(solution)/shard_map/ppermute | solution.py:243
  8.8 3.0 %collective-permute-start.12 = (bf16[2,64,512]{2,1,0:T(8,128)(2,1)S(1)}, bf16[2,64,512]{2,1,0:T(8,128)(2,1)S(1)}, u32[]{:S(2)}, u32[]{:S(2)}) collective-permute-start(bf16[2,64,512]{2,1,0:T(8,128)(2,1)S(1)} %get-tuple-element.36), channel_id=1, source_target_pairs={{0,20},{2,22},{4,16},{6,18},{8,28},{10,30},{12,24},{14,26},{16,4},... | collective-permute-start | bytes 393224 | tf_op jit(solution)/shard_map/ppermute | solution.py:243
  11.9 1.4 %front.7 = (bf16[2,64,512]{2,1,0:T(8,128)(2,1)S(1)}, bf16[2,64,512]{2,1,0:T(8,128)(2,1)S(1)}, bf16[2,64,512]{2,1,0:T(8,128)(2,1)S(1)}, bf16[2,64,512]{2,1,0:T(8,128)(2,1)S(1)}) custom-call(s32[1]{0:T(128)} %bitcast.me_ref, s32[1,64]{1,0:T(1,128)} %bitcast.20, bf16[8192,128]{1,0:T(8,128)(2,1)} %bitcast.14), custom_call_target="tpu_custom_call" | custom-call | tf_op jit(solution)/shard_map/front/pallas_call | solution.py:225
  13.3 0.5 collective-permute-start.7
  13.8 1.4 %front.6 = (bf16[2,64,512]{2,1,0:T(8,128)(2,1)S(1)}, bf16[2,64,512]{2,1,0:T(8,128)(2,1)S(1)}, bf16[2,64,512]{2,1,0:T(8,128)(2,1)S(1)}, bf16[2,64,512]{2,1,0:T(8,128)(2,1)S(1)}) custom-call(s32[1]{0:T(128)} %bitcast.me_ref, s32[1,64]{1,0:T(1,128)} %bitcast.21, bf16[8192,128]{1,0:T(8,128)(2,1)} %bitcast.15), custom_call_target="tpu_custom_call" | custom-call | tf_op jit(solution)/shard_map/front/pallas_call | solution.py:225
  15.3 0.6 collective-permute-done.13.refs_14_
  15.9 0.0 collective-permute-start.8
  15.9 4.1 %collective-permute-done.14.refs_15_ = bf16[2,64,512]{2,1,0:T(8,128)(2,1)S(1)} collective-permute-done((bf16[2,64,512]{2,1,0:T(8,128)(2,1)S(1)}, bf16[2,64,512]{2,1,0:T(8,128)(2,1)S(1)}, u32[]{:S(2)}, u32[]{:S(2)}) %collective-permute-start.14) | collective-permute-done | bytes 131104 | tf_op jit(solution)/shard_map/ppermute | solution.py:243
  20.0 3.3 %collective-permute-start.9 = (bf16[2,64,512]{2,1,0:T(8,128)(2,1)S(1)}, bf16[2,64,512]{2,1,0:T(8,128)(2,1)S(1)}, u32[]{:S(2)}, u32[]{:S(2)}) collective-permute-start(bf16[2,64,512]{2,1,0:T(8,128)(2,1)S(1)} %get-tuple-element.33), channel_id=1, source_target_pairs={{0,12},{2,14},{4,8},{6,10},{8,4},{10,6},{12,0},{14,2},{16,28},{18,... | collective-permute-start | bytes 393224 | tf_op jit(solution)/shard_map/ppermute | solution.py:243
  23.3 0.0 collective-permute-done.11.refs_12_
  23.3 1.8 %collective-permute-start.10 = (bf16[2,64,512]{2,1,0:T(8,128)(2,1)S(1)}, bf16[2,64,512]{2,1,0:T(8,128)(2,1)S(1)}, u32[]{:S(2)}, u32[]{:S(2)}) collective-permute-start(bf16[2,64,512]{2,1,0:T(8,128)(2,1)S(1)} %get-tuple-element.34), channel_id=1, source_target_pairs={{0,24},{2,26},{4,28},{6,30},{8,16},{10,18},{12,20},{14,22},{16,8},... | collective-permute-start | bytes 393224 | tf_op jit(solution)/shard_map/ppermute | solution.py:243
  25.2 3.4 %collective-permute-done.12.refs_13_ = bf16[2,64,512]{2,1,0:T(8,128)(2,1)S(1)} collective-permute-done((bf16[2,64,512]{2,1,0:T(8,128)(2,1)S(1)}, bf16[2,64,512]{2,1,0:T(8,128)(2,1)S(1)}, u32[]{:S(2)}, u32[]{:S(2)}) %collective-permute-start.12) | collective-permute-done | bytes 131104 | tf_op jit(solution)/shard_map/ppermute | solution.py:243
  28.5 0.0 collective-permute-start.3
  28.5 0.0 collective-permute-done.7.refs_8_
  28.5 1.9 %collective-permute-start.4 = (bf16[2,64,512]{2,1,0:T(8,128)(2,1)S(1)}, bf16[2,64,512]{2,1,0:T(8,128)(2,1)S(1)}, u32[]{:S(2)}, u32[]{:S(2)}) collective-permute-start(bf16[2,64,512]{2,1,0:T(8,128)(2,1)S(1)} %get-tuple-element.28), channel_id=1, source_target_pairs={{0,26},{2,24},{4,30},{6,28},{8,18},{10,16},{12,22},{14,20},{16,10}... | collective-permute-start | bytes 393224 | tf_op jit(solution)/shard_map/ppermute | solution.py:243
  30.5 1.4 %front.5 = (bf16[2,64,512]{2,1,0:T(8,128)(2,1)S(1)}, bf16[2,64,512]{2,1,0:T(8,128)(2,1)S(1)}, bf16[2,64,512]{2,1,0:T(8,128)(2,1)S(1)}, bf16[2,64,512]{2,1,0:T(8,128)(2,1)S(1)}, s32[64]{0:T(128)S(1)}) custom-call(s32[1]{0:T(128)} %bitcast.me_ref, s32[1,64]{1,0:T(1,128)} %bitcast.22, bf16[8192,128]{1,0:T(8,128)(2,1)} %bitcast.16, s32[64]{0:T(128)} %refs_0_.1), custom_call_target="tpu_custom_call" | custom-call | tf_op jit(solution)/shard_map/front/pallas_call | solution.py:225
  31.9 0.0 collective-permute-done.8.refs_9_
  31.9 0.6 collective-permute-start.5
  32.5 2.2 %collective-permute-done.9.refs_10_ = bf16[2,64,512]{2,1,0:T(8,128)(2,1)S(1)} collective-permute-done((bf16[2,64,512]{2,1,0:T(8,128)(2,1)S(1)}, bf16[2,64,512]{2,1,0:T(8,128)(2,1)S(1)}, u32[]{:S(2)}, u32[]{:S(2)}) %collective-permute-start.9) | collective-permute-done | bytes 131104 | tf_op jit(solution)/shard_map/ppermute | solution.py:243
  34.8 7.4 %collective-permute-start.6 = (bf16[2,64,512]{2,1,0:T(8,128)(2,1)S(1)}, bf16[2,64,512]{2,1,0:T(8,128)(2,1)S(1)}, u32[]{:S(2)}, u32[]{:S(2)}) collective-permute-start(bf16[2,64,512]{2,1,0:T(8,128)(2,1)S(1)} %get-tuple-element.30), channel_id=1, source_target_pairs={{0,28},{2,30},{4,24},{6,26},{8,20},{10,22},{12,16},{14,18},{16,12}... | collective-permute-start | bytes 393224 | tf_op jit(solution)/shard_map/ppermute | solution.py:243
  42.1 0.0 collective-permute-done.10.refs_11_
  42.1 0.8 %collective-permute-start = (bf16[2,64,512]{2,1,0:T(8,128)(2,1)S(1)}, bf16[2,64,512]{2,1,0:T(8,128)(2,1)S(1)}, u32[]{:S(2)}, u32[]{:S(2)}) collective-permute-start(bf16[2,64,512]{2,1,0:T(8,128)(2,1)S(1)} %get-tuple-element.23), channel_id=1, source_target_pairs={{0,6},{2,4},{4,2},{6,0},{8,14},{10,12},{12,10},{14,8},{16,22},{18,... | collective-permute-start | bytes 393224 | tf_op jit(solution)/shard_map/ppermute | solution.py:243
  42.9 0.0 collective-permute-done.3.refs_4_
  42.9 1.6 %collective-permute-start.1 = (bf16[2,64,512]{2,1,0:T(8,128)(2,1)S(1)}, bf16[2,64,512]{2,1,0:T(8,128)(2,1)S(1)}, u32[]{:S(2)}, u32[]{:S(2)}) collective-permute-start(bf16[2,64,512]{2,1,0:T(8,128)(2,1)S(1)} %get-tuple-element.24), channel_id=1, source_target_pairs={{0,30},{2,28},{4,26},{6,24},{8,22},{10,20},{12,18},{14,16},{16,14}... | collective-permute-start | bytes 393224 | tf_op jit(solution)/shard_map/ppermute | solution.py:243
  44.5 0.0 collective-permute-done.4.refs_5_
  44.5 0.5 collective-permute-start.2
  45.0 0.0 collective-permute-done.5.refs_6_
  45.0 1.0 %collective-permute-done.6.refs_7_ = bf16[2,64,512]{2,1,0:T(8,128)(2,1)S(1)} collective-permute-done((bf16[2,64,512]{2,1,0:T(8,128)(2,1)S(1)}, bf16[2,64,512]{2,1,0:T(8,128)(2,1)S(1)}, u32[]{:S(2)}, u32[]{:S(2)}) %collective-permute-start.6) | collective-permute-done | bytes 131104 | tf_op jit(solution)/shard_map/ppermute | solution.py:243
  45.9 4.4 %collective-permute-done.refs_0_ = bf16[2,64,512]{2,1,0:T(8,128)(2,1)S(1)} collective-permute-done((bf16[2,64,512]{2,1,0:T(8,128)(2,1)S(1)}, bf16[2,64,512]{2,1,0:T(8,128)(2,1)S(1)}, u32[]{:S(2)}, u32[]{:S(2)}) %collective-permute-start) | collective-permute-done | bytes 131104 | tf_op jit(solution)/shard_map/ppermute | solution.py:243
  50.3 0.1 collective-permute-done.1.refs_1_
  50.5 0.0 collective-permute-done.2.refs_2_
  50.5 0.2 join.1.v_ref
  50.6 0.0 copy-start
  50.6 1.1 %sent.1 = f32[3,2,128,128]{3,2,1,0:T(8,128)S(1)} custom-call(s32[64]{0:T(128)S(1)} %get-tuple-element.22.table_ref, s32[1]{0:T(128)} %bitcast.5.me_ref, bf16[2,1024,512]{2,1,0:T(8,128)(2,1)S(1)} %join.1.v_ref), custom_call_target="tpu_custom_call" | custom-call | tf_op jit(solution)/shard_map/sent/pallas_call | solution.py:320
  51.8 1.6 %collective-permute-start.15 = (f32[3,2,128,128]{3,2,1,0:T(8,128)S(1)}, f32[3,2,128,128]{3,2,1,0:T(8,128)S(1)}, u32[]{:S(2)}, u32[]{:S(2)}) collective-permute-start(f32[3,2,128,128]{3,2,1,0:T(8,128)S(1)} %sent.1), channel_id=1, source_target_pairs={{0,1},{1,0},{2,3},{3,2},{4,5},{5,4},{6,7},{7,6},{8,9},{9,8},{10,11... | collective-permute-start | bytes 1179656 | tf_op jit(solution)/shard_map/ppermute | solution.py:318
  53.4 0.0 copy-done
  53.4 8.0 %calibrate.1 = (f32[1,1024]{1,0:T(1,128)}, f32[8,128]{1,0:T(8,128)S(1)}, bf16[1,2,128,128]{3,2,1,0:T(8,128)(2,1)S(1)}) custom-call(s32[64]{0:T(128)S(1)} %get-tuple-element.22.table_ref, s32[1]{0:T(128)} %bitcast.5.me_ref, bf16[2,1024,512]{2,1,0:T(8,128)(2,1)S(1)} %join.1.v_ref, f32[8,1024]{1,0:T(8,128)S(1)} %copy-done), custom_call_target="tpu_custom_call" | custom-call | tf_op jit(solution)/shard_map/calibrate/pallas_call | solution.py:330
  61.4 0.5 collective-permute-start.16
  61.9 1.5 %collective-permute-start.17 = (f32[8,128]{1,0:T(8,128)S(1)}, f32[8,128]{1,0:T(8,128)S(1)}, u32[]{:S(2)}, u32[]{:S(2)}) collective-permute-start(f32[8,128]{1,0:T(8,128)S(1)} %get-tuple-element.40.gains_ref), channel_id=1, source_target_pairs={{0,1},{1,0},{2,3},{3,2},{4,5},{5,4},{6,7},{7,6},{8,9},{9,8},{10,11... | collective-permute-start | bytes 12296 | tf_op jit(solution)/shard_map/ppermute | solution.py:318
  63.4 2.0 %own.1.refs_3_ = bf16[2,4,2,128,128]{4,3,2,1,0:T(8,128)(2,1)} custom-call(s32[64]{0:T(128)S(1)} %get-tuple-element.22.table_ref, s32[1]{0:T(128)} %bitcast.5.me_ref, bf16[2,1024,512]{2,1,0:T(8,128)(2,1)S(1)} %join.1.v_ref, f32[8,128]{1,0:T(8,128)S(1)} %get-tuple-element.40.gains_ref), custom_call_target="tpu_custom_call" | custom-call | tf_op jit(solution)/shard_map/own/pallas_call | solution.py:347
  65.4 0.6 collective-permute-done.17.refs_2_
  66.0 0.0 collective-permute-done.16.refs_1_
  66.0 0.0 collective-permute-done.15.refs_0_
  66.0 1.4 %others.1 = bf16[2,4,2,128,128]{4,3,2,1,0:T(8,128)(2,1)} custom-call(s32[64]{0:T(128)S(1)} %get-tuple-element.22.table_ref, s32[1]{0:T(128)} %bitcast.5.me_ref, f32[3,2,128,128]{3,2,1,0:T(8,128)S(1)} %collective-permute-done.15.refs_0_, bf16[1,2,128,128]{3,2,1,0:T(8,128)(2,1)S(1)} %collective-permute-done.16.refs_1_, ...), custom_call_target="tpu_custom_call", output_to_operand_aliasing={{}: (5, {})} | custom-call | tf_op jit(solution)/shard_map/others/pallas_call | solution.py:356
Async XLA Ops:
  1.9 14.0 %collective-permute-start.13 = (bf16[2,64,512]{2,1,0:T(8,128)(2,1)S(1)}, bf16[2,64,512]{2,1,0:T(8,128)(2,1)S(1)}, u32[]{:S(2)}, u32[]{:S(2)}) collective-permute-start(bf16[2,64,512]{2,1,0:T(8,128)(2,1)S(1)} %get-tuple-element.37), channel_id=1, source_target_pairs={{0,16},{2,18},{4,20},{6,22},{8,24},{10,26},{12,28},{14,30},{16,0},... | collective-permute-start | bytes 393224 | tf_op jit(solution)/shard_map/ppermute | solution.py:243
  6.0 14.0 %collective-permute-start.14 = (bf16[2,64,512]{2,1,0:T(8,128)(2,1)S(1)}, bf16[2,64,512]{2,1,0:T(8,128)(2,1)S(1)}, u32[]{:S(2)}, u32[]{:S(2)}) collective-permute-start(bf16[2,64,512]{2,1,0:T(8,128)(2,1)S(1)} %get-tuple-element.38), channel_id=1, source_target_pairs={{0,18},{2,16},{4,22},{6,20},{8,26},{10,24},{12,30},{14,28},{16,2},... | collective-permute-start | bytes 393224 | tf_op jit(solution)/shard_map/ppermute | solution.py:243
  7.2 16.1 %collective-permute-start.11 = (bf16[2,64,512]{2,1,0:T(8,128)(2,1)S(1)}, bf16[2,64,512]{2,1,0:T(8,128)(2,1)S(1)}, u32[]{:S(2)}, u32[]{:S(2)}) collective-permute-start(bf16[2,64,512]{2,1,0:T(8,128)(2,1)S(1)} %get-tuple-element.35), channel_id=1, source_target_pairs={{0,8},{2,10},{4,12},{6,14},{8,0},{10,2},{12,4},{14,6},{16,24},{18,... | collective-permute-start | bytes 393224 | tf_op jit(solution)/shard_map/ppermute | solution.py:243
  8.8 19.7 %collective-permute-start.12 = (bf16[2,64,512]{2,1,0:T(8,128)(2,1)S(1)}, bf16[2,64,512]{2,1,0:T(8,128)(2,1)S(1)}, u32[]{:S(2)}, u32[]{:S(2)}) collective-permute-start(bf16[2,64,512]{2,1,0:T(8,128)(2,1)S(1)} %get-tuple-element.36), channel_id=1, source_target_pairs={{0,20},{2,22},{4,16},{6,18},{8,28},{10,30},{12,24},{14,26},{16,4},... | collective-permute-start | bytes 393224 | tf_op jit(solution)/shard_map/ppermute | solution.py:243
  13.3 15.2 %collective-permute-start.7 = (bf16[2,64,512]{2,1,0:T(8,128)(2,1)S(1)}, bf16[2,64,512]{2,1,0:T(8,128)(2,1)S(1)}, u32[]{:S(2)}, u32[]{:S(2)}) collective-permute-start(bf16[2,64,512]{2,1,0:T(8,128)(2,1)S(1)} %get-tuple-element.31), channel_id=1, source_target_pairs={{0,10},{2,8},{4,14},{6,12},{8,2},{10,0},{12,6},{14,4},{16,26},{18,... | collective-permute-start | bytes 393224 | tf_op jit(solution)/shard_map/ppermute | solution.py:243
  15.9 16.0 %collective-permute-start.8 = (bf16[2,64,512]{2,1,0:T(8,128)(2,1)S(1)}, bf16[2,64,512]{2,1,0:T(8,128)(2,1)S(1)}, u32[]{:S(2)}, u32[]{:S(2)}) collective-permute-start(bf16[2,64,512]{2,1,0:T(8,128)(2,1)S(1)} %get-tuple-element.32), channel_id=1, source_target_pairs={{0,22},{2,20},{4,18},{6,16},{8,30},{10,28},{12,26},{14,24},{16,6},... | collective-permute-start | bytes 393224 | tf_op jit(solution)/shard_map/ppermute | solution.py:243
  20.0 14.8 %collective-permute-start.9 = (bf16[2,64,512]{2,1,0:T(8,128)(2,1)S(1)}, bf16[2,64,512]{2,1,0:T(8,128)(2,1)S(1)}, u32[]{:S(2)}, u32[]{:S(2)}) collective-permute-start(bf16[2,64,512]{2,1,0:T(8,128)(2,1)S(1)} %get-tuple-element.33), channel_id=1, source_target_pairs={{0,12},{2,14},{4,8},{6,10},{8,4},{10,6},{12,0},{14,2},{16,28},{18,... | collective-permute-start | bytes 393224 | tf_op jit(solution)/shard_map/ppermute | solution.py:243
  23.3 18.8 %collective-permute-start.10 = (bf16[2,64,512]{2,1,0:T(8,128)(2,1)S(1)}, bf16[2,64,512]{2,1,0:T(8,128)(2,1)S(1)}, u32[]{:S(2)}, u32[]{:S(2)}) collective-permute-start(bf16[2,64,512]{2,1,0:T(8,128)(2,1)S(1)} %get-tuple-element.34), channel_id=1, source_target_pairs={{0,24},{2,26},{4,28},{6,30},{8,16},{10,18},{12,20},{14,22},{16,8},... | collective-permute-start | bytes 393224 | tf_op jit(solution)/shard_map/ppermute | solution.py:243
  28.5 14.4 %collective-permute-start.3 = (bf16[2,64,512]{2,1,0:T(8,128)(2,1)S(1)}, bf16[2,64,512]{2,1,0:T(8,128)(2,1)S(1)}, u32[]{:S(2)}, u32[]{:S(2)}) collective-permute-start(bf16[2,64,512]{2,1,0:T(8,128)(2,1)S(1)} %get-tuple-element.27), channel_id=1, source_target_pairs={{0,14},{2,12},{4,10},{6,8},{8,6},{10,4},{12,2},{14,0},{16,30},{18,... | collective-permute-start | bytes 393224 | tf_op jit(solution)/shard_map/ppermute | solution.py:243
  28.5 16.0 %collective-permute-start.4 = (bf16[2,64,512]{2,1,0:T(8,128)(2,1)S(1)}, bf16[2,64,512]{2,1,0:T(8,128)(2,1)S(1)}, u32[]{:S(2)}, u32[]{:S(2)}) collective-permute-start(bf16[2,64,512]{2,1,0:T(8,128)(2,1)S(1)} %get-tuple-element.28), channel_id=1, source_target_pairs={{0,26},{2,24},{4,30},{6,28},{8,18},{10,16},{12,22},{14,20},{16,10}... | collective-permute-start | bytes 393224 | tf_op jit(solution)/shard_map/ppermute | solution.py:243
  31.9 13.1 %collective-permute-start.5 = (bf16[2,64,512]{2,1,0:T(8,128)(2,1)S(1)}, bf16[2,64,512]{2,1,0:T(8,128)(2,1)S(1)}, u32[]{:S(2)}, u32[]{:S(2)}) collective-permute-start(bf16[2,64,512]{2,1,0:T(8,128)(2,1)S(1)} %get-tuple-element.29), channel_id=1, source_target_pairs={{0,4},{2,6},{4,0},{6,2},{8,12},{10,14},{12,8},{14,10},{16,20},{18,... | collective-permute-start | bytes 393224 | tf_op jit(solution)/shard_map/ppermute | solution.py:243
  34.8 11.2 %collective-permute-start.6 = (bf16[2,64,512]{2,1,0:T(8,128)(2,1)S(1)}, bf16[2,64,512]{2,1,0:T(8,128)(2,1)S(1)}, u32[]{:S(2)}, u32[]{:S(2)}) collective-permute-start(bf16[2,64,512]{2,1,0:T(8,128)(2,1)S(1)} %get-tuple-element.30), channel_id=1, source_target_pairs={{0,28},{2,30},{4,24},{6,26},{8,20},{10,22},{12,16},{14,18},{16,12}... | collective-permute-start | bytes 393224 | tf_op jit(solution)/shard_map/ppermute | solution.py:243
  42.1 8.2 %collective-permute-start = (bf16[2,64,512]{2,1,0:T(8,128)(2,1)S(1)}, bf16[2,64,512]{2,1,0:T(8,128)(2,1)S(1)}, u32[]{:S(2)}, u32[]{:S(2)}) collective-permute-start(bf16[2,64,512]{2,1,0:T(8,128)(2,1)S(1)} %get-tuple-element.23), channel_id=1, source_target_pairs={{0,6},{2,4},{4,2},{6,0},{8,14},{10,12},{12,10},{14,8},{16,22},{18,... | collective-permute-start | bytes 393224 | tf_op jit(solution)/shard_map/ppermute | solution.py:243
  42.9 7.6 %collective-permute-start.1 = (bf16[2,64,512]{2,1,0:T(8,128)(2,1)S(1)}, bf16[2,64,512]{2,1,0:T(8,128)(2,1)S(1)}, u32[]{:S(2)}, u32[]{:S(2)}) collective-permute-start(bf16[2,64,512]{2,1,0:T(8,128)(2,1)S(1)} %get-tuple-element.24), channel_id=1, source_target_pairs={{0,30},{2,28},{4,26},{6,24},{8,22},{10,20},{12,18},{14,16},{16,14}... | collective-permute-start | bytes 393224 | tf_op jit(solution)/shard_map/ppermute | solution.py:243
  44.5 5.9 %collective-permute-start.2 = (bf16[2,64,512]{2,1,0:T(8,128)(2,1)S(1)}, bf16[2,64,512]{2,1,0:T(8,128)(2,1)S(1)}, u32[]{:S(2)}, u32[]{:S(2)}) collective-permute-start(bf16[2,64,512]{2,1,0:T(8,128)(2,1)S(1)} %get-tuple-element.25), channel_id=1, source_target_pairs={{0,2},{2,0},{4,6},{6,4},{8,10},{10,8},{12,14},{14,12},{16,18},{18,... | collective-permute-start | bytes 393224 | tf_op jit(solution)/shard_map/ppermute | solution.py:243
  50.6 2.7 %copy-start = (f32[8,1024]{1,0:T(8,128)S(1)}, f32[8,1024]{1,0:T(8,128)}, u32[]{:S(2)}) copy-start(f32[8,1024]{1,0:T(8,128)} %constant.10.clone.first) | copy-start | bytes 98308
  51.8 14.3 %collective-permute-start.15 = (f32[3,2,128,128]{3,2,1,0:T(8,128)S(1)}, f32[3,2,128,128]{3,2,1,0:T(8,128)S(1)}, u32[]{:S(2)}, u32[]{:S(2)}) collective-permute-start(f32[3,2,128,128]{3,2,1,0:T(8,128)S(1)} %sent.1), channel_id=1, source_target_pairs={{0,1},{1,0},{2,3},{3,2},{4,5},{5,4},{6,7},{7,6},{8,9},{9,8},{10,11... | collective-permute-start | bytes 1179656 | tf_op jit(solution)/shard_map/ppermute | solution.py:318
  61.4 4.7 %collective-permute-start.16 = (bf16[1,2,128,128]{3,2,1,0:T(8,128)(2,1)S(1)}, bf16[1,2,128,128]{3,2,1,0:T(8,128)(2,1)S(1)}, u32[]{:S(2)}, u32[]{:S(2)}) collective-permute-start(bf16[1,2,128,128]{3,2,1,0:T(8,128)(2,1)S(1)} %get-tuple-element.39), channel_id=1, source_target_pairs={{0,1},{1,0},{2,3},{3,2},{4,5},{5,4},{6,7},{7,6},{8,9},{9,8},{10,11... | collective-permute-start | bytes 196616 | tf_op jit(solution)/shard_map/ppermute | solution.py:318
  61.9 4.2 %collective-permute-start.17 = (f32[8,128]{1,0:T(8,128)S(1)}, f32[8,128]{1,0:T(8,128)S(1)}, u32[]{:S(2)}, u32[]{:S(2)}) collective-permute-start(f32[8,128]{1,0:T(8,128)S(1)} %get-tuple-element.40.gains_ref), channel_id=1, source_target_pairs={{0,1},{1,0},{2,3},{3,2},{4,5},{5,4},{6,7},{7,6},{8,9},{9,8},{10,11... | collective-permute-start | bytes 12296 | tf_op jit(solution)/shard_map/ppermute | solution.py:318

commit v8 on v7

--- a/solution.py
+++ b/solution.py
@@ -18,7 +18,8 @@
 GROUP = 4
 FIRST = 2
 RAW = 3
-SPLITS = 2
+TERMS = 2
+FIRST_TERMS = 3
 
 VMEM = pl.BlockSpec(memory_space=pltpu.VMEM)
 ANY = pl.BlockSpec(memory_space=pl.ANY)
@@ -33,10 +34,10 @@
     return (both / math.sqrt(count)).astype(np.float32)
 
 
-def pieces(x):
+def pieces(x, terms):
     parts = []
     rest = x
-    for k in range(SPLITS):
+    for k in range(terms):
         part = rest.astype(jnp.bfloat16).astype(jnp.float32)
         parts.append(part)
         rest = rest - part
@@ -45,10 +46,11 @@
 
 def dot(x, y):
     split = lax.dot_general(x, y, (((1,), (0,)), ((), ())), preferred_element_type=jnp.float32)
-    rows = split.shape[0] // SPLITS
-    total = split[(SPLITS - 1) * rows :]
-    for k in range(SPLITS - 2, -1, -1):
-        total = total + split[k * rows : (k + 1) * rows]
+    rows = 2 * RANK
+    last = split.shape[0] - rows
+    total = split[last:]
+    for k in range(last - rows, -1, -rows):
+        total = total + split[k : k + rows]
     return total
 
 
@@ -95,18 +97,20 @@
         for k in range(0, count, 2 * TB):
             vt_ref[part, :, k : k + 2 * TB] = jnp.transpose(v_ref[part, k : k + 2 * TB, :])
 
-    def project(q):
-        x = pieces(q)
+    def project(q, terms=TERMS):
+        x = pieces(q, terms)
         return dot(x, v_ref[0]) + sign * swap(dot(x, v_ref[1]))
 
-    def expand(y):
-        z = dot(pieces(y), vt_ref[0]) - dot(pieces(sign * swap(y)), vt_ref[1])
+    def expand(y, terms=TERMS):
+        z = dot(pieces(y, terms), vt_ref[0]) - dot(pieces(sign * swap(y), terms), vt_ref[1])
         return z * (1.0 / frames)
 
     def step(_, z):
         return expand(gram_schmidt(z, project(z), sign, order)[1])
 
-    z = lax.fori_loop(0, ITERS - 1, step, expand(project(first[...])))
+    z = expand(project(first[...], FIRST_TERMS), FIRST_TERMS)
+    z = expand(gram_schmidt(z, project(z, FIRST_TERMS), sign, order)[1])
+    z = lax.fori_loop(0, ITERS - 2, step, z)
     q, y = gram_schmidt(z, project(z), sign, order)
     turned = sign * swap(y)
     u = jnp.zeros_like(q)

time: 67.9 us -> 68.1 us (level)
  no operation moved by 1% of the time
where the time goes in v8:
time: 68.1 us; the launch traced here: 67.6 us
  starting transfers between devices  30.8 us (45%)
  Pallas kernels  19.6 us (29%)
  waiting for transfers between devices  16.5 us (24%)
  between operations  0.73 us (1%)
    ppermute x15, starting transfers between devices, corner_turn(): blocks.append(lax.ppermute(block, 'inp', pairs) if d else block)  27.2 us
    ppermute x15, waiting for transfers between devices, corner_turn(): blocks.append(lax.ppermute(block, 'inp', pairs) if d else block)  15.8 us
    pallas_call x1, Pallas kernels, body(): pl.pallas_call(functools.partial(calibrate_kernel, owners, slots), out_sh...  8.2 us
    pallas_call x5, Pallas kernels, corner_turn(): pl.pallas_call(functools.partial(front_kernel, targets, min(size, 16)), o...  6.79 us
    ppermute x3, starting transfers between devices, shift(): lax.ppermute(x, 'chan', [(j, (j + d) % owners) for j in range(owners)])  3.62 us
    pallas_call x1, Pallas kernels, body(): pl.pallas_call(functools.partial(own_kernel, slots), out_shape=vis_shape,...  1.97 us
  transfers between devices with their start and end apart: 18, of which 8 were waited for; matrix products, arithmetic and copies ran while one was open for 0% of the time, Pallas kernels for 23%

profile of v8, /device:TPU:0, one launch (start us, length us, event | category | flops | bytes accessed | tf_op | source)
XLA Modules:
  0.0 67.6 jit_solution(11928028904896332562)
XLA Ops:
  0.6 1.2 %front.9 = (bf16[2,64,512]{2,1,0:T(8,128)(2,1)S(1)}, bf16[2,64,512]{2,1,0:T(8,128)(2,1)S(1)}) custom-call(s32[1]{0:T(128)} %bitcast.me_ref, s32[1,64]{1,0:T(1,128)} %bitcast.18, bf16[8192,128]{1,0:T(8,128)(2,1)} %bitcast.12), custom_call_target="tpu_custom_call" | custom-call | tf_op jit(solution)/shard_map/front/pallas_call | solution.py:229
  1.9 4.1 %collective-permute-start.13 = (bf16[2,64,512]{2,1,0:T(8,128)(2,1)S(1)}, bf16[2,64,512]{2,1,0:T(8,128)(2,1)S(1)}, u32[]{:S(2)}, u32[]{:S(2)}) collective-permute-start(bf16[2,64,512]{2,1,0:T(8,128)(2,1)S(1)} %get-tuple-element.37), channel_id=1, source_target_pairs={{0,16},{2,18},{4,20},{6,22},{8,24},{10,26},{12,28},{14,30},{16,0},... | collective-permute-start | bytes 393224 | tf_op jit(solution)/shard_map/ppermute | solution.py:247
  6.0 0.0 collective-permute-start.14
  6.0 1.2 %front.8 = (bf16[2,64,512]{2,1,0:T(8,128)(2,1)S(1)}, bf16[2,64,512]{2,1,0:T(8,128)(2,1)S(1)}) custom-call(s32[1]{0:T(128)} %bitcast.me_ref, s32[1,64]{1,0:T(1,128)} %bitcast.19, bf16[8192,128]{1,0:T(8,128)(2,1)} %bitcast.13), custom_call_target="tpu_custom_call" | custom-call | tf_op jit(solution)/shard_map/front/pallas_call | solution.py:229
  7.2 1.6 %collective-permute-start.11 = (bf16[2,64,512]{2,1,0:T(8,128)(2,1)S(1)}, bf16[2,64,512]{2,1,0:T(8,128)(2,1)S(1)}, u32[]{:S(2)}, u32[]{:S(2)}) collective-permute-start(bf16[2,64,512]{2,1,0:T(8,128)(2,1)S(1)} %get-tuple-element.35), channel_id=1, source_target_pairs={{0,8},{2,10},{4,12},{6,14},{8,0},{10,2},{12,4},{14,6},{16,24},{18,... | collective-permute-start | bytes 393224 | tf_op jit(solution)/shard_map/ppermute | solution.py:247
  8.8 3.0 %collective-permute-start.12 = (bf16[2,64,512]{2,1,0:T(8,128)(2,1)S(1)}, bf16[2,64,512]{2,1,0:T(8,128)(2,1)S(1)}, u32[]{:S(2)}, u32[]{:S(2)}) collective-permute-start(bf16[2,64,512]{2,1,0:T(8,128)(2,1)S(1)} %get-tuple-element.36), channel_id=1, source_target_pairs={{0,20},{2,22},{4,16},{6,18},{8,28},{10,30},{12,24},{14,26},{16,4},... | collective-permute-start | bytes 393224 | tf_op jit(solution)/shard_map/ppermute | solution.py:247
  11.9 1.4 %front.7 = (bf16[2,64,512]{2,1,0:T(8,128)(2,1)S(1)}, bf16[2,64,512]{2,1,0:T(8,128)(2,1)S(1)}, bf16[2,64,512]{2,1,0:T(8,128)(2,1)S(1)}, bf16[2,64,512]{2,1,0:T(8,128)(2,1)S(1)}) custom-call(s32[1]{0:T(128)} %bitcast.me_ref, s32[1,64]{1,0:T(1,128)} %bitcast.20, bf16[8192,128]{1,0:T(8,128)(2,1)} %bitcast.14), custom_call_target="tpu_custom_call" | custom-call | tf_op jit(solution)/shard_map/front/pallas_call | solution.py:229
  13.3 0.5 collective-permute-start.7
  13.8 1.4 %front.6 = (bf16[2,64,512]{2,1,0:T(8,128)(2,1)S(1)}, bf16[2,64,512]{2,1,0:T(8,128)(2,1)S(1)}, bf16[2,64,512]{2,1,0:T(8,128)(2,1)S(1)}, bf16[2,64,512]{2,1,0:T(8,128)(2,1)S(1)}) custom-call(s32[1]{0:T(128)} %bitcast.me_ref, s32[1,64]{1,0:T(1,128)} %bitcast.21, bf16[8192,128]{1,0:T(8,128)(2,1)} %bitcast.15), custom_call_target="tpu_custom_call" | custom-call | tf_op jit(solution)/shard_map/front/pallas_call | solution.py:229
  15.3 0.6 collective-permute-done.13.refs_14_
  15.9 0.0 collective-permute-start.8
  15.9 4.1 %collective-permute-done.14.refs_15_ = bf16[2,64,512]{2,1,0:T(8,128)(2,1)S(1)} collective-permute-done((bf16[2,64,512]{2,1,0:T(8,128)(2,1)S(1)}, bf16[2,64,512]{2,1,0:T(8,128)(2,1)S(1)}, u32[]{:S(2)}, u32[]{:S(2)}) %collective-permute-start.14) | collective-permute-done | bytes 131104 | tf_op jit(solution)/shard_map/ppermute | solution.py:247
  20.0 3.3 %collective-permute-start.9 = (bf16[2,64,512]{2,1,0:T(8,128)(2,1)S(1)}, bf16[2,64,512]{2,1,0:T(8,128)(2,1)S(1)}, u32[]{:S(2)}, u32[]{:S(2)}) collective-permute-start(bf16[2,64,512]{2,1,0:T(8,128)(2,1)S(1)} %get-tuple-element.33), channel_id=1, source_target_pairs={{0,12},{2,14},{4,8},{6,10},{8,4},{10,6},{12,0},{14,2},{16,28},{18,... | collective-permute-start | bytes 393224 | tf_op jit(solution)/shard_map/ppermute | solution.py:247
  23.3 0.0 collective-permute-done.11.refs_12_
  23.3 1.8 %collective-permute-start.10 = (bf16[2,64,512]{2,1,0:T(8,128)(2,1)S(1)}, bf16[2,64,512]{2,1,0:T(8,128)(2,1)S(1)}, u32[]{:S(2)}, u32[]{:S(2)}) collective-permute-start(bf16[2,64,512]{2,1,0:T(8,128)(2,1)S(1)} %get-tuple-element.34), channel_id=1, source_target_pairs={{0,24},{2,26},{4,28},{6,30},{8,16},{10,18},{12,20},{14,22},{16,8},... | collective-permute-start | bytes 393224 | tf_op jit(solution)/shard_map/ppermute | solution.py:247
  25.2 3.4 %collective-permute-done.12.refs_13_ = bf16[2,64,512]{2,1,0:T(8,128)(2,1)S(1)} collective-permute-done((bf16[2,64,512]{2,1,0:T(8,128)(2,1)S(1)}, bf16[2,64,512]{2,1,0:T(8,128)(2,1)S(1)}, u32[]{:S(2)}, u32[]{:S(2)}) %collective-permute-start.12) | collective-permute-done | bytes 131104 | tf_op jit(solution)/shard_map/ppermute | solution.py:247
  28.5 0.0 collective-permute-start.3
  28.5 0.0 collective-permute-done.7.refs_8_
  28.5 1.9 %collective-permute-start.4 = (bf16[2,64,512]{2,1,0:T(8,128)(2,1)S(1)}, bf16[2,64,512]{2,1,0:T(8,128)(2,1)S(1)}, u32[]{:S(2)}, u32[]{:S(2)}) collective-permute-start(bf16[2,64,512]{2,1,0:T(8,128)(2,1)S(1)} %get-tuple-element.28), channel_id=1, source_target_pairs={{0,26},{2,24},{4,30},{6,28},{8,18},{10,16},{12,22},{14,20},{16,10}... | collective-permute-start | bytes 393224 | tf_op jit(solution)/shard_map/ppermute | solution.py:247
  30.5 1.4 %front.5 = (bf16[2,64,512]{2,1,0:T(8,128)(2,1)S(1)}, bf16[2,64,512]{2,1,0:T(8,128)(2,1)S(1)}, bf16[2,64,512]{2,1,0:T(8,128)(2,1)S(1)}, bf16[2,64,512]{2,1,0:T(8,128)(2,1)S(1)}, s32[64]{0:T(128)S(1)}) custom-call(s32[1]{0:T(128)} %bitcast.me_ref, s32[1,64]{1,0:T(1,128)} %bitcast.22, bf16[8192,128]{1,0:T(8,128)(2,1)} %bitcast.16, s32[64]{0:T(128)} %refs_0_.1), custom_call_target="tpu_custom_call" | custom-call | tf_op jit(solution)/shard_map/front/pallas_call | solution.py:229
  31.9 0.0 collective-permute-done.8.refs_9_
  31.9 0.6 collective-permute-start.5
  32.5 2.2 %collective-permute-done.9.refs_10_ = bf16[2,64,512]{2,1,0:T(8,128)(2,1)S(1)} collective-permute-done((bf16[2,64,512]{2,1,0:T(8,128)(2,1)S(1)}, bf16[2,64,512]{2,1,0:T(8,128)(2,1)S(1)}, u32[]{:S(2)}, u32[]{:S(2)}) %collective-permute-start.9) | collective-permute-done | bytes 131104 | tf_op jit(solution)/shard_map/ppermute | solution.py:247
  34.8 7.4 %collective-permute-start.6 = (bf16[2,64,512]{2,1,0:T(8,128)(2,1)S(1)}, bf16[2,64,512]{2,1,0:T(8,128)(2,1)S(1)}, u32[]{:S(2)}, u32[]{:S(2)}) collective-permute-start(bf16[2,64,512]{2,1,0:T(8,128)(2,1)S(1)} %get-tuple-element.30), channel_id=1, source_target_pairs={{0,28},{2,30},{4,24},{6,26},{8,20},{10,22},{12,16},{14,18},{16,12}... | collective-permute-start | bytes 393224 | tf_op jit(solution)/shard_map/ppermute | solution.py:247
  42.1 0.0 collective-permute-done.10.refs_11_
  42.1 0.8 %collective-permute-start = (bf16[2,64,512]{2,1,0:T(8,128)(2,1)S(1)}, bf16[2,64,512]{2,1,0:T(8,128)(2,1)S(1)}, u32[]{:S(2)}, u32[]{:S(2)}) collective-permute-start(bf16[2,64,512]{2,1,0:T(8,128)(2,1)S(1)} %get-tuple-element.23), channel_id=1, source_target_pairs={{0,6},{2,4},{4,2},{6,0},{8,14},{10,12},{12,10},{14,8},{16,22},{18,... | collective-permute-start | bytes 393224 | tf_op jit(solution)/shard_map/ppermute | solution.py:247
  42.9 0.0 collective-permute-done.3.refs_4_
  42.9 1.6 %collective-permute-start.1 = (bf16[2,64,512]{2,1,0:T(8,128)(2,1)S(1)}, bf16[2,64,512]{2,1,0:T(8,128)(2,1)S(1)}, u32[]{:S(2)}, u32[]{:S(2)}) collective-permute-start(bf16[2,64,512]{2,1,0:T(8,128)(2,1)S(1)} %get-tuple-element.24), channel_id=1, source_target_pairs={{0,30},{2,28},{4,26},{6,24},{8,22},{10,20},{12,18},{14,16},{16,14}... | collective-permute-start | bytes 393224 | tf_op jit(solution)/shard_map/ppermute | solution.py:247
  44.5 0.0 collective-permute-done.4.refs_5_
  44.5 0.5 collective-permute-start.2
  45.0 0.0 collective-permute-done.5.refs_6_
  45.0 1.0 %collective-permute-done.6.refs_7_ = bf16[2,64,512]{2,1,0:T(8,128)(2,1)S(1)} collective-permute-done((bf16[2,64,512]{2,1,0:T(8,128)(2,1)S(1)}, bf16[2,64,512]{2,1,0:T(8,128)(2,1)S(1)}, u32[]{:S(2)}, u32[]{:S(2)}) %collective-permute-start.6) | collective-permute-done | bytes 131104 | tf_op jit(solution)/shard_map/ppermute | solution.py:247
  45.9 4.4 %collective-permute-done.refs_0_ = bf16[2,64,512]{2,1,0:T(8,128)(2,1)S(1)} collective-permute-done((bf16[2,64,512]{2,1,0:T(8,128)(2,1)S(1)}, bf16[2,64,512]{2,1,0:T(8,128)(2,1)S(1)}, u32[]{:S(2)}, u32[]{:S(2)}) %collective-permute-start) | collective-permute-done | bytes 131104 | tf_op jit(solution)/shard_map/ppermute | solution.py:247
  50.3 0.1 collective-permute-done.1.refs_1_
  50.5 0.0 collective-permute-done.2.refs_2_
  50.5 0.2 join.1.v_ref
  50.6 0.0 copy-start
  50.6 1.1 %sent.1 = f32[3,2,128,128]{3,2,1,0:T(8,128)S(1)} custom-call(s32[64]{0:T(128)S(1)} %get-tuple-element.22.table_ref, s32[1]{0:T(128)} %bitcast.5.me_ref, bf16[2,1024,512]{2,1,0:T(8,128)(2,1)S(1)} %join.1.v_ref), custom_call_target="tpu_custom_call" | custom-call | tf_op jit(solution)/shard_map/sent/pallas_call | solution.py:324
  51.8 1.6 %collective-permute-start.15 = (f32[3,2,128,128]{3,2,1,0:T(8,128)S(1)}, f32[3,2,128,128]{3,2,1,0:T(8,128)S(1)}, u32[]{:S(2)}, u32[]{:S(2)}) collective-permute-start(f32[3,2,128,128]{3,2,1,0:T(8,128)S(1)} %sent.1), channel_id=1, source_target_pairs={{0,1},{1,0},{2,3},{3,2},{4,5},{5,4},{6,7},{7,6},{8,9},{9,8},{10,11... | collective-permute-start | bytes 1179656 | tf_op jit(solution)/shard_map/ppermute | solution.py:322
  53.4 0.0 copy-done
  53.4 8.2 %calibrate.1 = (f32[1,1024]{1,0:T(1,128)}, f32[8,128]{1,0:T(8,128)S(1)}, bf16[1,2,128,128]{3,2,1,0:T(8,128)(2,1)S(1)}) custom-call(s32[64]{0:T(128)S(1)} %get-tuple-element.22.table_ref, s32[1]{0:T(128)} %bitcast.5.me_ref, bf16[2,1024,512]{2,1,0:T(8,128)(2,1)S(1)} %join.1.v_ref, f32[8,1024]{1,0:T(8,128)S(1)} %copy-done), custom_call_target="tpu_custom_call" | custom-call | tf_op jit(solution)/shard_map/calibrate/pallas_call | solution.py:334
  61.6 0.5 collective-permute-start.16
  62.1 1.5 %collective-permute-start.17 = (f32[8,128]{1,0:T(8,128)S(1)}, f32[8,128]{1,0:T(8,128)S(1)}, u32[]{:S(2)}, u32[]{:S(2)}) collective-permute-start(f32[8,128]{1,0:T(8,128)S(1)} %get-tuple-element.40.gains_ref), channel_id=1, source_target_pairs={{0,1},{1,0},{2,3},{3,2},{4,5},{5,4},{6,7},{7,6},{8,9},{9,8},{10,11... | collective-permute-start | bytes 12296 | tf_op jit(solution)/shard_map/ppermute | solution.py:322
  63.6 2.0 %own.1.refs_3_ = bf16[2,4,2,128,128]{4,3,2,1,0:T(8,128)(2,1)} custom-call(s32[64]{0:T(128)S(1)} %get-tuple-element.22.table_ref, s32[1]{0:T(128)} %bitcast.5.me_ref, bf16[2,1024,512]{2,1,0:T(8,128)(2,1)S(1)} %join.1.v_ref, f32[8,128]{1,0:T(8,128)S(1)} %get-tuple-element.40.gains_ref), custom_call_target="tpu_custom_call" | custom-call | tf_op jit(solution)/shard_map/own/pallas_call | solution.py:351
  65.6 0.6 collective-permute-done.17.refs_2_
  66.2 0.0 collective-permute-done.16.refs_1_
  66.2 0.0 collective-permute-done.15.refs_0_
  66.2 1.4 %others.1 = bf16[2,4,2,128,128]{4,3,2,1,0:T(8,128)(2,1)} custom-call(s32[64]{0:T(128)S(1)} %get-tuple-element.22.table_ref, s32[1]{0:T(128)} %bitcast.5.me_ref, f32[3,2,128,128]{3,2,1,0:T(8,128)S(1)} %collective-permute-done.15.refs_0_, bf16[1,2,128,128]{3,2,1,0:T(8,128)(2,1)S(1)} %collective-permute-done.16.refs_1_, ...), custom_call_target="tpu_custom_call", output_to_operand_aliasing={{}: (5, {})} | custom-call | tf_op jit(solution)/shard_map/others/pallas_call | solution.py:360
Async XLA Ops:
  1.9 14.0 %collective-permute-start.13 = (bf16[2,64,512]{2,1,0:T(8,128)(2,1)S(1)}, bf16[2,64,512]{2,1,0:T(8,128)(2,1)S(1)}, u32[]{:S(2)}, u32[]{:S(2)}) collective-permute-start(bf16[2,64,512]{2,1,0:T(8,128)(2,1)S(1)} %get-tuple-element.37), channel_id=1, source_target_pairs={{0,16},{2,18},{4,20},{6,22},{8,24},{10,26},{12,28},{14,30},{16,0},... | collective-permute-start | bytes 393224 | tf_op jit(solution)/shard_map/ppermute | solution.py:247
  6.0 14.0 %collective-permute-start.14 = (bf16[2,64,512]{2,1,0:T(8,128)(2,1)S(1)}, bf16[2,64,512]{2,1,0:T(8,128)(2,1)S(1)}, u32[]{:S(2)}, u32[]{:S(2)}) collective-permute-start(bf16[2,64,512]{2,1,0:T(8,128)(2,1)S(1)} %get-tuple-element.38), channel_id=1, source_target_pairs={{0,18},{2,16},{4,22},{6,20},{8,26},{10,24},{12,30},{14,28},{16,2},... | collective-permute-start | bytes 393224 | tf_op jit(solution)/shard_map/ppermute | solution.py:247
  7.2 16.1 %collective-permute-start.11 = (bf16[2,64,512]{2,1,0:T(8,128)(2,1)S(1)}, bf16[2,64,512]{2,1,0:T(8,128)(2,1)S(1)}, u32[]{:S(2)}, u32[]{:S(2)}) collective-permute-start(bf16[2,64,512]{2,1,0:T(8,128)(2,1)S(1)} %get-tuple-element.35), channel_id=1, source_target_pairs={{0,8},{2,10},{4,12},{6,14},{8,0},{10,2},{12,4},{14,6},{16,24},{18,... | collective-permute-start | bytes 393224 | tf_op jit(solution)/shard_map/ppermute | solution.py:247
  8.8 19.7 %collective-permute-start.12 = (bf16[2,64,512]{2,1,0:T(8,128)(2,1)S(1)}, bf16[2,64,512]{2,1,0:T(8,128)(2,1)S(1)}, u32[]{:S(2)}, u32[]{:S(2)}) collective-permute-start(bf16[2,64,512]{2,1,0:T(8,128)(2,1)S(1)} %get-tuple-element.36), channel_id=1, source_target_pairs={{0,20},{2,22},{4,16},{6,18},{8,28},{10,30},{12,24},{14,26},{16,4},... | collective-permute-start | bytes 393224 | tf_op jit(solution)/shard_map/ppermute | solution.py:247
  13.3 15.2 %collective-permute-start.7 = (bf16[2,64,512]{2,1,0:T(8,128)(2,1)S(1)}, bf16[2,64,512]{2,1,0:T(8,128)(2,1)S(1)}, u32[]{:S(2)}, u32[]{:S(2)}) collective-permute-start(bf16[2,64,512]{2,1,0:T(8,128)(2,1)S(1)} %get-tuple-element.31), channel_id=1, source_target_pairs={{0,10},{2,8},{4,14},{6,12},{8,2},{10,0},{12,6},{14,4},{16,26},{18,... | collective-permute-start | bytes 393224 | tf_op jit(solution)/shard_map/ppermute | solution.py:247
  15.9 16.0 %collective-permute-start.8 = (bf16[2,64,512]{2,1,0:T(8,128)(2,1)S(1)}, bf16[2,64,512]{2,1,0:T(8,128)(2,1)S(1)}, u32[]{:S(2)}, u32[]{:S(2)}) collective-permute-start(bf16[2,64,512]{2,1,0:T(8,128)(2,1)S(1)} %get-tuple-element.32), channel_id=1, source_target_pairs={{0,22},{2,20},{4,18},{6,16},{8,30},{10,28},{12,26},{14,24},{16,6},... | collective-permute-start | bytes 393224 | tf_op jit(solution)/shard_map/ppermute | solution.py:247
  20.0 14.8 %collective-permute-start.9 = (bf16[2,64,512]{2,1,0:T(8,128)(2,1)S(1)}, bf16[2,64,512]{2,1,0:T(8,128)(2,1)S(1)}, u32[]{:S(2)}, u32[]{:S(2)}) collective-permute-start(bf16[2,64,512]{2,1,0:T(8,128)(2,1)S(1)} %get-tuple-element.33), channel_id=1, source_target_pairs={{0,12},{2,14},{4,8},{6,10},{8,4},{10,6},{12,0},{14,2},{16,28},{18,... | collective-permute-start | bytes 393224 | tf_op jit(solution)/shard_map/ppermute | solution.py:247
  23.3 18.8 %collective-permute-start.10 = (bf16[2,64,512]{2,1,0:T(8,128)(2,1)S(1)}, bf16[2,64,512]{2,1,0:T(8,128)(2,1)S(1)}, u32[]{:S(2)}, u32[]{:S(2)}) collective-permute-start(bf16[2,64,512]{2,1,0:T(8,128)(2,1)S(1)} %get-tuple-element.34), channel_id=1, source_target_pairs={{0,24},{2,26},{4,28},{6,30},{8,16},{10,18},{12,20},{14,22},{16,8},... | collective-permute-start | bytes 393224 | tf_op jit(solution)/shard_map/ppermute | solution.py:247
  28.5 14.4 %collective-permute-start.3 = (bf16[2,64,512]{2,1,0:T(8,128)(2,1)S(1)}, bf16[2,64,512]{2,1,0:T(8,128)(2,1)S(1)}, u32[]{:S(2)}, u32[]{:S(2)}) collective-permute-start(bf16[2,64,512]{2,1,0:T(8,128)(2,1)S(1)} %get-tuple-element.27), channel_id=1, source_target_pairs={{0,14},{2,12},{4,10},{6,8},{8,6},{10,4},{12,2},{14,0},{16,30},{18,... | collective-permute-start | bytes 393224 | tf_op jit(solution)/shard_map/ppermute | solution.py:247
  28.5 16.0 %collective-permute-start.4 = (bf16[2,64,512]{2,1,0:T(8,128)(2,1)S(1)}, bf16[2,64,512]{2,1,0:T(8,128)(2,1)S(1)}, u32[]{:S(2)}, u32[]{:S(2)}) collective-permute-start(bf16[2,64,512]{2,1,0:T(8,128)(2,1)S(1)} %get-tuple-element.28), channel_id=1, source_target_pairs={{0,26},{2,24},{4,30},{6,28},{8,18},{10,16},{12,22},{14,20},{16,10}... | collective-permute-start | bytes 393224 | tf_op jit(solution)/shard_map/ppermute | solution.py:247
  31.9 13.1 %collective-permute-start.5 = (bf16[2,64,512]{2,1,0:T(8,128)(2,1)S(1)}, bf16[2,64,512]{2,1,0:T(8,128)(2,1)S(1)}, u32[]{:S(2)}, u32[]{:S(2)}) collective-permute-start(bf16[2,64,512]{2,1,0:T(8,128)(2,1)S(1)} %get-tuple-element.29), channel_id=1, source_target_pairs={{0,4},{2,6},{4,0},{6,2},{8,12},{10,14},{12,8},{14,10},{16,20},{18,... | collective-permute-start | bytes 393224 | tf_op jit(solution)/shard_map/ppermute | solution.py:247
  34.8 11.2 %collective-permute-start.6 = (bf16[2,64,512]{2,1,0:T(8,128)(2,1)S(1)}, bf16[2,64,512]{2,1,0:T(8,128)(2,1)S(1)}, u32[]{:S(2)}, u32[]{:S(2)}) collective-permute-start(bf16[2,64,512]{2,1,0:T(8,128)(2,1)S(1)} %get-tuple-element.30), channel_id=1, source_target_pairs={{0,28},{2,30},{4,24},{6,26},{8,20},{10,22},{12,16},{14,18},{16,12}... | collective-permute-start | bytes 393224 | tf_op jit(solution)/shard_map/ppermute | solution.py:247
  42.1 8.2 %collective-permute-start = (bf16[2,64,512]{2,1,0:T(8,128)(2,1)S(1)}, bf16[2,64,512]{2,1,0:T(8,128)(2,1)S(1)}, u32[]{:S(2)}, u32[]{:S(2)}) collective-permute-start(bf16[2,64,512]{2,1,0:T(8,128)(2,1)S(1)} %get-tuple-element.23), channel_id=1, source_target_pairs={{0,6},{2,4},{4,2},{6,0},{8,14},{10,12},{12,10},{14,8},{16,22},{18,... | collective-permute-start | bytes 393224 | tf_op jit(solution)/shard_map/ppermute | solution.py:247
  42.9 7.6 %collective-permute-start.1 = (bf16[2,64,512]{2,1,0:T(8,128)(2,1)S(1)}, bf16[2,64,512]{2,1,0:T(8,128)(2,1)S(1)}, u32[]{:S(2)}, u32[]{:S(2)}) collective-permute-start(bf16[2,64,512]{2,1,0:T(8,128)(2,1)S(1)} %get-tuple-element.24), channel_id=1, source_target_pairs={{0,30},{2,28},{4,26},{6,24},{8,22},{10,20},{12,18},{14,16},{16,14}... | collective-permute-start | bytes 393224 | tf_op jit(solution)/shard_map/ppermute | solution.py:247
  44.5 5.9 %collective-permute-start.2 = (bf16[2,64,512]{2,1,0:T(8,128)(2,1)S(1)}, bf16[2,64,512]{2,1,0:T(8,128)(2,1)S(1)}, u32[]{:S(2)}, u32[]{:S(2)}) collective-permute-start(bf16[2,64,512]{2,1,0:T(8,128)(2,1)S(1)} %get-tuple-element.25), channel_id=1, source_target_pairs={{0,2},{2,0},{4,6},{6,4},{8,10},{10,8},{12,14},{14,12},{16,18},{18,... | collective-permute-start | bytes 393224 | tf_op jit(solution)/shard_map/ppermute | solution.py:247
  50.6 2.7 %copy-start = (f32[8,1024]{1,0:T(8,128)S(1)}, f32[8,1024]{1,0:T(8,128)}, u32[]{:S(2)}) copy-start(f32[8,1024]{1,0:T(8,128)} %constant.10.clone.first) | copy-start | bytes 98308
  51.8 14.5 %collective-permute-start.15 = (f32[3,2,128,128]{3,2,1,0:T(8,128)S(1)}, f32[3,2,128,128]{3,2,1,0:T(8,128)S(1)}, u32[]{:S(2)}, u32[]{:S(2)}) collective-permute-start(f32[3,2,128,128]{3,2,1,0:T(8,128)S(1)} %sent.1), channel_id=1, source_target_pairs={{0,1},{1,0},{2,3},{3,2},{4,5},{5,4},{6,7},{7,6},{8,9},{9,8},{10,11... | collective-permute-start | bytes 1179656 | tf_op jit(solution)/shard_map/ppermute | solution.py:322
  61.6 4.7 %collective-permute-start.16 = (bf16[1,2,128,128]{3,2,1,0:T(8,128)(2,1)S(1)}, bf16[1,2,128,128]{3,2,1,0:T(8,128)(2,1)S(1)}, u32[]{:S(2)}, u32[]{:S(2)}) collective-permute-start(bf16[1,2,128,128]{3,2,1,0:T(8,128)(2,1)S(1)} %get-tuple-element.39), channel_id=1, source_target_pairs={{0,1},{1,0},{2,3},{3,2},{4,5},{5,4},{6,7},{7,6},{8,9},{9,8},{10,11... | collective-permute-start | bytes 196616 | tf_op jit(solution)/shard_map/ppermute | solution.py:322
  62.1 4.1 %collective-permute-start.17 = (f32[8,128]{1,0:T(8,128)S(1)}, f32[8,128]{1,0:T(8,128)S(1)}, u32[]{:S(2)}, u32[]{:S(2)}) collective-permute-start(f32[8,128]{1,0:T(8,128)S(1)} %get-tuple-element.40.gains_ref), channel_id=1, source_target_pairs={{0,1},{1,0},{2,3},{3,2},{4,5},{5,4},{6,7},{7,6},{8,9},{9,8},{10,11... | collective-permute-start | bytes 12296 | tf_op jit(solution)/shard_map/ppermute | solution.py:322

commit v9 on v8

--- a/solution.py
+++ b/solution.py
@@ -109,7 +109,7 @@
         return expand(gram_schmidt(z, project(z), sign, order)[1])
 
     z = expand(project(first[...], FIRST_TERMS), FIRST_TERMS)
-    z = expand(gram_schmidt(z, project(z, FIRST_TERMS), sign, order)[1])
+    z = expand(project(gram_schmidt(z, z, sign, order)[0]))
     z = lax.fori_loop(0, ITERS - 2, step, z)
     q, y = gram_schmidt(z, project(z), sign, order)
     turned = sign * swap(y)

time: 68.1 us -> 68.4 us (level)
  transfers between devices with their start and end apart: 18 -> 18, of which waited for: 8 -> 8; matrix products, arithmetic and copies ran while one was open for 0% -> 0% of each run, Pallas kernels for 23% -> 24%
where the time goes in v9:
time: 68.4 us; the launch traced here: 67.9 us
  starting transfers between devices  30.8 us (45%)
  Pallas kernels  19.9 us (29%)
  waiting for transfers between devices  16.5 us (24%)
  between operations  0.73 us (1%)
    ppermute x15, starting transfers between devices, corner_turn(): blocks.append(lax.ppermute(block, 'inp', pairs) if d else block)  27.2 us
    ppermute x15, waiting for transfers between devices, corner_turn(): blocks.append(lax.ppermute(block, 'inp', pairs) if d else block)  15.8 us
    pallas_call x1, Pallas kernels, body(): pl.pallas_call(functools.partial(calibrate_kernel, owners, slots), out_sh...  8.49 us
    pallas_call x5, Pallas kernels, corner_turn(): pl.pallas_call(functools.partial(front_kernel, targets, min(size, 16)), o...  6.79 us
    ppermute x3, starting transfers between devices, shift(): lax.ppermute(x, 'chan', [(j, (j + d) % owners) for j in range(owners)])  3.62 us
    pallas_call x1, Pallas kernels, body(): pl.pallas_call(functools.partial(own_kernel, slots), out_shape=vis_shape,...  1.97 us
  transfers between devices with their start and end apart: 18, of which 8 were waited for; matrix products, arithmetic and copies ran while one was open for 0% of the time, Pallas kernels for 24%

profile of v9, /device:TPU:0, one launch (start us, length us, event | category | flops | bytes accessed | tf_op | source)
XLA Modules:
  0.0 67.9 jit_solution(12745929601089861674)
XLA Ops:
  0.6 1.2 %front.9 = (bf16[2,64,512]{2,1,0:T(8,128)(2,1)S(1)}, bf16[2,64,512]{2,1,0:T(8,128)(2,1)S(1)}) custom-call(s32[1]{0:T(128)} %bitcast.me_ref, s32[1,64]{1,0:T(1,128)} %bitcast.18, bf16[8192,128]{1,0:T(8,128)(2,1)} %bitcast.12), custom_call_target="tpu_custom_call" | custom-call | tf_op jit(solution)/shard_map/front/pallas_call | solution.py:229
  1.9 4.1 %collective-permute-start.13 = (bf16[2,64,512]{2,1,0:T(8,128)(2,1)S(1)}, bf16[2,64,512]{2,1,0:T(8,128)(2,1)S(1)}, u32[]{:S(2)}, u32[]{:S(2)}) collective-permute-start(bf16[2,64,512]{2,1,0:T(8,128)(2,1)S(1)} %get-tuple-element.37), channel_id=1, source_target_pairs={{0,16},{2,18},{4,20},{6,22},{8,24},{10,26},{12,28},{14,30},{16,0},... | collective-permute-start | bytes 393224 | tf_op jit(solution)/shard_map/ppermute | solution.py:247
  6.0 0.0 collective-permute-start.14
  6.0 1.2 %front.8 = (bf16[2,64,512]{2,1,0:T(8,128)(2,1)S(1)}, bf16[2,64,512]{2,1,0:T(8,128)(2,1)S(1)}) custom-call(s32[1]{0:T(128)} %bitcast.me_ref, s32[1,64]{1,0:T(1,128)} %bitcast.19, bf16[8192,128]{1,0:T(8,128)(2,1)} %bitcast.13), custom_call_target="tpu_custom_call" | custom-call | tf_op jit(solution)/shard_map/front/pallas_call | solution.py:229
  7.2 1.6 %collective-permute-start.11 = (bf16[2,64,512]{2,1,0:T(8,128)(2,1)S(1)}, bf16[2,64,512]{2,1,0:T(8,128)(2,1)S(1)}, u32[]{:S(2)}, u32[]{:S(2)}) collective-permute-start(bf16[2,64,512]{2,1,0:T(8,128)(2,1)S(1)} %get-tuple-element.35), channel_id=1, source_target_pairs={{0,8},{2,10},{4,12},{6,14},{8,0},{10,2},{12,4},{14,6},{16,24},{18,... | collective-permute-start | bytes 393224 | tf_op jit(solution)/shard_map/ppermute | solution.py:247
  8.8 3.0 %collective-permute-start.12 = (bf16[2,64,512]{2,1,0:T(8,128)(2,1)S(1)}, bf16[2,64,512]{2,1,0:T(8,128)(2,1)S(1)}, u32[]{:S(2)}, u32[]{:S(2)}) collective-permute-start(bf16[2,64,512]{2,1,0:T(8,128)(2,1)S(1)} %get-tuple-element.36), channel_id=1, source_target_pairs={{0,20},{2,22},{4,16},{6,18},{8,28},{10,30},{12,24},{14,26},{16,4},... | collective-permute-start | bytes 393224 | tf_op jit(solution)/shard_map/ppermute | solution.py:247
  11.9 1.4 %front.7 = (bf16[2,64,512]{2,1,0:T(8,128)(2,1)S(1)}, bf16[2,64,512]{2,1,0:T(8,128)(2,1)S(1)}, bf16[2,64,512]{2,1,0:T(8,128)(2,1)S(1)}, bf16[2,64,512]{2,1,0:T(8,128)(2,1)S(1)}) custom-call(s32[1]{0:T(128)} %bitcast.me_ref, s32[1,64]{1,0:T(1,128)} %bitcast.20, bf16[8192,128]{1,0:T(8,128)(2,1)} %bitcast.14), custom_call_target="tpu_custom_call" | custom-call | tf_op jit(solution)/shard_map/front/pallas_call | solution.py:229
  13.3 0.5 collective-permute-start.7
  13.8 1.4 %front.6 = (bf16[2,64,512]{2,1,0:T(8,128)(2,1)S(1)}, bf16[2,64,512]{2,1,0:T(8,128)(2,1)S(1)}, bf16[2,64,512]{2,1,0:T(8,128)(2,1)S(1)}, bf16[2,64,512]{2,1,0:T(8,128)(2,1)S(1)}) custom-call(s32[1]{0:T(128)} %bitcast.me_ref, s32[1,64]{1,0:T(1,128)} %bitcast.21, bf16[8192,128]{1,0:T(8,128)(2,1)} %bitcast.15), custom_call_target="tpu_custom_call" | custom-call | tf_op jit(solution)/shard_map/front/pallas_call | solution.py:229
  15.3 0.6 collective-permute-done.13.refs_14_
  15.9 0.0 collective-permute-start.8
  15.9 4.1 %collective-permute-done.14.refs_15_ = bf16[2,64,512]{2,1,0:T(8,128)(2,1)S(1)} collective-permute-done((bf16[2,64,512]{2,1,0:T(8,128)(2,1)S(1)}, bf16[2,64,512]{2,1,0:T(8,128)(2,1)S(1)}, u32[]{:S(2)}, u32[]{:S(2)}) %collective-permute-start.14) | collective-permute-done | bytes 131104 | tf_op jit(solution)/shard_map/ppermute | solution.py:247
  20.0 3.3 %collective-permute-start.9 = (bf16[2,64,512]{2,1,0:T(8,128)(2,1)S(1)}, bf16[2,64,512]{2,1,0:T(8,128)(2,1)S(1)}, u32[]{:S(2)}, u32[]{:S(2)}) collective-permute-start(bf16[2,64,512]{2,1,0:T(8,128)(2,1)S(1)} %get-tuple-element.33), channel_id=1, source_target_pairs={{0,12},{2,14},{4,8},{6,10},{8,4},{10,6},{12,0},{14,2},{16,28},{18,... | collective-permute-start | bytes 393224 | tf_op jit(solution)/shard_map/ppermute | solution.py:247
  23.3 0.0 collective-permute-done.11.refs_12_
  23.3 1.8 %collective-permute-start.10 = (bf16[2,64,512]{2,1,0:T(8,128)(2,1)S(1)}, bf16[2,64,512]{2,1,0:T(8,128)(2,1)S(1)}, u32[]{:S(2)}, u32[]{:S(2)}) collective-permute-start(bf16[2,64,512]{2,1,0:T(8,128)(2,1)S(1)} %get-tuple-element.34), channel_id=1, source_target_pairs={{0,24},{2,26},{4,28},{6,30},{8,16},{10,18},{12,20},{14,22},{16,8},... | collective-permute-start | bytes 393224 | tf_op jit(solution)/shard_map/ppermute | solution.py:247
  25.2 3.4 %collective-permute-done.12.refs_13_ = bf16[2,64,512]{2,1,0:T(8,128)(2,1)S(1)} collective-permute-done((bf16[2,64,512]{2,1,0:T(8,128)(2,1)S(1)}, bf16[2,64,512]{2,1,0:T(8,128)(2,1)S(1)}, u32[]{:S(2)}, u32[]{:S(2)}) %collective-permute-start.12) | collective-permute-done | bytes 131104 | tf_op jit(solution)/shard_map/ppermute | solution.py:247
  28.5 0.0 collective-permute-start.3
  28.5 0.0 collective-permute-done.7.refs_8_
  28.5 1.9 %collective-permute-start.4 = (bf16[2,64,512]{2,1,0:T(8,128)(2,1)S(1)}, bf16[2,64,512]{2,1,0:T(8,128)(2,1)S(1)}, u32[]{:S(2)}, u32[]{:S(2)}) collective-permute-start(bf16[2,64,512]{2,1,0:T(8,128)(2,1)S(1)} %get-tuple-element.28), channel_id=1, source_target_pairs={{0,26},{2,24},{4,30},{6,28},{8,18},{10,16},{12,22},{14,20},{16,10}... | collective-permute-start | bytes 393224 | tf_op jit(solution)/shard_map/ppermute | solution.py:247
  30.5 1.4 %front.5 = (bf16[2,64,512]{2,1,0:T(8,128)(2,1)S(1)}, bf16[2,64,512]{2,1,0:T(8,128)(2,1)S(1)}, bf16[2,64,512]{2,1,0:T(8,128)(2,1)S(1)}, bf16[2,64,512]{2,1,0:T(8,128)(2,1)S(1)}, s32[64]{0:T(128)S(1)}) custom-call(s32[1]{0:T(128)} %bitcast.me_ref, s32[1,64]{1,0:T(1,128)} %bitcast.22, bf16[8192,128]{1,0:T(8,128)(2,1)} %bitcast.16, s32[64]{0:T(128)} %refs_0_.1), custom_call_target="tpu_custom_call" | custom-call | tf_op jit(solution)/shard_map/front/pallas_call | solution.py:229
  31.9 0.0 collective-permute-done.8.refs_9_
  31.9 0.6 collective-permute-start.5
  32.5 2.2 %collective-permute-done.9.refs_10_ = bf16[2,64,512]{2,1,0:T(8,128)(2,1)S(1)} collective-permute-done((bf16[2,64,512]{2,1,0:T(8,128)(2,1)S(1)}, bf16[2,64,512]{2,1,0:T(8,128)(2,1)S(1)}, u32[]{:S(2)}, u32[]{:S(2)}) %collective-permute-start.9) | collective-permute-done | bytes 131104 | tf_op jit(solution)/shard_map/ppermute | solution.py:247
  34.8 7.4 %collective-permute-start.6 = (bf16[2,64,512]{2,1,0:T(8,128)(2,1)S(1)}, bf16[2,64,512]{2,1,0:T(8,128)(2,1)S(1)}, u32[]{:S(2)}, u32[]{:S(2)}) collective-permute-start(bf16[2,64,512]{2,1,0:T(8,128)(2,1)S(1)} %get-tuple-element.30), channel_id=1, source_target_pairs={{0,28},{2,30},{4,24},{6,26},{8,20},{10,22},{12,16},{14,18},{16,12}... | collective-permute-start | bytes 393224 | tf_op jit(solution)/shard_map/ppermute | solution.py:247
  42.1 0.0 collective-permute-done.10.refs_11_
  42.1 0.8 %collective-permute-start = (bf16[2,64,512]{2,1,0:T(8,128)(2,1)S(1)}, bf16[2,64,512]{2,1,0:T(8,128)(2,1)S(1)}, u32[]{:S(2)}, u32[]{:S(2)}) collective-permute-start(bf16[2,64,512]{2,1,0:T(8,128)(2,1)S(1)} %get-tuple-element.23), channel_id=1, source_target_pairs={{0,6},{2,4},{4,2},{6,0},{8,14},{10,12},{12,10},{14,8},{16,22},{18,... | collective-permute-start | bytes 393224 | tf_op jit(solution)/shard_map/ppermute | solution.py:247
  42.9 0.0 collective-permute-done.3.refs_4_
  42.9 1.6 %collective-permute-start.1 = (bf16[2,64,512]{2,1,0:T(8,128)(2,1)S(1)}, bf16[2,64,512]{2,1,0:T(8,128)(2,1)S(1)}, u32[]{:S(2)}, u32[]{:S(2)}) collective-permute-start(bf16[2,64,512]{2,1,0:T(8,128)(2,1)S(1)} %get-tuple-element.24), channel_id=1, source_target_pairs={{0,30},{2,28},{4,26},{6,24},{8,22},{10,20},{12,18},{14,16},{16,14}... | collective-permute-start | bytes 393224 | tf_op jit(solution)/shard_map/ppermute | solution.py:247
  44.5 0.0 collective-permute-done.4.refs_5_
  44.5 0.5 collective-permute-start.2
  45.0 0.0 collective-permute-done.5.refs_6_
  45.0 1.0 %collective-permute-done.6.refs_7_ = bf16[2,64,512]{2,1,0:T(8,128)(2,1)S(1)} collective-permute-done((bf16[2,64,512]{2,1,0:T(8,128)(2,1)S(1)}, bf16[2,64,512]{2,1,0:T(8,128)(2,1)S(1)}, u32[]{:S(2)}, u32[]{:S(2)}) %collective-permute-start.6) | collective-permute-done | bytes 131104 | tf_op jit(solution)/shard_map/ppermute | solution.py:247
  45.9 4.4 %collective-permute-done.refs_0_ = bf16[2,64,512]{2,1,0:T(8,128)(2,1)S(1)} collective-permute-done((bf16[2,64,512]{2,1,0:T(8,128)(2,1)S(1)}, bf16[2,64,512]{2,1,0:T(8,128)(2,1)S(1)}, u32[]{:S(2)}, u32[]{:S(2)}) %collective-permute-start) | collective-permute-done | bytes 131104 | tf_op jit(solution)/shard_map/ppermute | solution.py:247
  50.3 0.1 collective-permute-done.1.refs_1_
  50.5 0.0 collective-permute-done.2.refs_2_
  50.5 0.2 join.1.v_ref
  50.6 0.0 copy-start
  50.6 1.1 %sent.1 = f32[3,2,128,128]{3,2,1,0:T(8,128)S(1)} custom-call(s32[64]{0:T(128)S(1)} %get-tuple-element.22.table_ref, s32[1]{0:T(128)} %bitcast.5.me_ref, bf16[2,1024,512]{2,1,0:T(8,128)(2,1)S(1)} %join.1.v_ref), custom_call_target="tpu_custom_call" | custom-call | tf_op jit(solution)/shard_map/sent/pallas_call | solution.py:324
  51.8 1.6 %collective-permute-start.15 = (f32[3,2,128,128]{3,2,1,0:T(8,128)S(1)}, f32[3,2,128,128]{3,2,1,0:T(8,128)S(1)}, u32[]{:S(2)}, u32[]{:S(2)}) collective-permute-start(f32[3,2,128,128]{3,2,1,0:T(8,128)S(1)} %sent.1), channel_id=1, source_target_pairs={{0,1},{1,0},{2,3},{3,2},{4,5},{5,4},{6,7},{7,6},{8,9},{9,8},{10,11... | collective-permute-start | bytes 1179656 | tf_op jit(solution)/shard_map/ppermute | solution.py:322
  53.4 0.0 copy-done
  53.4 8.5 %calibrate.1 = (f32[1,1024]{1,0:T(1,128)}, f32[8,128]{1,0:T(8,128)S(1)}, bf16[1,2,128,128]{3,2,1,0:T(8,128)(2,1)S(1)}) custom-call(s32[64]{0:T(128)S(1)} %get-tuple-element.22.table_ref, s32[1]{0:T(128)} %bitcast.5.me_ref, bf16[2,1024,512]{2,1,0:T(8,128)(2,1)S(1)} %join.1.v_ref, f32[8,1024]{1,0:T(8,128)S(1)} %copy-done), custom_call_target="tpu_custom_call" | custom-call | tf_op jit(solution)/shard_map/calibrate/pallas_call | solution.py:334
  61.8 0.5 collective-permute-start.16
  62.3 1.5 %collective-permute-start.17 = (f32[8,128]{1,0:T(8,128)S(1)}, f32[8,128]{1,0:T(8,128)S(1)}, u32[]{:S(2)}, u32[]{:S(2)}) collective-permute-start(f32[8,128]{1,0:T(8,128)S(1)} %get-tuple-element.40.gains_ref), channel_id=1, source_target_pairs={{0,1},{1,0},{2,3},{3,2},{4,5},{5,4},{6,7},{7,6},{8,9},{9,8},{10,11... | collective-permute-start | bytes 12296 | tf_op jit(solution)/shard_map/ppermute | solution.py:322
  63.9 2.0 %own.1.refs_3_ = bf16[2,4,2,128,128]{4,3,2,1,0:T(8,128)(2,1)} custom-call(s32[64]{0:T(128)S(1)} %get-tuple-element.22.table_ref, s32[1]{0:T(128)} %bitcast.5.me_ref, bf16[2,1024,512]{2,1,0:T(8,128)(2,1)S(1)} %join.1.v_ref, f32[8,128]{1,0:T(8,128)S(1)} %get-tuple-element.40.gains_ref), custom_call_target="tpu_custom_call" | custom-call | tf_op jit(solution)/shard_map/own/pallas_call | solution.py:351
  65.8 0.6 collective-permute-done.17.refs_2_
  66.5 0.0 collective-permute-done.16.refs_1_
  66.5 0.0 collective-permute-done.15.refs_0_
  66.5 1.4 %others.1 = bf16[2,4,2,128,128]{4,3,2,1,0:T(8,128)(2,1)} custom-call(s32[64]{0:T(128)S(1)} %get-tuple-element.22.table_ref, s32[1]{0:T(128)} %bitcast.5.me_ref, f32[3,2,128,128]{3,2,1,0:T(8,128)S(1)} %collective-permute-done.15.refs_0_, bf16[1,2,128,128]{3,2,1,0:T(8,128)(2,1)S(1)} %collective-permute-done.16.refs_1_, ...), custom_call_target="tpu_custom_call", output_to_operand_aliasing={{}: (5, {})} | custom-call | tf_op jit(solution)/shard_map/others/pallas_call | solution.py:360
Async XLA Ops:
  1.9 14.0 %collective-permute-start.13 = (bf16[2,64,512]{2,1,0:T(8,128)(2,1)S(1)}, bf16[2,64,512]{2,1,0:T(8,128)(2,1)S(1)}, u32[]{:S(2)}, u32[]{:S(2)}) collective-permute-start(bf16[2,64,512]{2,1,0:T(8,128)(2,1)S(1)} %get-tuple-element.37), channel_id=1, source_target_pairs={{0,16},{2,18},{4,20},{6,22},{8,24},{10,26},{12,28},{14,30},{16,0},... | collective-permute-start | bytes 393224 | tf_op jit(solution)/shard_map/ppermute | solution.py:247
  6.0 14.0 %collective-permute-start.14 = (bf16[2,64,512]{2,1,0:T(8,128)(2,1)S(1)}, bf16[2,64,512]{2,1,0:T(8,128)(2,1)S(1)}, u32[]{:S(2)}, u32[]{:S(2)}) collective-permute-start(bf16[2,64,512]{2,1,0:T(8,128)(2,1)S(1)} %get-tuple-element.38), channel_id=1, source_target_pairs={{0,18},{2,16},{4,22},{6,20},{8,26},{10,24},{12,30},{14,28},{16,2},... | collective-permute-start | bytes 393224 | tf_op jit(solution)/shard_map/ppermute | solution.py:247
  7.2 16.1 %collective-permute-start.11 = (bf16[2,64,512]{2,1,0:T(8,128)(2,1)S(1)}, bf16[2,64,512]{2,1,0:T(8,128)(2,1)S(1)}, u32[]{:S(2)}, u32[]{:S(2)}) collective-permute-start(bf16[2,64,512]{2,1,0:T(8,128)(2,1)S(1)} %get-tuple-element.35), channel_id=1, source_target_pairs={{0,8},{2,10},{4,12},{6,14},{8,0},{10,2},{12,4},{14,6},{16,24},{18,... | collective-permute-start | bytes 393224 | tf_op jit(solution)/shard_map/ppermute | solution.py:247
  8.8 19.7 %collective-permute-start.12 = (bf16[2,64,512]{2,1,0:T(8,128)(2,1)S(1)}, bf16[2,64,512]{2,1,0:T(8,128)(2,1)S(1)}, u32[]{:S(2)}, u32[]{:S(2)}) collective-permute-start(bf16[2,64,512]{2,1,0:T(8,128)(2,1)S(1)} %get-tuple-element.36), channel_id=1, source_target_pairs={{0,20},{2,22},{4,16},{6,18},{8,28},{10,30},{12,24},{14,26},{16,4},... | collective-permute-start | bytes 393224 | tf_op jit(solution)/shard_map/ppermute | solution.py:247
  13.3 15.2 %collective-permute-start.7 = (bf16[2,64,512]{2,1,0:T(8,128)(2,1)S(1)}, bf16[2,64,512]{2,1,0:T(8,128)(2,1)S(1)}, u32[]{:S(2)}, u32[]{:S(2)}) collective-permute-start(bf16[2,64,512]{2,1,0:T(8,128)(2,1)S(1)} %get-tuple-element.31), channel_id=1, source_target_pairs={{0,10},{2,8},{4,14},{6,12},{8,2},{10,0},{12,6},{14,4},{16,26},{18,... | collective-permute-start | bytes 393224 | tf_op jit(solution)/shard_map/ppermute | solution.py:247
  15.9 16.0 %collective-permute-start.8 = (bf16[2,64,512]{2,1,0:T(8,128)(2,1)S(1)}, bf16[2,64,512]{2,1,0:T(8,128)(2,1)S(1)}, u32[]{:S(2)}, u32[]{:S(2)}) collective-permute-start(bf16[2,64,512]{2,1,0:T(8,128)(2,1)S(1)} %get-tuple-element.32), channel_id=1, source_target_pairs={{0,22},{2,20},{4,18},{6,16},{8,30},{10,28},{12,26},{14,24},{16,6},... | collective-permute-start | bytes 393224 | tf_op jit(solution)/shard_map/ppermute | solution.py:247
  20.0 14.8 %collective-permute-start.9 = (bf16[2,64,512]{2,1,0:T(8,128)(2,1)S(1)}, bf16[2,64,512]{2,1,0:T(8,128)(2,1)S(1)}, u32[]{:S(2)}, u32[]{:S(2)}) collective-permute-start(bf16[2,64,512]{2,1,0:T(8,128)(2,1)S(1)} %get-tuple-element.33), channel_id=1, source_target_pairs={{0,12},{2,14},{4,8},{6,10},{8,4},{10,6},{12,0},{14,2},{16,28},{18,... | collective-permute-start | bytes 393224 | tf_op jit(solution)/shard_map/ppermute | solution.py:247
  23.3 18.8 %collective-permute-start.10 = (bf16[2,64,512]{2,1,0:T(8,128)(2,1)S(1)}, bf16[2,64,512]{2,1,0:T(8,128)(2,1)S(1)}, u32[]{:S(2)}, u32[]{:S(2)}) collective-permute-start(bf16[2,64,512]{2,1,0:T(8,128)(2,1)S(1)} %get-tuple-element.34), channel_id=1, source_target_pairs={{0,24},{2,26},{4,28},{6,30},{8,16},{10,18},{12,20},{14,22},{16,8},... | collective-permute-start | bytes 393224 | tf_op jit(solution)/shard_map/ppermute | solution.py:247
  28.5 14.4 %collective-permute-start.3 = (bf16[2,64,512]{2,1,0:T(8,128)(2,1)S(1)}, bf16[2,64,512]{2,1,0:T(8,128)(2,1)S(1)}, u32[]{:S(2)}, u32[]{:S(2)}) collective-permute-start(bf16[2,64,512]{2,1,0:T(8,128)(2,1)S(1)} %get-tuple-element.27), channel_id=1, source_target_pairs={{0,14},{2,12},{4,10},{6,8},{8,6},{10,4},{12,2},{14,0},{16,30},{18,... | collective-permute-start | bytes 393224 | tf_op jit(solution)/shard_map/ppermute | solution.py:247
  28.5 16.0 %collective-permute-start.4 = (bf16[2,64,512]{2,1,0:T(8,128)(2,1)S(1)}, bf16[2,64,512]{2,1,0:T(8,128)(2,1)S(1)}, u32[]{:S(2)}, u32[]{:S(2)}) collective-permute-start(bf16[2,64,512]{2,1,0:T(8,128)(2,1)S(1)} %get-tuple-element.28), channel_id=1, source_target_pairs={{0,26},{2,24},{4,30},{6,28},{8,18},{10,16},{12,22},{14,20},{16,10}... | collective-permute-start | bytes 393224 | tf_op jit(solution)/shard_map/ppermute | solution.py:247
  31.9 13.1 %collective-permute-start.5 = (bf16[2,64,512]{2,1,0:T(8,128)(2,1)S(1)}, bf16[2,64,512]{2,1,0:T(8,128)(2,1)S(1)}, u32[]{:S(2)}, u32[]{:S(2)}) collective-permute-start(bf16[2,64,512]{2,1,0:T(8,128)(2,1)S(1)} %get-tuple-element.29), channel_id=1, source_target_pairs={{0,4},{2,6},{4,0},{6,2},{8,12},{10,14},{12,8},{14,10},{16,20},{18,... | collective-permute-start | bytes 393224 | tf_op jit(solution)/shard_map/ppermute | solution.py:247
  34.8 11.2 %collective-permute-start.6 = (bf16[2,64,512]{2,1,0:T(8,128)(2,1)S(1)}, bf16[2,64,512]{2,1,0:T(8,128)(2,1)S(1)}, u32[]{:S(2)}, u32[]{:S(2)}) collective-permute-start(bf16[2,64,512]{2,1,0:T(8,128)(2,1)S(1)} %get-tuple-element.30), channel_id=1, source_target_pairs={{0,28},{2,30},{4,24},{6,26},{8,20},{10,22},{12,16},{14,18},{16,12}... | collective-permute-start | bytes 393224 | tf_op jit(solution)/shard_map/ppermute | solution.py:247
  42.1 8.2 %collective-permute-start = (bf16[2,64,512]{2,1,0:T(8,128)(2,1)S(1)}, bf16[2,64,512]{2,1,0:T(8,128)(2,1)S(1)}, u32[]{:S(2)}, u32[]{:S(2)}) collective-permute-start(bf16[2,64,512]{2,1,0:T(8,128)(2,1)S(1)} %get-tuple-element.23), channel_id=1, source_target_pairs={{0,6},{2,4},{4,2},{6,0},{8,14},{10,12},{12,10},{14,8},{16,22},{18,... | collective-permute-start | bytes 393224 | tf_op jit(solution)/shard_map/ppermute | solution.py:247
  42.9 7.6 %collective-permute-start.1 = (bf16[2,64,512]{2,1,0:T(8,128)(2,1)S(1)}, bf16[2,64,512]{2,1,0:T(8,128)(2,1)S(1)}, u32[]{:S(2)}, u32[]{:S(2)}) collective-permute-start(bf16[2,64,512]{2,1,0:T(8,128)(2,1)S(1)} %get-tuple-element.24), channel_id=1, source_target_pairs={{0,30},{2,28},{4,26},{6,24},{8,22},{10,20},{12,18},{14,16},{16,14}... | collective-permute-start | bytes 393224 | tf_op jit(solution)/shard_map/ppermute | solution.py:247
  44.5 5.9 %collective-permute-start.2 = (bf16[2,64,512]{2,1,0:T(8,128)(2,1)S(1)}, bf16[2,64,512]{2,1,0:T(8,128)(2,1)S(1)}, u32[]{:S(2)}, u32[]{:S(2)}) collective-permute-start(bf16[2,64,512]{2,1,0:T(8,128)(2,1)S(1)} %get-tuple-element.25), channel_id=1, source_target_pairs={{0,2},{2,0},{4,6},{6,4},{8,10},{10,8},{12,14},{14,12},{16,18},{18,... | collective-permute-start | bytes 393224 | tf_op jit(solution)/shard_map/ppermute | solution.py:247
  50.6 2.7 %copy-start = (f32[8,1024]{1,0:T(8,128)S(1)}, f32[8,1024]{1,0:T(8,128)}, u32[]{:S(2)}) copy-start(f32[8,1024]{1,0:T(8,128)} %constant.10.clone.first) | copy-start | bytes 98308
  51.8 14.7 %collective-permute-start.15 = (f32[3,2,128,128]{3,2,1,0:T(8,128)S(1)}, f32[3,2,128,128]{3,2,1,0:T(8,128)S(1)}, u32[]{:S(2)}, u32[]{:S(2)}) collective-permute-start(f32[3,2,128,128]{3,2,1,0:T(8,128)S(1)} %sent.1), channel_id=1, source_target_pairs={{0,1},{1,0},{2,3},{3,2},{4,5},{5,4},{6,7},{7,6},{8,9},{9,8},{10,11... | collective-permute-start | bytes 1179656 | tf_op jit(solution)/shard_map/ppermute | solution.py:322
  61.8 4.7 %collective-permute-start.16 = (bf16[1,2,128,128]{3,2,1,0:T(8,128)(2,1)S(1)}, bf16[1,2,128,128]{3,2,1,0:T(8,128)(2,1)S(1)}, u32[]{:S(2)}, u32[]{:S(2)}) collective-permute-start(bf16[1,2,128,128]{3,2,1,0:T(8,128)(2,1)S(1)} %get-tuple-element.39), channel_id=1, source_target_pairs={{0,1},{1,0},{2,3},{3,2},{4,5},{5,4},{6,7},{7,6},{8,9},{9,8},{10,11... | collective-permute-start | bytes 196616 | tf_op jit(solution)/shard_map/ppermute | solution.py:322
  62.3 4.2 %collective-permute-start.17 = (f32[8,128]{1,0:T(8,128)S(1)}, f32[8,128]{1,0:T(8,128)S(1)}, u32[]{:S(2)}, u32[]{:S(2)}) collective-permute-start(f32[8,128]{1,0:T(8,128)S(1)} %get-tuple-element.40.gains_ref), channel_id=1, source_target_pairs={{0,1},{1,0},{2,3},{3,2},{4,5},{5,4},{6,7},{7,6},{8,9},{9,8},{10,11... | collective-permute-start | bytes 12296 | tf_op jit(solution)/shard_map/ppermute | solution.py:322
